TPU v7x, 32 devices: a whole 2x2x4 slice. The times are simulated.
32 devices in a mesh: shard: 2 (over y), ctx: 4 (over z), tp: 4 (over x, core).
Axes of the slice: x: 2, y: 2, z: 4, core: 2. Of those that a mesh axis runs over, the one named last changes fastest.
Arguments:
- inputs: bfloat16 [2, 4096, 768], P('shard', 'ctx'), may hold values from -6 to 6
- lengths: int32 [2], P('shard'), may hold values from 1024 to 4096, as said below
- global_blocks: int32 [2, 2], P('shard'), may hold values from 0 to 15, as said below
- random_blocks: int32 [2, 64, 3], P('shard', 'ctx'), may hold values from 0 to 63
- master_blocks: float32 [768, 96, 96], P(('shard', 'ctx', 'tp'))
- outer_vectors: float32 [6, 768], replicated
- inner_biases: float32 [4, 1152], P('tp'), may hold values from -4 to 4
- left_stats: float32 [768, 96, 96], P(('shard', 'ctx', 'tp')), as said below
- right_stats: float32 [768, 96, 96], P(('shard', 'ctx', 'tp')), as said below
- left_roots: float32 [768, 96, 96], P(('shard', 'ctx', 'tp')), as said below
- right_roots: float32 [768, 96, 96], P(('shard', 'ctx', 'tp')), as said below
- cotangent: bfloat16 [2, 4096, 768], P('shard', 'ctx'), may hold values from -6 to 6
Outputs:
- output: bfloat16 [2, 4096, 768], P('shard', 'ctx')
- input_grad: bfloat16 [2, 4096, 768], P('shard', 'ctx')
- block_grads: float32 [768, 96, 96], P(('shard', 'ctx', 'tp'))
- outer_grads: float32 [6, 768], P(None, ('shard', 'ctx'))
- inner_grads: float32 [4, 1152], P('tp', ('shard', 'ctx'))
- maxima: float32 [12], P('tp')
- left_new: float32 [768, 96, 96], P(('shard', 'ctx', 'tp'))
- right_new: float32 [768, 96, 96], P(('shard', 'ctx', 'tp'))
- new_blocks: float32 [768, 96, 96], P(('shard', 'ctx', 'tp'))
- new_outer: float32 [6, 768], P(None, ('shard', 'ctx'))
- new_inner: float32 [4, 1152], P('tp', ('shard', 'ctx'))
Inputs may be any that keep to these rules, and one draw needn't show every extreme that they name: `lengths`: sequence 0 holds 4096 valid tokens. `global_blocks`: the two ids of a sequence differ. `left_stats`: each block is symmetric. `right_stats`: each block is symmetric. `left_roots`: each block is symmetric. `right_roots`: each block is symmetric.
All inputs are finite; a program needn't handle non-finite values.
Results may differ from a plain program's by a relative error of at most 0.018.
Values may be sent and summed in bfloat16 or wider, within the bound.
No kernel may reach another device: no remote copies, remote signals or barrier semaphores. Data moves between devices by JAX's collectives and lax.ppermute only.
A program may use at most 192 MiB of HBM per device.

v0:
```python
import functools

import jax
import jax.numpy as jnp
from jax import lax
from jax.experimental import pallas as pl
from jax.experimental.pallas import tpu as pltpu
from jax.sharding import PartitionSpec as P

D = 768
HEADS = 12
HEAD = 64
FF = 3072
BLOCK = 64
SEQ = 4096
PB = 96
LIST = 8
WIDE = 8

eps_norm = 1e-06
tau_clip = 9.0
rate_matrix = 0.3
rate_vector = 0.001
neg_large = -1e30
bf16 = jnp.bfloat16
f32 = jnp.float32
vmem_limit = 56 << 20
OWN = ("shard", "ctx")


def params_of(**more):
    return pltpu.CompilerParams(vmem_limit_bytes=vmem_limit, **more)


def small_params(**more):
    return pltpu.CompilerParams(vmem_limit_bytes=32 << 20, **more)


def dot32(left, right, dims=((1,), (0,))):
    return lax.dot_general(left, right, (dims, ((), ())), preferred_element_type=f32)


def layer_norm(values, gain, shift):
    mean_val = jnp.mean(values, axis=-1, keepdims=True)
    centred = values - mean_val
    var_val = jnp.mean(centred * centred, axis=-1, keepdims=True)
    return centred * lax.rsqrt(var_val + eps_norm) * gain + shift


def gelu_tanh(values):
    return jax.nn.gelu(values, approximate=True)


def swap(rows, mask):
    count = lax.axis_size("tp")
    return lax.ppermute(rows, "tp", [(i, i ^ mask) for i in range(count)])


def shift_ctx(rows, step):
    count = lax.axis_size("ctx")
    return lax.ppermute(rows, "ctx", [(i, (i + step) % count) for i in range(count)])


def shift_shard(rows, step):
    count = lax.axis_size("shard")
    return lax.ppermute(rows, "shard", [(i, (i + step) % count) for i in range(count)])


def owner_move(rows, pairs):
    return lax.ppermute(rows, OWN, pairs)


def after(value, *others):
    return lax.optimization_barrier((value,) + others)[0]


def near_first(count):
    return sorted(range(1, count), key=lambda step: min(step, count - step))


def gather_quarters(own):
    side = swap(own, 1)
    across = swap(own, 2)
    return own, side, across, swap(across, 1)


def scatter_sum(part):
    sent = swap(jnp.concatenate([part[1], part[3]], axis=0), 1)
    rows = part.shape[1]
    far = (part[2].astype(f32) + sent[rows:].astype(f32)).astype(bf16)
    got = swap(far, 2)
    return part[0].astype(f32) + sent[:rows].astype(f32) + got.astype(f32)


def pack_kernel(blocks_ref, out_ref):
    for j in range(WIDE):
        out_ref[:, PB * j : PB * (j + 1)] = blocks_ref[j].astype(bf16)


def pack_rows(blocks):
    rows = blocks.shape[0] // WIDE
    return pl.pallas_call(
        pack_kernel,
        grid=(rows,),
        in_specs=[pl.BlockSpec((WIDE, PB, PB), lambda i: (i, 0, 0))],
        out_specs=pl.BlockSpec((PB, PB * WIDE), lambda i: (i, 0)),
        out_shape=jax.ShapeDtypeStruct((rows * PB, PB * WIDE), bf16),
        compiler_params=params_of(),
        name="pack_rows",
    )(blocks)


def unpack_kernel(place_ref, near_ref, far_ref, q_ref, kv_ref, out_ref, all_ref, *, cols):
    half = near_ref.shape[0]
    all_ref[:half] = near_ref[...]
    all_ref[half:] = far_ref[...]
    q_ref[...] = jnp.zeros(q_ref.shape, bf16)
    for i in range(D // PB):
        for c in range(3):
            unit = 3 * i + c
            piece = all_ref[place_ref[unit // 4], :, cols * (unit % 4) : cols * (unit % 4 + 1)]
            if c == 0:
                q_ref[PB * i : PB * (i + 1), :cols] = piece
            else:
                kv_ref[PB * i : PB * (i + 1), cols * (c - 1) : cols * c] = piece
    pad = out_ref.shape[0] - cols
    out_ref[:pad, :] = jnp.zeros((pad, D), bf16)
    for i in range(cols // PB):
        out_ref[pad + PB * i : pad + PB * (i + 1), :] = all_ref[place_ref[3 * cols // PB + i]]


def unpack_first(place, near, far, cols, wide):
    full = pl.BlockSpec(memory_space=pltpu.VMEM)
    return pl.pallas_call(
        functools.partial(unpack_kernel, cols=cols),
        in_specs=[pl.BlockSpec(memory_space=pltpu.SMEM), full, full],
        out_specs=[full, full, full],
        out_shape=(
            jax.ShapeDtypeStruct((D, wide), bf16),
            jax.ShapeDtypeStruct((D, 2 * cols), bf16),
            jax.ShapeDtypeStruct((wide, D), bf16),
        ),
        scratch_shapes=[pltpu.VMEM((near.shape[0] + far.shape[0], PB, D), bf16)],
        compiler_params=params_of(),
        name="unpack_first",
    )(place, near, far)


def qkv_pack_kernel(q_ref, kv_ref, out_ref, *, cols):
    for i in range(D // PB):
        for c in range(3):
            unit = 3 * i + c
            rows = slice(PB * i, PB * (i + 1))
            piece = q_ref[rows, :cols] if c == 0 else kv_ref[rows, cols * (c - 1) : cols * c]
            out_ref[
                PB * (unit // 4) : PB * (unit // 4 + 1), cols * (unit % 4) : cols * (unit % 4 + 1)
            ] = piece.astype(bf16)


def qkv_pack(grad_q, grad_kv, cols):
    return pl.pallas_call(
        functools.partial(qkv_pack_kernel, cols=cols),
        out_shape=jax.ShapeDtypeStruct((3 * cols, D), bf16),
        compiler_params=params_of(),
        name="qkv_pack",
    )(grad_q, grad_kv)


def head_masks(wide, heads, first):
    lane = lax.broadcasted_iota(jnp.int32, (BLOCK, wide), 1) // HEAD
    return [lane == h + first for h in range(heads)]


def spread(block, masks):
    zero = jnp.zeros_like(block)
    return jnp.concatenate([jnp.where(mask, block, zero) for mask in masks], axis=0)


def fold(stacked, masks):
    total = None
    for h, mask in enumerate(masks):
        part = jnp.where(mask, stacked[BLOCK * h : BLOCK * (h + 1)], 0.0)
        total = part if total is None else total + part
    return total


def listed_rows(addr_ref, kv_ref, i):
    return jnp.concatenate(
        [
            kv_ref[pl.ds(pl.multiple_of(addr_ref[i * LIST + e] * BLOCK, BLOCK), BLOCK), :]
            for e in range(LIST)
        ],
        axis=0,
    )


def load_chunks(chunk_refs, all_ref, sem):
    rows = chunk_refs[0].shape[0]
    copies = [
        pltpu.make_async_copy(ref, all_ref.at[pl.ds(c * rows, rows)], sem.at[c])
        for c, ref in enumerate(chunk_refs)
    ]
    for copy in copies:
        copy.start()
    for copy in copies:
        copy.wait()


def fwd_kernel(addr_ref, valid_ref, query_ref, q_ref, *refs, heads, group, chunks):
    chunk_refs = refs[:chunks]
    att_ref, p_ref, top_ref, kv_ref, sem = refs[chunks:]
    i = pl.program_id(0)
    wide = q_ref.shape[1]
    start = kv_ref.shape[1] - wide

    @pl.when(i == 0)
    def _():
        top_ref[...] = jnp.full(top_ref.shape, neg_large, f32)
        load_chunks(chunk_refs, kv_ref, sem)

    scale = jnp.asarray(HEAD ** (-0.5), bf16)
    q_masks = head_masks(wide, heads, 0)
    v_masks = head_masks(wide, heads, (heads * HEAD - start) // HEAD)
    lane = lax.broadcasted_iota(jnp.int32, (1, LIST * BLOCK), 1)
    for u in range(group):
        block = i * group + u
        mine = slice(u * BLOCK, (u + 1) * BLOCK)
        q_all = spread(q_ref[mine] * scale, q_masks)
        listed = listed_rows(addr_ref, kv_ref, block)
        scores = dot32(q_all, listed[:, :wide], ((1,), (1,)))
        limit = jnp.zeros((1, LIST * BLOCK), jnp.int32)
        for e in range(LIST):
            limit = jnp.where(lane // BLOCK == e, valid_ref[block * LIST + e], limit)
        scores = jnp.where(lane % BLOCK < limit, scores, neg_large)
        row_top = jnp.max(scores, axis=1, keepdims=True)
        shifted = jnp.exp(scores - row_top)
        probs = shifted * (1.0 / jnp.sum(shifted, axis=1, keepdims=True))
        probs_low = probs.astype(bf16)
        p_ref[u] = probs_low
        out = dot32(probs_low, listed[:, start:])
        att_ref[mine] = fold(out, v_masks).astype(bf16)
        row = lax.broadcasted_iota(jnp.int32, row_top.shape, 0) % BLOCK
        seen = jnp.where(row < query_ref[block], row_top, neg_large)
        for h in range(heads):
            best = jnp.max(seen[BLOCK * h : BLOCK * (h + 1)], axis=0, keepdims=True)
            top_ref[h : h + 1, :] = jnp.maximum(top_ref[h : h + 1, :], best)


def attention_forward(queries, kv_chunks, addr, valid, query_valid, heads, group=2):
    tokens, wide = queries.shape
    blocks = tokens // BLOCK
    rows = heads * BLOCK
    cols = LIST * BLOCK
    chunks = len(kv_chunks)
    kv_shape = (chunks * tokens, kv_chunks[0].shape[1])
    return pl.pallas_call(
        functools.partial(fwd_kernel, heads=heads, group=group, chunks=chunks),
        grid_spec=pltpu.PrefetchScalarGridSpec(
            num_scalar_prefetch=3,
            grid=(blocks // group,),
            in_specs=[pl.BlockSpec((group * BLOCK, wide), lambda i, *_: (i, 0))]
            + [pl.BlockSpec(memory_space=pl.ANY)] * chunks,
            out_specs=[
                pl.BlockSpec((group * BLOCK, wide), lambda i, *_: (i, 0)),
                pl.BlockSpec((group, rows, cols), lambda i, *_: (i, 0, 0)),
                pl.BlockSpec((8, 128), lambda i, *_: (0, 0)),
            ],
            scratch_shapes=[pltpu.VMEM(kv_shape, bf16), pltpu.SemaphoreType.DMA((chunks,))],
        ),
        out_shape=(
            jax.ShapeDtypeStruct((tokens, wide), bf16),
            jax.ShapeDtypeStruct((blocks, rows, cols), bf16),
            jax.ShapeDtypeStruct((8, 128), f32),
        ),
        compiler_params=small_params(dimension_semantics=("arbitrary",)),
        cost_estimate=pl.CostEstimate(
            flops=4 * blocks * rows * cols * wide,
            bytes_accessed=2 * (kv_shape[0] * kv_shape[1] + 2 * queries.size + blocks * rows * cols),
            transcendentals=blocks * rows * cols,
        ),
        name="attention_forward",
    )(addr, valid, query_valid, queries, *kv_chunks)


def bwd_kernel(addr_ref, q_ref, do_ref, p_ref, *refs, heads, group, chunks):
    chunk_refs = refs[:chunks]
    dq_ref, dkv_ref, sums_ref, kv_ref, acc_ref, sem = refs[chunks:]
    i = pl.program_id(0)
    wide = q_ref.shape[1]
    start = kv_ref.shape[1] - wide

    @pl.when(i == 0)
    def _():
        acc_ref[...] = jnp.zeros(acc_ref.shape, f32)
        sums_ref[...] = jnp.zeros(sums_ref.shape, f32)
        load_chunks(chunk_refs, kv_ref, sem)

    scale = jnp.asarray(HEAD ** (-0.5), bf16)
    q_masks = head_masks(wide, heads, 0)
    v_masks = head_masks(wide, heads, (heads * HEAD - start) // HEAD)
    for u in range(group):
        block = i * group + u
        mine = slice(u * BLOCK, (u + 1) * BLOCK)
        q_all = spread(q_ref[mine] * scale, q_masks)
        do_all = spread(do_ref[mine], v_masks)
        listed = listed_rows(addr_ref, kv_ref, block)
        probs_low = p_ref[u]
        probs = probs_low.astype(f32)
        d_probs = dot32(do_all, listed[:, start:], ((1,), (1,)))
        delta = jnp.sum(probs * d_probs, axis=1, keepdims=True)
        d_scores = (probs * (d_probs - delta)).astype(bf16)
        d_query = (fold(dot32(d_scores, listed[:, :wide]), q_masks) * HEAD ** (-0.5)).astype(bf16)
        dq_ref[mine] = d_query
        sums_ref[0:1, :wide] += jnp.sum(d_query.astype(f32), axis=0, keepdims=True)
        d_key = dot32(d_scores, q_all, ((0,), (0,)))
        d_value = dot32(probs_low, do_all, ((0,), (0,)))
        sums_ref[1:2, :wide] += jnp.sum(d_value, axis=0, keepdims=True)
        for e in range(LIST):
            rows = pl.ds(pl.multiple_of(addr_ref[block * LIST + e] * BLOCK, BLOCK), BLOCK)
            part = slice(BLOCK * e, BLOCK * (e + 1))
            acc_ref[rows, :start] += d_key[part, :start]
            acc_ref[rows, start:wide] += d_key[part, start:] + d_value[part, : wide - start]
            acc_ref[rows, wide:] += d_value[part, wide - start :]

    @pl.when(i == pl.num_programs(0) - 1)
    def _():
        dkv_ref[...] = acc_ref[...].astype(bf16)


def attention_backward(queries, d_out, probs, kv_chunks, addr, heads, group=2):
    tokens, wide = queries.shape
    blocks = tokens // BLOCK
    rows = heads * BLOCK
    cols = LIST * BLOCK
    chunks = len(kv_chunks)
    kv_shape = (chunks * tokens, kv_chunks[0].shape[1])
    return pl.pallas_call(
        functools.partial(bwd_kernel, heads=heads, group=group, chunks=chunks),
        grid_spec=pltpu.PrefetchScalarGridSpec(
            num_scalar_prefetch=1,
            grid=(blocks // group,),
            in_specs=[
                pl.BlockSpec((group * BLOCK, wide), lambda i, *_: (i, 0)),
                pl.BlockSpec((group * BLOCK, wide), lambda i, *_: (i, 0)),
                pl.BlockSpec((group, rows, cols), lambda i, *_: (i, 0, 0)),
            ]
            + [pl.BlockSpec(memory_space=pl.ANY)] * chunks,
            out_specs=[
                pl.BlockSpec((group * BLOCK, wide), lambda i, *_: (i, 0)),
                pl.BlockSpec(kv_shape, lambda i, *_: (0, 0), pipeline_mode=pl.Buffered(1)),
                pl.BlockSpec((8, wide), lambda i, *_: (0, 0)),
            ],
            scratch_shapes=[
                pltpu.VMEM(kv_shape, bf16),
                pltpu.VMEM(kv_shape, f32),
                pltpu.SemaphoreType.DMA((chunks,)),
            ],
        ),
        out_shape=(
            jax.ShapeDtypeStruct((tokens, wide), bf16),
            jax.ShapeDtypeStruct(kv_shape, bf16),
            jax.ShapeDtypeStruct((8, wide), f32),
        ),
        compiler_params=small_params(dimension_semantics=("arbitrary",)),
        cost_estimate=pl.CostEstimate(
            flops=8 * blocks * rows * cols * wide,
            bytes_accessed=2 * (2 * kv_shape[0] * kv_shape[1] + 3 * queries.size + blocks * rows * cols),
            transcendentals=0,
        ),
        name="attention_backward",
    )(addr, queries, d_out, probs, *kv_chunks)


def two_parts(values):
    high = values.astype(bf16)
    return high, (values - high.astype(f32)).astype(bf16)


def shampoo_kernel(
    g_ref, mb_ref, ls_ref, rs_ref, lr_ref, rr_ref, fac_ref, bg_ref, ln_ref, rn_ref, nb_ref, *, width
):
    for j in range(width):
        grad = g_ref[:, PB * j : PB * (j + 1)]
        bg_ref[j] = grad.astype(f32)
        ln_ref[j] = 0.5 * ls_ref[j] + 0.5 * dot32(grad, grad, ((1,), (1,)))
        rn_ref[j] = 0.5 * rs_ref[j] + 0.5 * dot32(grad, grad, ((0,), (0,)))
        left_hi, left_lo = two_parts(lr_ref[j])
        applied_hi, applied_lo = two_parts(dot32(left_hi, grad) + dot32(left_lo, grad))
        right_hi, right_lo = two_parts(rr_ref[j])
        step_val = (
            dot32(applied_hi, right_hi) + dot32(applied_hi, right_lo) + dot32(applied_lo, right_hi)
        )
        nb_ref[j] = (mb_ref[j] - rate_matrix * step_val) * fac_ref[j]


def shampoo(grads, width, master, left_s, right_s, left_r, right_r, factor):
    count = master.shape[0]
    block = pl.BlockSpec((width, PB, PB), lambda i: (i, 0, 0))
    shape = jax.ShapeDtypeStruct((count, PB, PB), f32)
    return pl.pallas_call(
        functools.partial(shampoo_kernel, width=width),
        grid=(count // width,),
        in_specs=[pl.BlockSpec((PB, PB * width), lambda i: (i, 0))]
        + [block] * 5
        + [pl.BlockSpec((width, 1, PB), lambda i: (i, 0, 0))],
        out_specs=[block] * 4,
        out_shape=[shape] * 4,
        compiler_params=params_of(),
        name="shampoo",
    )(grads, master, left_s, right_s, left_r, right_r, factor)


def per_device(
    inputs,
    lengths,
    global_blocks,
    random_blocks,
    master_blocks,
    outer_vectors,
    inner_biases,
    left_stats,
    right_stats,
    left_roots,
    right_roots,
    cotangent,
):
    tensor_count = lax.axis_size("tp")
    owner_count = lax.axis_size(OWN)
    ctx_count = lax.axis_size("ctx")
    heads_here = HEADS // tensor_count
    cols = heads_here * HEAD
    units = FF // tensor_count
    wide = 256
    pad = wide - cols
    tokens = inputs.shape[1]
    quarter = tokens // 4
    rows_blocks = tokens // BLOCK
    quarter_blocks = rows_blocks // 4
    block_count = SEQ // BLOCK
    blocks_here = master_blocks.shape[0]
    packed = owner_count == WIDE and blocks_here == 3 * WIDE
    shard_count = lax.axis_size("shard")
    me = lax.axis_index("tp")
    z = lax.axis_index("ctx")
    y = lax.axis_index("shard")
    owner = lax.axis_index(OWN)
    bo, b2, g1, beta1, g2, beta2 = [outer_vectors[i] for i in range(6)]

    first = jnp.arange(WIDE, dtype=jnp.int32)
    flat_in = inputs.reshape(tokens, D)
    own_in = lax.dynamic_slice_in_dim(flat_in, me * quarter, quarter, 0)
    if packed:
        own_packed = pack_rows(master_blocks)
        held_row = None
        for j in range(3):
            moved = owner_move(
                own_packed[PB * j : PB * (j + 1)],
                [(d, 3 * d + j) for d in range(WIDE) if 3 * d + j < WIDE],
            )
            held_row = moved if held_row is None else held_row + moved
        near = jnp.stack(
            [held_row] + [shift_ctx(held_row, step) for step in range(1, ctx_count)], axis=0
        )
        far = jnp.concatenate([shift_shard(near, u) for u in range(1, shard_count)], axis=0)
        weights = lax.all_gather(after(own_packed, far), OWN, axis=0, tiled=True)
        row_place = ((y - first // ctx_count) % shard_count) * ctx_count + (
            z - first % ctx_count
        ) % ctx_count
    else:
        weights = pack_rows(lax.all_gather(master_blocks.astype(bf16), OWN, axis=0, tiled=True))
        halves = weights[: WIDE * PB].reshape(2, WIDE // 2, PB, D)
        near, far = halves[0], halves[1]
        row_place = first
    w_q, w_kv, w_out = unpack_first(row_place, near, far, cols, wide)
    edge = 4 * cols
    w_up = weights[edge : edge + D]
    w_down = weights[edge + D :]

    chunks = [None] * ctx_count
    chunks[0] = jnp.concatenate(
        [lax.dynamic_slice_in_dim(flat_in, (me ^ r) * quarter, quarter, 0) for r in range(4)],
        axis=0,
    )
    moved = []
    for n, step in enumerate(near_first(ctx_count)):
        source = own_in if n < 2 else after(own_in, moved[n - 2])
        moved.append(shift_ctx(source, step))
        chunks[step] = jnp.concatenate(gather_quarters(moved[n]), axis=0)

    rel = jnp.arange(rows_blocks, dtype=jnp.int32)
    place = ((rel // quarter_blocks) ^ me) * quarter_blocks + rel % quarter_blocks
    rows = z * rows_blocks + place
    length = lengths[0]
    listed = jnp.concatenate(
        [
            jnp.stack([rows - 1, rows, rows + 1], axis=1),
            jnp.broadcast_to(global_blocks[0][None, :], (rows_blocks, 2)),
            random_blocks[0][place],
        ],
        axis=1,
    ).astype(jnp.int32)
    inside = (listed >= 0) & (listed < block_count)
    held = jnp.clip(listed, 0, block_count - 1)
    valid = jnp.where(inside, jnp.clip(length - listed * BLOCK, 0, BLOCK), 0).reshape(-1)
    local = held % rows_blocks
    addr = (
        ((z - held // rows_blocks) % ctx_count) * rows_blocks
        + ((local // quarter_blocks) ^ me) * quarter_blocks
        + local % quarter_blocks
    ).reshape(-1)
    query_valid = jnp.clip(length - rows * BLOCK, 0, BLOCK)

    inner_row = inner_biases[0]
    q_bias = jnp.concatenate([inner_row[:cols], jnp.zeros((pad,), f32)])
    kv_bias = jnp.concatenate([jnp.zeros((cols,), f32), inner_row[cols : 2 * cols]])
    up_bias = inner_row[2 * cols :]
    queries = (dot32(chunks[0], w_q) + q_bias).astype(bf16)
    kv_chunks = [(dot32(c, w_kv) + kv_bias).astype(bf16) for c in chunks]
    in_all = jnp.concatenate(chunks, axis=0)
    att, probs, tops = attention_forward(queries, kv_chunks, addr, valid, query_valid, heads_here)
    tops = tops[:heads_here, 0]

    own_f32 = own_in.astype(f32)
    branch = scatter_sum(dot32(att, w_out).astype(bf16).reshape(4, quarter, D)) + bo
    hidden = own_f32 + branch
    x_first, back_first = jax.vjp(layer_norm, hidden, g1, beta1)
    x_low = jnp.concatenate(gather_quarters(x_first.astype(bf16)), axis=0)
    gate = dot32(x_low, w_up) + up_bias
    act_low = gelu_tanh(gate).astype(bf16)
    ff = scatter_sum(dot32(act_low, w_down).astype(bf16).reshape(4, quarter, D)) + b2
    result, back_second = jax.vjp(layer_norm, x_first + ff, g2, beta2)
    out_own = result.astype(bf16)

    own_cot = lax.dynamic_slice_in_dim(cotangent.reshape(tokens, D), me * quarter, quarter, 0)
    positions = z * tokens + me * quarter + jnp.arange(quarter, dtype=jnp.int32)
    d_result = own_cot.astype(f32) * (positions < length).astype(f32)[:, None]
    d_mixed, d_gain2, d_shift2 = back_second(d_result)
    d_ff_own = d_mixed.astype(bf16)
    d_bias2 = jnp.sum(d_ff_own.astype(f32), axis=0)
    d_ff = jnp.concatenate(gather_quarters(d_ff_own), axis=0)
    d_act = dot32(d_ff, w_down, ((1,), (1,)))
    _, back_gelu = jax.vjp(gelu_tanh, gate)
    d_gate = back_gelu(d_act)[0].astype(bf16)
    d_upbias = jnp.sum(d_gate.astype(f32), axis=0)
    d_first = d_mixed + scatter_sum(
        dot32(d_gate, w_up, ((1,), (1,))).astype(bf16).reshape(4, quarter, D)
    )
    d_hidden, d_gain1, d_shift1 = back_first(d_first)
    d_branch_own = d_hidden.astype(bf16)
    d_bias_out = jnp.sum(d_branch_own.astype(f32), axis=0)
    d_branch = jnp.concatenate(gather_quarters(d_branch_own), axis=0)
    d_att = dot32(d_branch, w_out, ((1,), (1,))).astype(bf16)
    out_quarters = gather_quarters(after(out_own, d_branch))
    d_query, d_kv, sums = attention_backward(
        queries, d_att, probs, kv_chunks, addr, heads_here
    )

    g_down = dot32(act_low, d_ff, ((0,), (0,))).astype(bf16)
    g_up = dot32(x_low, d_gate, ((0,), (0,))).astype(bf16)
    if packed:
        early = jnp.concatenate([jnp.zeros((edge, D), bf16), g_up, g_down], axis=0)
        early_own = lax.psum_scatter(early, OWN, scatter_dimension=0, tiled=True)
    g_out = dot32(att, d_branch, ((0,), (0,)))[pad:].astype(bf16)

    total = d_hidden
    parts = []
    for step in near_first(ctx_count)[::-1] + [0]:
        part = dot32(d_kv[step * tokens : (step + 1) * tokens], w_kv, ((1,), (1,)))
        if step == 0:
            part = part + dot32(d_query, w_q, ((1,), (1,)))
        part = part.astype(bf16)
        parts.append(part)
        mine = scatter_sum(part.reshape(4, quarter, D))
        if step:
            mine = shift_ctx(mine.astype(bf16), ctx_count - step).astype(f32)
        total = total + mine
    grad_quarters = gather_quarters(total.astype(bf16))

    d_kv_late = after(d_kv, *parts[:2])
    g_q = dot32(chunks[0], d_query, ((0,), (0,)))
    g_kv = dot32(in_all, d_kv_late, ((0,), (0,)))
    g_qkv = qkv_pack(g_q, g_kv, cols)
    outer_part = jnp.stack([d_bias_out, d_bias2, d_gain1, d_shift1, d_gain2, d_shift2], axis=0)
    inner_part = jnp.concatenate([sums[0, :cols], sums[1, pad:], d_upbias])
    outer_cols = D // owner_count
    inner_cols = inner_part.shape[0] // owner_count
    if packed:
        extra = 16
        vector = jnp.concatenate(
            [
                outer_part.reshape(6, owner_count, outer_cols)
                .transpose(1, 0, 2)
                .reshape(owner_count, -1),
                inner_part.reshape(owner_count, inner_cols),
            ],
            axis=1,
        ).astype(bf16)
        used = vector.shape[1]
        left = tops
        pieces = []
        for _ in range(3):
            piece = lax.reduce_precision(left, 8, 7)
            pieces.append(piece)
            left = left - piece
        slots = jnp.where(
            (jnp.arange(owner_count) == owner)[:, None], jnp.concatenate(pieces)[None, :], 0.0
        ).astype(bf16)
        slots = jnp.broadcast_to(slots.reshape(1, -1), (owner_count, slots.size))
        vector = jnp.stack(
            [
                jnp.pad(vector, ((0, 0), (0, D - used))),
                jnp.pad(slots, ((0, 0), (0, D - slots.shape[1]))),
            ],
            axis=1,
        )
        vector = jnp.pad(vector, ((0, 0), (0, extra - 2), (0, 0)))
        rows_of = jnp.concatenate([g_qkv, g_out], axis=0).reshape(owner_count, PB, D)
        late = jnp.concatenate([rows_of, vector], axis=1).reshape(
            shard_count, ctx_count, PB + extra, D
        )
        half = lax.dynamic_index_in_dim(late, y, 0, keepdims=False).astype(f32)
        for u in range(1, shard_count):
            sent = lax.dynamic_index_in_dim(late, (y + u) % shard_count, 0, keepdims=False)
            half = half + shift_shard(sent, u).astype(f32)
        half = half.astype(bf16)
        late_own = lax.dynamic_index_in_dim(half, z, 0, keepdims=False).astype(f32)
        for step in near_first(ctx_count):
            sent = lax.dynamic_index_in_dim(half, (z + step) % ctx_count, 0, keepdims=False)
            late_own = late_own + shift_ctx(sent, step).astype(f32)
        late_low = late_own[:PB].astype(bf16)
        own_grads = early_own + jnp.concatenate(
            [
                owner_move(
                    late_low, [(3 * d + j, d) for d in range(WIDE) if 3 * d + j < WIDE]
                )
                for j in range(3)
            ],
            axis=0,
        )
        row = late_own[PB]
        outer_own = row[: 6 * outer_cols].reshape(6, outer_cols)
        inner_own = row[6 * outer_cols : used][None, :]
        seen = late_own[PB + 1, : slots.shape[1]].reshape(owner_count, 3, heads_here)
        maxima = jnp.max(seen[:, 0] + seen[:, 1] + seen[:, 2], axis=0)
        width = WIDE
    else:
        grads = jnp.concatenate([g_qkv, g_out, g_up, g_down], axis=0)
        blocks = grads.reshape(-1, PB, WIDE, PB).transpose(0, 2, 1, 3).reshape(-1, PB, PB)
        own_grads = lax.psum_scatter(blocks, OWN, scatter_dimension=0, tiled=True)
        own_grads = own_grads.reshape(blocks_here * PB, PB)
        outer_own = lax.psum_scatter(outer_part, OWN, scatter_dimension=1, tiled=True)
        inner_own = lax.psum_scatter(inner_part[None, :], OWN, scatter_dimension=1, tiled=True)
        maxima = lax.pmax(tops, OWN)
        width = 1
    outer_own = outer_own + swap(outer_own, 1)
    outer_own = outer_own + swap(outer_own, 2)

    clip_sqrt = jnp.sqrt(tau_clip / jnp.maximum(maxima, tau_clip))
    head_factor = jnp.repeat(clip_sqrt, HEAD)
    table = jnp.concatenate([head_factor, head_factor, jnp.ones((cols,), f32)]).reshape(-1, PB)
    own_index = owner * blocks_here + jnp.arange(blocks_here, dtype=jnp.int32)
    per_row = 3 * cols // PB
    own_factor = jnp.where(
        (own_index < D // PB * per_row)[:, None], table[own_index % per_row], 1.0
    )
    block_sum, left_new, right_new, new_blocks = shampoo(
        own_grads,
        width,
        master_blocks,
        left_stats,
        right_stats,
        left_roots,
        right_roots,
        own_factor[:, None, :],
    )
    own_outer = lax.dynamic_slice_in_dim(outer_vectors, owner * outer_cols, outer_cols, 1)
    new_outer = own_outer - rate_vector * outer_own
    inner_factor = jnp.concatenate([head_factor, jnp.ones((cols + units,), f32)])
    own_inner_factor = lax.dynamic_slice_in_dim(inner_factor, owner * inner_cols, inner_cols, 0)
    own_inner = lax.dynamic_slice_in_dim(inner_biases, owner * inner_cols, inner_cols, 1)
    new_inner = (own_inner - rate_vector * inner_own) * own_inner_factor[None, :]

    def placed(quarters):
        whole = jnp.zeros((tokens, D), bf16)
        for r, piece in enumerate(quarters):
            whole = lax.dynamic_update_slice_in_dim(whole, piece, (me ^ r) * quarter, 0)
        return whole.reshape(inputs.shape)

    return (
        placed(out_quarters),
        placed(grad_quarters),
        block_sum,
        outer_own,
        inner_own,
        maxima,
        left_new,
        right_new,
        new_blocks,
        new_outer,
        new_inner,
    )


def solution(mesh):
    return jax.shard_map(
        per_device,
        mesh=mesh,
        in_specs=(
            P("shard", "ctx", None),
            P("shard"),
            P("shard", None),
            P("shard", "ctx", None),
            P(("shard", "ctx", "tp"), None, None),
            P(),
            P("tp", None),
            P(("shard", "ctx", "tp"), None, None),
            P(("shard", "ctx", "tp"), None, None),
            P(("shard", "ctx", "tp"), None, None),
            P(("shard", "ctx", "tp"), None, None),
            P("shard", "ctx", None),
        ),
        out_specs=(
            P("shard", "ctx", None),
            P("shard", "ctx", None),
            P(("shard", "ctx", "tp"), None, None),
            P(None, ("shard", "ctx")),
            P("tp", ("shard", "ctx")),
            P("tp"),
            P(("shard", "ctx", "tp"), None, None),
            P(("shard", "ctx", "tp"), None, None),
            P(("shard", "ctx", "tp"), None, None),
            P(None, ("shard", "ctx")),
            P("tp", ("shard", "ctx")),
        ),
        check_vma=False,
    )
```

profile of v0, /device:TPU:9, one launch (start us, length us, event | category | flops | bytes accessed | tf_op | source)
XLA Modules:
  0.0 375.8 jit_solution(5054185727190933717)
XLA Ops:
  14.7 4.9 %collective-permute-start.1 = (bf16[96,768]{1,0:T(8,128)(2,1)S(1)}, bf16[96,768]{1,0:T(8,128)(2,1)S(1)}, u32[]{:S(2)}, u32[]{:S(2)}) collective-permute-start(bf16[96,768]{1,0:T(8,128)(2,1)S(1)} %get-tuple-element.104), channel_id=1, source_target_pairs={{0,4},{4,16},{8,28},{1,5},{5,17},{9,29},{2,6},{6,18},{10,30},{3,7}... | collective-permute-start | bytes 442376 | tf_op jit(solution)/shard_map/ppermute | solution.py:70
  22.3 10.5 %collective-permute-done.1 = bf16[96,768]{1,0:T(8,128)(2,1)S(1)} collective-permute-done((bf16[96,768]{1,0:T(8,128)(2,1)S(1)}, bf16[96,768]{1,0:T(8,128)(2,1)S(1)}, u32[]{:S(2)}, u32[]{:S(2)}) %collective-permute-start.1) | collective-permute-done | bytes 147488 | tf_op jit(solution)/shard_map/ppermute | solution.py:70
  39.8 5.3 %collective-permute-done.4 = bf16[96,768]{1,0:T(8,128)(2,1)S(1)} collective-permute-done((bf16[96,768]{1,0:T(8,128)(2,1)S(1)}, bf16[96,768]{1,0:T(8,128)(2,1)S(1)}, u32[]{:S(2)}, u32[]{:S(2)}) %collective-permute-start.4) | collective-permute-done | bytes 147488 | tf_op jit(solution)/shard_map/ppermute | solution.py:61
  56.0 7.3 %collective-permute-done.6.far_ref = bf16[4,96,768]{2,1,0:T(8,128)(2,1)} collective-permute-done((bf16[4,96,768]{2,1,0:T(8,128)(2,1)S(1)}, bf16[4,96,768]{2,1,0:T(8,128)(2,1)}, u32[]{:S(2)}, u32[]{:S(2)}) %collective-permute-start.6) | collective-permute-done | bytes 589856 | tf_op jit(solution)/shard_map/ppermute | solution.py:66
  67.2 3.9 %collective-permute-done.17 = bf16[256,768]{1,0:T(8,128)(2,1)S(1)} collective-permute-done((bf16[256,768]{1,0:T(8,128)(2,1)S(1)}, bf16[256,768]{1,0:T(8,128)(2,1)S(1)}, u32[]{:S(2)}, u32[]{:S(2)}) %collective-permute-start.17) | collective-permute-done | bytes 393248 | tf_op jit(solution)/shard_map/ppermute | solution.py:56
  71.2 3.5 collective-permute-start.18
  82.2 3.4 collective-permute-done.13
  93.4 6.9 %attention_forward.1 = (bf16[1024,256]{1,0:T(8,128)(2,1)S(1)}, bf16[16,192,512]{2,1,0:T(8,128)(2,1)S(1)}, f32[8,128]{1,0:T(8,128)S(1)}) custom-call(s32[128]{0:T(128)S(1)} %fusion.88.addr_ref, s32[128]{0:T(128)S(1)} %select_n.238.valid_ref, s32[16]{0:T(128)S(1)} %fusion.94.query_ref, bf16[1024,256]{1,0:T(8,128)(2,1)S(1)} %fusion.38.q_ref, ...), custom_call_target="tpu_custom_call" | custom-call | flops 1610612736 | bytes 7340032 | tf_op jit(solution)/shard_map/attention_forward/pallas_call | solution.py:256
  104.9 9.4 %collective-permute-done.20 = bf16[256,768]{1,0:T(8,128)(2,1)S(1)} collective-permute-done((bf16[256,768]{1,0:T(8,128)(2,1)S(1)}, bf16[256,768]{1,0:T(8,128)(2,1)S(1)}, u32[]{:S(2)}, u32[]{:S(2)}) %collective-permute-start.20) | collective-permute-done | bytes 393248 | tf_op jit(solution)/shard_map/ppermute | solution.py:56
  117.5 7.5 %collective-permute-done.22 = bf16[256,768]{1,0:T(8,128)(2,1)S(1)} collective-permute-done((bf16[256,768]{1,0:T(8,128)(2,1)S(1)}, bf16[256,768]{1,0:T(8,128)(2,1)S(1)}, u32[]{:S(2)}, u32[]{:S(2)}) %collective-permute-start.22) | collective-permute-done | bytes 393248 | tf_op jit(solution)/shard_map/ppermute | solution.py:56
  149.1 5.3 %collective-permute-done.25 = bf16[256,768]{1,0:T(8,128)(2,1)S(1)} collective-permute-done((bf16[256,768]{1,0:T(8,128)(2,1)S(1)}, bf16[256,768]{1,0:T(8,128)(2,1)S(1)}, u32[]{:S(2)}, u32[]{:S(2)}) %collective-permute-start.25) | collective-permute-done | bytes 393248 | tf_op jit(solution)/shard_map/ppermute | solution.py:56
  159.6 6.5 %collective-permute-done.27 = bf16[256,768]{1,0:T(8,128)(2,1)S(1)} collective-permute-done((bf16[256,768]{1,0:T(8,128)(2,1)S(1)}, bf16[256,768]{1,0:T(8,128)(2,1)S(1)}, u32[]{:S(2)}, u32[]{:S(2)}) %collective-permute-start.27) | collective-permute-done | bytes 393248 | tf_op jit(solution)/shard_map/ppermute | solution.py:56
  169.1 5.2 %fusion.129 = (bf16[768]{0:T(1024)(128)(2,1)}, bf16[1024,768]{1,0:T(8,128)(2,1)S(1)}) fusion(f32[1024,768]{1,0:T(8,128)S(1)} %fusion.45, f32[768]{0:T(1024)S(1)} %slice_reduce_fusion.3, bf16[2304,768]{1,0:T(8,128)(2,1)S(1)} %copy-done.81, bf16[256,768]{1,0:T(8,128)(2,1)S(1)} %collective-permute-done.28, bf16[256,768]{1,0:T(8,128)(2,1)S(1)} %collective-permute-done.27, ...), kind=kOutput, calls=%fused_computation.306 | convolution fusion | flops 1231551744 | bytes 7476736 | tf_op jit(solution)/shard_map/dot_general | solution.py:40
  181.9 4.4 %convolution_convert_fusion.6 = bf16[768,768]{1,0:T(8,128)(2,1)S(1)} fusion(bf16[256,768]{1,0:T(8,128)(2,1)} %copy-done.90, bf16[256,768]{1,0:T(8,128)(2,1)} %copy-done.88, bf16[256,768]{1,0:T(8,128)(2,1)} %copy-done.89, bf16[256,768]{1,0:T(8,128)(2,1)} %copy-done.66, f32[1024,768]{1,0:T(8,128)} %copy-done.91, f32[768]{0:T(1024)S(1)} %slice_reduce_fusion.3), kind=kOutput, calls=%fused_computation.54 | convolution fusion | flops 1222705152 | bytes 5901312 | tf_op jit(solution)/shard_map/dot_general | solution.py:40
  189.2 7.8 %collective-permute-done.30 = bf16[256,768]{1,0:T(8,128)(2,1)S(1)} collective-permute-done((bf16[256,768]{1,0:T(8,128)(2,1)S(1)}, bf16[256,768]{1,0:T(8,128)(2,1)S(1)}, u32[]{:S(2)}, u32[]{:S(2)}) %collective-permute-start.30) | collective-permute-done | bytes 393248 | tf_op jit(solution)/shard_map/ppermute | solution.py:56
  199.4 4.5 %pad_maximum_fusion = bf16[2304,768]{1,0:T(8,128)(2,1)} fusion(bf16[768,768]{1,0:T(8,128)(2,1)S(1)} %convolution_convert_fusion.6, bf16[768,768]{1,0:T(8,128)(2,1)S(1)} %convolution_convert_fusion.7, bf16[2304]{0:T(1024)(128)(2,1)S(1)} %pad.35.clone), kind=kLoop, calls=%fused_computation.4 | loop fusion | flops 10616832 | bytes 5902848 | tf_op jit(solution)/shard_map/concatenate | solution.py:561
  214.4 11.6 %attention_backward.1 = (bf16[1024,256]{1,0:T(8,128)(2,1)S(1)}, bf16[4096,384]{1,0:T(8,128)(2,1)S(1)}, f32[8,256]{1,0:T(8,128)S(1)}) custom-call(s32[128]{0:T(128)S(1)} %fusion.88.addr_ref, bf16[1024,256]{1,0:T(8,128)(2,1)S(1)} %copy-done.11, bf16[1024,256]{1,0:T(8,128)(2,1)S(1)} %convolution_convert_fusion.8.do_ref, bf16[16,192,512]{2,1,0:T(8,128)(2,1)S(1)} %copy-done.1, ...), custom_call_target="tpu_custom_call" | custom-call | flops 3221225472 | bytes 11010048 | tf_op jit(solution)/shard_map/attention_backward/pallas_call | solution.py:337
  242.4 6.6 %fusion.131.kv_ref = f32[768,384]{1,0:T(8,128)} fusion(bf16[4096,768]{1,0:T(8,128)(2,1)} %constant_dynamic-update-slice_fusion, bf16[4096,384]{1,0:T(8,128)(2,1)S(1)} %get-tuple-element.38), kind=kOutput, calls=%fused_computation.308 | convolution fusion | flops 2415919104 | bytes 10616832 | tf_op jit(solution)/shard_map/dot_general | solution.py:40
  259.7 13.8 %collective-permute-done.51 = bf16[4,112,768]{2,1,0:T(8,128)(2,1)S(1)} collective-permute-done((bf16[4,112,768]{2,1,0:T(8,128)(2,1)S(1)}, bf16[4,112,768]{2,1,0:T(8,128)(2,1)S(1)}, u32[]{:S(2)}, u32[]{:S(2)}) %collective-permute-start.51) | collective-permute-done | bytes 688160 | tf_op jit(solution)/shard_map/ppermute | solution.py:66
  287.2 9.3 %collective-permute-done.54 = bf16[112,768]{1,0:T(8,128)(2,1)S(1)} collective-permute-done((bf16[112,768]{1,0:T(8,128)(2,1)S(1)}, bf16[112,768]{1,0:T(8,128)(2,1)S(1)}, u32[]{:S(2)}, u32[]{:S(2)}) %collective-permute-start.54) | collective-permute-done | bytes 172064 | tf_op jit(solution)/shard_map/ppermute | solution.py:61
  320.4 15.4 %collective-permute-done.39 = bf16[256,768]{1,0:T(8,128)(2,1)S(1)} collective-permute-done((bf16[256,768]{1,0:T(8,128)(2,1)}, bf16[256,768]{1,0:T(8,128)(2,1)S(1)}, u32[]{:S(2)}, u32[]{:S(2)}) %collective-permute-start.39) | collective-permute-done | bytes 393248 | tf_op jit(solution)/shard_map/ppermute | solution.py:61
  336.6 6.3 %collective-permute-done.45 = bf16[256,768]{1,0:T(8,128)(2,1)} collective-permute-done((bf16[256,768]{1,0:T(8,128)(2,1)S(1)}, bf16[256,768]{1,0:T(8,128)(2,1)}, u32[]{:S(2)}, u32[]{:S(2)}) %collective-permute-start.45) | collective-permute-done | bytes 393248 | tf_op jit(solution)/shard_map/ppermute | solution.py:61
  349.6 6.5 %collective-permute-done.49 = bf16[256,768]{1,0:T(8,128)(2,1)S(1)} collective-permute-done((bf16[256,768]{1,0:T(8,128)(2,1)S(1)}, bf16[256,768]{1,0:T(8,128)(2,1)S(1)}, u32[]{:S(2)}, u32[]{:S(2)}) %collective-permute-start.49) | collective-permute-done | bytes 393248 | tf_op jit(solution)/shard_map/ppermute | solution.py:56
  361.8 6.7 %shampoo.1 = (f32[24,96,96]{2,1,0:T(8,128)}, f32[24,96,96]{2,1,0:T(8,128)}, f32[24,96,96]{2,1,0:T(8,128)}, f32[24,96,96]{2,1,0:T(8,128)}) custom-call(bf16[288,768]{1,0:T(8,128)(2,1)} %maximum_add_fusion.g_ref, f32[24,96,96]{2,1,0:T(8,128)} %mb_ref.1, f32[24,96,96]{2,1,0:T(8,128)} %ls_ref.1, f32[24,96,96]{2,1,0:T(8,128)} %rs_ref.1, f32[24,96,96]{2,1,0:T(8,128)} %lr_ref.1, ...), custom_call_target="tpu_custom_call" | custom-call | tf_op jit(solution)/shard_map/shampoo/pallas_call | solution.py:400
  (472 shorter events, 186.6 us)
Async XLA Ops:
  7.2 122.6 %all-gather.2.cloned.1.call-start = ((), (), s32[]{:S(2)}) async-start(), calls=%async_computation.1 | async-start | bytes 3981312 | tf_op jit(solution)/shard_map/all_gather | solution.py:465
  9.2 46.6 %collective-permute-start.15 = (bf16[256,768]{1,0:T(8,128)(2,1)S(1)}, bf16[256,768]{1,0:T(8,128)(2,1)S(1)}, u32[]{:S(2)}, u32[]{:S(2)}) collective-permute-start(bf16[256,768]{1,0:T(8,128)(2,1)S(1)} %get-tuple-element.30), channel_id=1, source_target_pairs={{0,12},{4,0},{8,4},{12,8},{1,13},{5,1},{9,5},{13,9},{2,14},{6,2},{... | collective-permute-start | bytes 1179656 | tf_op jit(solution)/shard_map/ppermute | solution.py:61
  9.2 45.2 %collective-permute-start.7 = (bf16[256,768]{1,0:T(8,128)(2,1)S(1)}, bf16[256,768]{1,0:T(8,128)(2,1)}, u32[]{:S(2)}, u32[]{:S(2)}) collective-permute-start(bf16[256,768]{1,0:T(8,128)(2,1)S(1)} %get-tuple-element.30), channel_id=1, source_target_pairs={{0,4},{4,8},{8,12},{12,0},{1,5},{5,9},{9,13},{13,1},{2,6},{6,10},{... | collective-permute-start | bytes 1179656 | tf_op jit(solution)/shard_map/ppermute | solution.py:61
  14.7 18.1 %collective-permute-start.1 = (bf16[96,768]{1,0:T(8,128)(2,1)S(1)}, bf16[96,768]{1,0:T(8,128)(2,1)S(1)}, u32[]{:S(2)}, u32[]{:S(2)}) collective-permute-start(bf16[96,768]{1,0:T(8,128)(2,1)S(1)} %get-tuple-element.104), channel_id=1, source_target_pairs={{0,4},{4,16},{8,28},{1,5},{5,17},{9,29},{2,6},{6,18},{10,30},{3,7}... | collective-permute-start | bytes 442376 | tf_op jit(solution)/shard_map/ppermute | solution.py:70
  54.4 20.3 %collective-permute-start.11 = (bf16[256,768]{1,0:T(8,128)(2,1)S(1)}, bf16[256,768]{1,0:T(8,128)(2,1)}, u32[]{:S(2)}, u32[]{:S(2)}) collective-permute-start(bf16[256,768]{1,0:T(8,128)(2,1)S(1)} %get-tuple-element.30), channel_id=1, source_target_pairs={{0,8},{4,12},{8,0},{12,4},{1,9},{5,13},{9,1},{13,5},{2,10},{6,14},... | collective-permute-start | bytes 1179656 | tf_op jit(solution)/shard_map/ppermute | solution.py:61
  54.5 21.5 %collective-permute-start.9 = (bf16[256,768]{1,0:T(8,128)(2,1)}, bf16[256,768]{1,0:T(8,128)(2,1)}, u32[]{:S(2)}, u32[]{:S(2)}) collective-permute-start(bf16[256,768]{1,0:T(8,128)(2,1)} %collective-permute-done.7), channel_id=1, source_target_pairs={{0,2},{1,3},{2,0},{3,1},{4,6},{5,7},{6,4},{7,5},{8,10},{9,11},{10,... | collective-permute-start | bytes 1179656 | tf_op jit(solution)/shard_map/ppermute | solution.py:56
  63.3 296.5 %reduce-scatter.2.cloned.1.call-start = ((), (), s32[]{:S(2)}) async-start(), calls=%async_computation.2 | async-start | bytes 3981312 | tf_op jit(solution)/shard_map/reduce_scatter | solution.py:562
  64.5 24.2 %collective-permute-start.16 = (bf16[256,768]{1,0:T(8,128)(2,1)S(1)}, bf16[256,768]{1,0:T(8,128)(2,1)S(1)}, u32[]{:S(2)}, u32[]{:S(2)}) collective-permute-start(bf16[256,768]{1,0:T(8,128)(2,1)S(1)} %collective-permute-done.15), channel_id=1, source_target_pairs={{0,1},{1,0},{2,3},{3,2},{4,5},{5,4},{6,7},{7,6},{8,9},{9,8},{10,11... | collective-permute-start | bytes 1179656 | tf_op jit(solution)/shard_map/ppermute | solution.py:56
  71.2 17.6 %collective-permute-start.18 = (bf16[256,768]{1,0:T(8,128)(2,1)S(1)}, bf16[256,768]{1,0:T(8,128)(2,1)S(1)}, u32[]{:S(2)}, u32[]{:S(2)}) collective-permute-start(bf16[256,768]{1,0:T(8,128)(2,1)S(1)} %collective-permute-done.17), channel_id=1, source_target_pairs={{0,1},{1,0},{2,3},{3,2},{4,5},{5,4},{6,7},{7,6},{8,9},{9,8},{10,11... | collective-permute-start | bytes 1179656 | tf_op jit(solution)/shard_map/ppermute | solution.py:56
  212.5 45.9 %collective-permute-start.35 = (bf16[256,768]{1,0:T(8,128)(2,1)S(1)}, bf16[256,768]{1,0:T(8,128)(2,1)}, u32[]{:S(2)}, u32[]{:S(2)}) collective-permute-start(bf16[256,768]{1,0:T(8,128)(2,1)S(1)} %get-tuple-element.34), channel_id=1, source_target_pairs={{0,2},{1,3},{2,0},{3,1},{4,6},{5,7},{6,4},{7,5},{8,10},{9,11},{10,... | collective-permute-start | bytes 1179656 | tf_op jit(solution)/shard_map/ppermute | solution.py:56
  213.7 42.9 %collective-permute-start.34 = (bf16[256,768]{1,0:T(8,128)(2,1)S(1)}, bf16[256,768]{1,0:T(8,128)(2,1)}, u32[]{:S(2)}, u32[]{:S(2)}) collective-permute-start(bf16[256,768]{1,0:T(8,128)(2,1)S(1)} %get-tuple-element.34), channel_id=1, source_target_pairs={{0,1},{1,0},{2,3},{3,2},{4,5},{5,4},{6,7},{7,6},{8,9},{9,8},{10,11... | collective-permute-start | bytes 1179656 | tf_op jit(solution)/shard_map/ppermute | solution.py:56
  242.2 33.9 %collective-permute-start.40 = (bf16[512,768]{1,0:T(8,128)(2,1)S(1)}, bf16[512,768]{1,0:T(8,128)(2,1)}, u32[]{:S(2)}, u32[]{:S(2)}) collective-permute-start(bf16[512,768]{1,0:T(8,128)(2,1)S(1)} %pad_maximum_fusion.10), channel_id=1, source_target_pairs={{0,1},{1,0},{2,3},{3,2},{4,5},{5,4},{6,7},{7,6},{8,9},{9,8},{10,11... | collective-permute-start | bytes 2359304 | tf_op jit(solution)/shard_map/ppermute | solution.py:56
  253.2 20.2 %collective-permute-start.51 = (bf16[4,112,768]{2,1,0:T(8,128)(2,1)S(1)}, bf16[4,112,768]{2,1,0:T(8,128)(2,1)S(1)}, u32[]{:S(2)}, u32[]{:S(2)}) collective-permute-start(bf16[4,112,768]{2,1,0:T(8,128)(2,1)S(1)} %fusion.59), channel_id=1, source_target_pairs={{0,16},{16,0},{1,17},{17,1},{2,18},{18,2},{3,19},{19,3},{4,20},{20... | collective-permute-start | bytes 2064392 | tf_op jit(solution)/shard_map/ppermute | solution.py:66
  253.5 25.5 %collective-permute-start.37 = (bf16[512,768]{1,0:T(8,128)(2,1)S(1)}, bf16[512,768]{1,0:T(8,128)(2,1)S(1)}, u32[]{:S(2)}, u32[]{:S(2)}) collective-permute-start(bf16[512,768]{1,0:T(8,128)(2,1)S(1)} %pad_maximum_fusion.9), channel_id=1, source_target_pairs={{0,1},{1,0},{2,3},{3,2},{4,5},{5,4},{6,7},{7,6},{8,9},{9,8},{10,11... | collective-permute-start | bytes 2359304 | tf_op jit(solution)/shard_map/ppermute | solution.py:56
  256.6 24.6 %collective-permute-start.43 = (bf16[512,768]{1,0:T(8,128)(2,1)S(1)}, bf16[512,768]{1,0:T(8,128)(2,1)S(1)}, u32[]{:S(2)}, u32[]{:S(2)}) collective-permute-start(bf16[512,768]{1,0:T(8,128)(2,1)S(1)} %pad_maximum_fusion.11), channel_id=1, source_target_pairs={{0,1},{1,0},{2,3},{3,2},{4,5},{5,4},{6,7},{7,6},{8,9},{9,8},{10,11... | collective-permute-start | bytes 2359304 | tf_op jit(solution)/shard_map/ppermute | solution.py:56
  258.3 23.8 %collective-permute-start.46 = (bf16[512,768]{1,0:T(8,128)(2,1)S(1)}, bf16[512,768]{1,0:T(8,128)(2,1)S(1)}, u32[]{:S(2)}, u32[]{:S(2)}) collective-permute-start(bf16[512,768]{1,0:T(8,128)(2,1)S(1)} %pad_maximum_fusion.12), channel_id=1, source_target_pairs={{0,1},{1,0},{2,3},{3,2},{4,5},{5,4},{6,7},{7,6},{8,9},{9,8},{10,11... | collective-permute-start | bytes 2359304 | tf_op jit(solution)/shard_map/ppermute | solution.py:56
  284.2 17.6 %collective-permute-start.38 = (bf16[256,768]{1,0:T(8,128)(2,1)}, bf16[256,768]{1,0:T(8,128)(2,1)}, u32[]{:S(2)}, u32[]{:S(2)}) collective-permute-start(bf16[256,768]{1,0:T(8,128)(2,1)} %add_convert_fusion.12), channel_id=1, source_target_pairs={{0,2},{1,3},{2,0},{3,1},{4,6},{5,7},{6,4},{7,5},{8,10},{9,11},{10,... | collective-permute-start | bytes 1179656 | tf_op jit(solution)/shard_map/ppermute | solution.py:56
  285.9 23.6 %collective-permute-start.44 = (bf16[256,768]{1,0:T(8,128)(2,1)}, bf16[256,768]{1,0:T(8,128)(2,1)}, u32[]{:S(2)}, u32[]{:S(2)}) collective-permute-start(bf16[256,768]{1,0:T(8,128)(2,1)} %add_convert_fusion.8), channel_id=1, source_target_pairs={{0,2},{1,3},{2,0},{3,1},{4,6},{5,7},{6,4},{7,5},{8,10},{9,11},{10,... | collective-permute-start | bytes 1179656 | tf_op jit(solution)/shard_map/ppermute | solution.py:56
  296.5 21.4 %collective-permute-start.47 = (bf16[256,768]{1,0:T(8,128)(2,1)}, bf16[256,768]{1,0:T(8,128)(2,1)}, u32[]{:S(2)}, u32[]{:S(2)}) collective-permute-start(bf16[256,768]{1,0:T(8,128)(2,1)} %add_convert_fusion.6), channel_id=1, source_target_pairs={{0,2},{1,3},{2,0},{3,1},{4,6},{5,7},{6,4},{7,5},{8,10},{9,11},{10,... | collective-permute-start | bytes 1179656 | tf_op jit(solution)/shard_map/ppermute | solution.py:56
  303.8 32.1 %collective-permute-start.39 = (bf16[256,768]{1,0:T(8,128)(2,1)}, bf16[256,768]{1,0:T(8,128)(2,1)S(1)}, u32[]{:S(2)}, u32[]{:S(2)}) collective-permute-start(bf16[256,768]{1,0:T(8,128)(2,1)} %add_convert_fusion.11), channel_id=1, source_target_pairs={{0,8},{4,12},{8,0},{12,4},{1,9},{5,13},{9,1},{13,5},{2,10},{6,14},... | collective-permute-start | bytes 1179656 | tf_op jit(solution)/shard_map/ppermute | solution.py:61
  310.7 32.2 %collective-permute-start.45 = (bf16[256,768]{1,0:T(8,128)(2,1)S(1)}, bf16[256,768]{1,0:T(8,128)(2,1)}, u32[]{:S(2)}, u32[]{:S(2)}) collective-permute-start(bf16[256,768]{1,0:T(8,128)(2,1)S(1)} %add_convert_fusion.7), channel_id=1, source_target_pairs={{0,12},{4,0},{8,4},{12,8},{1,13},{5,1},{9,5},{13,9},{2,14},{6,2},{... | collective-permute-start | bytes 1179656 | tf_op jit(solution)/shard_map/ppermute | solution.py:61
  314.1 44.3 %collective-permute-start.56 = (bf16[96,768]{1,0:T(8,128)(2,1)S(1)}, bf16[96,768]{1,0:T(8,128)(2,1)S(1)}, u32[]{:S(2)}, u32[]{:S(2)}) collective-permute-start(bf16[96,768]{1,0:T(8,128)(2,1)S(1)} %slice.463), channel_id=1, source_target_pairs={{4,0},{16,4},{28,8},{5,1},{17,5},{29,9},{6,2},{18,6},{30,10},{7,3}... | collective-permute-start | bytes 442376 | tf_op jit(solution)/shard_map/ppermute | solution.py:70
  317.9 40.6 %collective-permute-start.55 = (bf16[96,768]{1,0:T(8,128)(2,1)S(1)}, bf16[96,768]{1,0:T(8,128)(2,1)S(1)}, u32[]{:S(2)}, u32[]{:S(2)}) collective-permute-start(bf16[96,768]{1,0:T(8,128)(2,1)S(1)} %slice.463), channel_id=1, source_target_pairs={{0,0},{12,4},{24,8},{1,1},{13,5},{25,9},{2,2},{14,6},{26,10},{3,3}... | collective-permute-start | bytes 442376 | tf_op jit(solution)/shard_map/ppermute | solution.py:70
  319.2 27.8 %collective-permute-start.59 = (f32[6,96]{1,0:T(8,128)S(1)}, f32[6,96]{1,0:T(8,128)S(1)}, u32[]{:S(2)}, u32[]{:S(2)}) collective-permute-start(f32[6,96]{1,0:T(8,128)S(1)} %add.664), channel_id=1, source_target_pairs={{0,2},{1,3},{2,0},{3,1},{4,6},{5,7},{6,4},{7,5},{8,10},{9,11},{10,... | collective-permute-start | bytes 6920 | tf_op jit(solution)/shard_map/ppermute | solution.py:56
  (133 other events, 1473.1 us)
Sparse Core Ops, SparseCore 0:
  63.4 66.3 all-gather.1
  204.1 82.5 reduce-scatter.1
where the time goes:
time: 382 us; the launch traced here: 376 us
  waiting for transfers between devices  138 us (36%)
  starting transfers between devices  71.6 us (19%)
  matrix products  43 us (11%)
  local copies, waits for them, and re-layouts  39.1 us (10%)
  other arithmetic  33.9 us (9%)
  Pallas kernels  33.8 us (9%)
  between operations  16.7 us (4%)
    ppermute x40, waiting for transfers between devices, swap(): return lax.ppermute(rows, 'tp', [(i, i ^ mask) for i in range(count)])  62.4 us
    ppermute x40, starting transfers between devices, swap(): return lax.ppermute(rows, 'tp', [(i, i ^ mask) for i in range(count)])  43.2 us
    dot_general x21, matrix products, dot32(): lax.dot_general(left, right, (dims, ((), ())), preferred_element_type=f32)  43 us
    ppermute x12, waiting for transfers between devices, shift_ctx(): lax.ppermute(rows, 'ctx', [(i, (i + step) % count) for i in range(count)])  41.9 us
    unnamed x209, local copies, waits for them, and re-layouts  23 us
    ppermute x2, waiting for transfers between devices, shift_shard(): lax.ppermute(rows, 'shard', [(i, (i + step) % count) for i in range(count)])  21.1 us
    ppermute x12, starting transfers between devices, shift_ctx(): lax.ppermute(rows, 'ctx', [(i, (i + step) % count) for i in range(count)])  14 us
    ppermute x6, starting transfers between devices, owner_move(): return lax.ppermute(rows, OWN, pairs)  12.6 us
  transfers between devices with their start and end apart: 62, of which 28 were waited for; matrix products, arithmetic and copies ran while one was open for 24% of the time, Pallas kernels for 7%

commit v1 on v0

v1 whole, which is shorter than its diff:
```python
import functools

import jax
import jax.numpy as jnp
from jax import lax
from jax.experimental import pallas as pl
from jax.experimental.pallas import tpu as pltpu
from jax.sharding import PartitionSpec as P


D = 768
HEADS = 12
HEAD = 64
BLOCK = 64
SEQ = 4096
PB = 96
LIST = 8
WIDE = 8

eps_norm = 1e-06
tau_clip = 9.0
rate_matrix = 0.3
rate_vector = 0.001
neg_large = -1e30
GELU = 0.7978845608028654
ANY = pl.ANY
bf16 = jnp.bfloat16
f32 = jnp.float32
OWN = ("shard", "ctx")


def params_of(mib, **more):
    return pltpu.CompilerParams(vmem_limit_bytes=mib << 20, **more)


def in_place():
    return pl.BlockSpec(memory_space=ANY)


def whole_block(shape, single=False):
    zeros = (0,) * len(shape)
    mode = dict(pipeline_mode=pl.Buffered(1)) if single else {}
    return pl.BlockSpec(shape, lambda *_: zeros, **mode)


def cost(flops, moved, exps=0):
    return pl.CostEstimate(flops=flops, bytes_accessed=moved, transcendentals=exps)


def dot32(left, right, dims=((1,), (0,))):
    return lax.dot_general(left, right, (dims, ((), ())), preferred_element_type=f32)


def normalized(values):
    centred = values - jnp.mean(values, axis=-1, keepdims=True)
    factor = lax.rsqrt(jnp.mean(centred * centred, axis=-1, keepdims=True) + eps_norm)
    return centred * factor, factor


def norm_back(grad, gain, unit, factor):
    scaled = grad * gain
    mean_grad = jnp.mean(scaled, axis=-1, keepdims=True)
    mean_unit = jnp.mean(scaled * unit, axis=-1, keepdims=True)
    return factor * (scaled - mean_grad - unit * mean_unit)


def column_sum(values):
    return jnp.sum(values, axis=0, keepdims=True)


def gelu_parts(gate):
    inner = GELU * (gate + 0.044715 * gate * gate * gate)
    return inner, jnp.tanh(inner)


def copy_in(source, target, sem):
    copy = pltpu.make_async_copy(source, target, sem)
    copy.start()
    return copy


def swap(rows, mask):
    count = lax.axis_size("tp")
    return lax.ppermute(rows, "tp", [(i, i ^ mask) for i in range(count)])


def shift_ctx(rows, step):
    count = lax.axis_size("ctx")
    return lax.ppermute(rows, "ctx", [(i, (i + step) % count) for i in range(count)])


def shift_shard(rows, step):
    count = lax.axis_size("shard")
    return lax.ppermute(rows, "shard", [(i, (i + step) % count) for i in range(count)])


def owner_move(rows, pairs):
    return lax.ppermute(rows, OWN, pairs)


def after(value, *others):
    return lax.optimization_barrier((value,) + others)[0]


def near_first(count):
    return sorted(range(1, count), key=lambda step: min(step, count - step))


def pack_kernel(blocks_ref, out_ref):
    for j in range(WIDE):
        out_ref[:, PB * j : PB * (j + 1)] = blocks_ref[j].astype(bf16)


def pack_rows(blocks):
    rows = blocks.shape[0] // WIDE
    return pl.pallas_call(
        pack_kernel,
        grid=(rows,),
        in_specs=[pl.BlockSpec((WIDE, PB, PB), lambda i: (i, 0, 0))],
        out_specs=pl.BlockSpec((PB, PB * WIDE), lambda i: (i, 0)),
        out_shape=jax.ShapeDtypeStruct((rows * PB, PB * WIDE), bf16),
        compiler_params=params_of(3),
        name="pack_rows",
    )(blocks)


def unpack_kernel(turn_ref, near_ref, far_ref, q_ref, kv_ref, out_ref, all_ref, *, cols):
    half = near_ref.shape[0]
    all_ref[:half] = near_ref[...]
    all_ref[half:] = far_ref[...]
    q_ref[...] = jnp.zeros(q_ref.shape, bf16)
    for i in range(D // PB):
        for c in range(3):
            unit = 3 * i + c
            piece = all_ref[turn_ref[unit // 4], :, cols * (unit % 4) : cols * (unit % 4 + 1)]
            if c == 0:
                q_ref[PB * i : PB * (i + 1), :cols] = piece
            else:
                kv_ref[PB * i : PB * (i + 1), cols * (c - 1) : cols * c] = piece
    pad = out_ref.shape[0] - cols
    out_ref[:pad, :] = jnp.zeros((pad, D), bf16)
    for i in range(cols // PB):
        out_ref[pad + PB * i : pad + PB * (i + 1), :] = all_ref[turn_ref[3 * cols // PB + i]]


def unpack_first(turns, near, far, cols, wide):
    full = pl.BlockSpec(memory_space=pltpu.VMEM)
    return pl.pallas_call(
        functools.partial(unpack_kernel, cols=cols),
        in_specs=[pl.BlockSpec(memory_space=pltpu.SMEM), full, full],
        out_specs=[full, full, full],
        out_shape=(
            jax.ShapeDtypeStruct((D, wide), bf16),
            jax.ShapeDtypeStruct((D, 2 * cols), bf16),
            jax.ShapeDtypeStruct((wide, D), bf16),
        ),
        scratch_shapes=[pltpu.VMEM((near.shape[0] + far.shape[0], PB, D), bf16)],
        compiler_params=params_of(8),
        name="unpack_first",
    )(turns, near, far)


def tables_kernel(
    ids_ref, len_ref, glob_ref, rand_ref, addr_ref, valid_ref, query_ref, turn_ref, *, rows_blocks, ctx_count, shard_count
):
    me, y, z, owner = ids_ref[0], ids_ref[1], ids_ref[2], ids_ref[3]
    per = rows_blocks // 4
    length = len_ref[0]
    block_count = SEQ // BLOCK

    def body(i, carry):
        place = (lax.div(i, per) ^ me) * per + lax.rem(i, per)
        row = z * rows_blocks + place
        listed = [row - 1, row, row + 1, glob_ref[0, 0], glob_ref[0, 1]]
        listed += [rand_ref[place, n] for n in range(3)]
        for e, block in enumerate(listed):
            held = jnp.clip(block, 0, block_count - 1)
            valid = jnp.clip(length - block * BLOCK, 0, BLOCK)
            valid_ref[i * LIST + e] = jnp.where(held == block, valid, 0)
            chunk = lax.div(held, rows_blocks)
            local = held - chunk * rows_blocks
            step = lax.rem(z - chunk + ctx_count, ctx_count)
            part = lax.div(local, per)
            addr_ref[i * LIST + e] = (
                step * rows_blocks + (part ^ me) * per + (local - part * per)
            )
        query_ref[i] = jnp.clip(length - row * BLOCK, 0, BLOCK)
        return carry

    lax.fori_loop(0, rows_blocks, body, 0)
    for k in range(WIDE):
        ky, kz = k // ctx_count, k % ctx_count
        turn_ref[k] = lax.rem(y - ky + shard_count, shard_count) * ctx_count + lax.rem(
            z - kz + ctx_count, ctx_count
        )
        turn_ref[WIDE + k] = lax.rem(ky - y + shard_count, shard_count) * ctx_count + lax.rem(
            kz - z + ctx_count, ctx_count
        )
        turn_ref[2 * WIDE + k] = lax.rem(y - ky + shard_count, shard_count) * ctx_count + lax.rem(
            z - kz + ctx_count, ctx_count
        )
    turn_ref[3 * WIDE] = owner
    turn_ref[3 * WIDE + 1] = me
    tokens = rows_blocks * BLOCK
    quarter = tokens // 4
    turn_ref[3 * WIDE + 2] = jnp.clip(length - z * tokens - me * quarter, 0, quarter)


def index_tables(ids, lengths, global_blocks, random_blocks, rows_blocks, ctx_count, shard_count):
    smem = pl.BlockSpec(memory_space=pltpu.SMEM)
    shapes = [(rows_blocks * LIST,), (rows_blocks * LIST,), (rows_blocks,), (3 * WIDE + 8,)]
    return pl.pallas_call(
        functools.partial(
            tables_kernel, rows_blocks=rows_blocks, ctx_count=ctx_count, shard_count=shard_count
        ),
        in_specs=[smem] * 4,
        out_specs=[smem] * 4,
        out_shape=[jax.ShapeDtypeStruct(shape, jnp.int32) for shape in shapes],
        compiler_params=params_of(2),
        name="index_tables",
    )(ids, lengths, global_blocks, random_blocks)


def pick_kernel(ids_ref, x_ref, out_ref):
    out_ref[...] = x_ref[...]


def pick_quarter(ids, values):
    rows = values.shape[0] // 4
    return pl.pallas_call(
        pick_kernel,
        grid_spec=pltpu.PrefetchScalarGridSpec(
            num_scalar_prefetch=1,
            grid=(1,),
            in_specs=[pl.BlockSpec((rows, D), lambda i, ids: (ids[0], 0))],
            out_specs=pl.BlockSpec((rows, D), lambda i, ids: (0, 0)),
        ),
        out_shape=jax.ShapeDtypeStruct((rows, D), bf16),
        compiler_params=params_of(3),
        name="pick_quarter",
    )(ids, values)


def place_kernel(ids_ref, *refs):
    pieces, (out_ref, sem) = refs[:4], refs[4:]
    rows = pieces[0].shape[0]
    loads = []
    for r, piece in enumerate(pieces):
        start = pl.multiple_of((ids_ref[0] ^ r) * rows, rows)
        loads.append(copy_in(piece, out_ref.at[pl.ds(start, rows)], sem.at[r]))
    for load in loads:
        load.wait()


def place_quarters(ids, pieces):
    rows = pieces[0].shape[0]
    return pl.pallas_call(
        place_kernel,
        grid_spec=pltpu.PrefetchScalarGridSpec(
            num_scalar_prefetch=1,
            grid=(1,),
            in_specs=[in_place()] * 4,
            out_specs=whole_block((4 * rows, D), single=True),
            scratch_shapes=[pltpu.SemaphoreType.DMA((4,))],
        ),
        out_shape=jax.ShapeDtypeStruct((4 * rows, D), bf16),
        compiler_params=params_of(4),
    )(ids, *pieces)


def sort_kernel(turn_ref, a_ref, b_ref, c_ref, first_ref, rest_ref):
    for group in range(3):
        slot = lax.rem(WIDE * group + turn_ref[3 * WIDE], 3)
        value = jnp.where(slot == 0, a_ref[...], jnp.where(slot == 1, b_ref[...], c_ref[...]))
        if group == 0:
            first_ref[...] = value
        else:
            rest_ref[PB * (group - 1) : PB * group] = value


def sort_held(turns, held):
    return pl.pallas_call(
        sort_kernel,
        grid_spec=pltpu.PrefetchScalarGridSpec(
            num_scalar_prefetch=1,
            grid=(1,),
            in_specs=[whole_block((PB, D))] * 3,
            out_specs=[whole_block((PB, D)), whole_block((2 * PB, D))],
        ),
        out_shape=[
            jax.ShapeDtypeStruct((PB, D), bf16),
            jax.ShapeDtypeStruct((2 * PB, D), bf16),
        ],
        compiler_params=params_of(4),
        name="sort_held",
    )(turns, *held)


def deal_kernel(turn_ref, first_ref, up_ref, down_ref, a_ref, b_ref, c_ref):
    groups = (first_ref[:PB].astype(bf16), up_ref[...].astype(bf16), down_ref[...].astype(bf16))
    for slot, out_ref in enumerate((a_ref, b_ref, c_ref)):
        target = lax.rem(3 * (turn_ref[3 * WIDE] + WIDE - slot), WIDE)
        group = lax.div(3 * target + slot, WIDE)
        out_ref[...] = jnp.where(group == 0, groups[0], jnp.where(group == 1, groups[1], groups[2]))


def deal_rows(turns, first, up, down):
    one = whole_block((PB, D))
    return pl.pallas_call(
        deal_kernel,
        grid_spec=pltpu.PrefetchScalarGridSpec(
            num_scalar_prefetch=1,
            grid=(1,),
            in_specs=[whole_block(first.shape), one, one],
            out_specs=[one] * 3,
        ),
        out_shape=[jax.ShapeDtypeStruct((PB, D), bf16)] * 3,
        compiler_params=params_of(6),
        name="deal_rows",
    )(turns, first, up, down)


def project_kernel(ids_ref, *refs, step, heads_q, chained):
    count = 1 if heads_q else 4
    pieces = refs[:count]
    rest = list(refs[count:])
    wkv_ref, bkv_ref = rest[:2]
    rest = rest[2:]
    if heads_q:
        wq_ref, bq_ref = rest[:2]
        rest = rest[2:]
    if chained:
        rest = rest[2:]
    in_all, kv_all = rest[:2]
    rest = rest[2:]
    if heads_q:
        q_ref = rest[0]
        rest = rest[1:]
    x_ref, kv_ref, sem, out_sem = rest
    tokens = x_ref.shape[0]
    rows = tokens // 4
    loads = []
    for r in range(4):
        if heads_q:
            source = pieces[0].at[pl.ds(pl.multiple_of((ids_ref[0] ^ r) * rows, rows), rows)]
        else:
            source = pieces[r]
        loads.append(copy_in(source, x_ref.at[pl.ds(r * rows, rows)], sem.at[r]))
    for load in loads:
        load.wait()
    saves = [copy_in(x_ref, in_all.at[pl.ds(step * tokens, tokens)], out_sem.at[0])]

    def body(r, carry):
        mine = pl.ds(pl.multiple_of(r * rows, rows), rows)
        kv_ref[mine, :] = (dot32(x_ref[mine, :], wkv_ref[...]) + bkv_ref[...]).astype(bf16)
        if heads_q:
            q_ref[mine, :] = (dot32(x_ref[mine, :], wq_ref[...]) + bq_ref[...]).astype(bf16)
        return carry

    lax.fori_loop(0, 4, body, 0)
    saves.append(copy_in(kv_ref, kv_all.at[pl.ds(step * tokens, tokens)], out_sem.at[1]))
    for save in saves:
        save.wait()


def project_chunk(ids, pieces, step, count, w_kv, b_kv, w_q, b_q, carried):
    width = pieces[0].shape[1]
    tokens = pieces[0].shape[0] * len(pieces)
    kv_cols = w_kv.shape[1]
    with_q = w_q is not None
    chained = carried is not None
    args = list(pieces) + [w_kv, b_kv]
    specs = [in_place()] * len(pieces) + [whole_block(w_kv.shape), whole_block(b_kv.shape)]
    if with_q:
        args += [w_q, b_q]
        specs += [whole_block(w_q.shape), whole_block(b_q.shape)]
    aliases = {}
    if chained:
        aliases = {len(args) + 1: 0, len(args) + 2: 1}
        args += list(carried)
        specs += [in_place()] * 2
    shapes = [
        jax.ShapeDtypeStruct((count * tokens, width), bf16),
        jax.ShapeDtypeStruct((count * tokens, kv_cols), bf16),
    ]
    outs = [in_place()] * 2
    if with_q:
        shapes.append(jax.ShapeDtypeStruct((tokens, w_q.shape[1]), bf16))
        outs.append(whole_block((tokens, w_q.shape[1])))
    return pl.pallas_call(
        functools.partial(project_kernel, step=step, heads_q=with_q, chained=chained),
        grid_spec=pltpu.PrefetchScalarGridSpec(
            num_scalar_prefetch=1,
            grid=(1,),
            in_specs=specs,
            out_specs=outs,
            scratch_shapes=[
                pltpu.VMEM((tokens, width), bf16),
                pltpu.VMEM((tokens, kv_cols), bf16),
                pltpu.SemaphoreType.DMA((4,)),
                pltpu.SemaphoreType.DMA((2,)),
            ],
        ),
        out_shape=shapes,
        input_output_aliases=aliases,
        compiler_params=params_of(8),
        cost_estimate=cost(2 * tokens * width * kv_cols, 4 * tokens * (width + kv_cols)),
    )(ids, *args)


def split_store(r, value, keep_ref, send_ref):
    @pl.when(r % 2 == 0)
    def _():
        keep_ref[...] = value

    @pl.when(r % 2 == 1)
    def _():
        send_ref[...] = value


def out_kernel(att_ref, w_ref, keep_ref, send_ref):
    split_store(
        pl.program_id(0), dot32(att_ref[...], w_ref[...]).astype(bf16), keep_ref, send_ref
    )


def out_project(att, w_out):
    tokens, wide = att.shape
    rows = tokens // 4
    half = pl.BlockSpec((rows, D), lambda r: (r // 2, 0))
    shape = jax.ShapeDtypeStruct((tokens // 2, D), bf16)
    return pl.pallas_call(
        out_kernel,
        grid=(4,),
        in_specs=[pl.BlockSpec((rows, wide), lambda r: (r, 0)), whole_block(w_out.shape)],
        out_specs=[half, half],
        out_shape=[shape, shape],
        compiler_params=params_of(4),
        cost_estimate=cost(2 * tokens * wide * D, 2 * tokens * (wide + D)),
        name="out_project",
    )(att, w_out)


def summed(keep_ref, sent_ref, got_ref):
    return keep_ref[...].astype(f32) + sent_ref[...].astype(f32) + got_ref[...].astype(f32)


def first_norm_kernel(ids_ref, x_ref, keep_ref, sent_ref, got_ref, vec_ref, hid_ref, x1_ref, low_ref):
    hidden = x_ref[...].astype(f32) + (summed(keep_ref, sent_ref, got_ref) + vec_ref[0:1, :])
    hid_ref[...] = hidden
    unit, _ = normalized(hidden)
    x1 = unit * vec_ref[2:3, :] + vec_ref[3:4, :]
    x1_ref[...] = x1
    low_ref[...] = x1.astype(bf16)


def norm_tiles(rows):
    return 4 if rows % 64 == 0 else 1


def first_norm(ids, values, keep, sent, got, vectors):
    rows = got.shape[0]
    tiles = norm_tiles(rows)
    block = pl.BlockSpec((rows // tiles, D), lambda i, ids: (i, 0))
    mine = pl.BlockSpec((rows // tiles, D), lambda i, ids: (ids[0] * tiles + i, 0))
    return pl.pallas_call(
        first_norm_kernel,
        grid_spec=pltpu.PrefetchScalarGridSpec(
            num_scalar_prefetch=1,
            grid=(tiles,),
            in_specs=[mine] + [block] * 3 + [whole_block(vectors.shape)],
            out_specs=[block] * 3,
        ),
        out_shape=[
            jax.ShapeDtypeStruct((rows, D), f32),
            jax.ShapeDtypeStruct((rows, D), f32),
            jax.ShapeDtypeStruct((rows, D), bf16),
        ],
        compiler_params=params_of(5),
        cost_estimate=cost(20 * rows * D, 20 * rows * D),
        name="first_norm",
    )(ids, values, keep, sent, got, vectors)


def second_norm_kernel(
    turn_ref, x1_ref, keep_ref, sent_ref, got_ref, cot_ref, vec_ref, out_ref, dmix_ref, low_ref, sums_ref
):
    i = pl.program_id(0)

    @pl.when(i == 0)
    def _():
        sums_ref[...] = jnp.zeros(sums_ref.shape, f32)

    mixed = x1_ref[...] + (summed(keep_ref, sent_ref, got_ref) + vec_ref[1:2, :])
    unit, factor = normalized(mixed)
    out_ref[...] = (unit * vec_ref[4:5, :] + vec_ref[5:6, :]).astype(bf16)
    row = lax.broadcasted_iota(jnp.int32, mixed.shape, 0) + i * mixed.shape[0]
    grad = jnp.where(row < turn_ref[3 * WIDE + 2], cot_ref[...].astype(f32), 0.0)
    d_mixed = norm_back(grad, vec_ref[4:5, :], unit, factor)
    dmix_ref[...] = d_mixed
    low = d_mixed.astype(bf16)
    low_ref[...] = low
    sums_ref[0:1, :] += column_sum(grad * unit)
    sums_ref[1:2, :] += column_sum(grad)
    sums_ref[2:3, :] += column_sum(low.astype(f32))


def second_norm(turns, x1, keep, sent, got, cot, vectors):
    rows = x1.shape[0]
    tiles = norm_tiles(rows)
    block = pl.BlockSpec((rows // tiles, D), lambda i, *_: (i, 0))
    mine = pl.BlockSpec((rows // tiles, D), lambda i, turns: (turns[3 * WIDE + 1] * tiles + i, 0))
    return pl.pallas_call(
        second_norm_kernel,
        grid_spec=pltpu.PrefetchScalarGridSpec(
            num_scalar_prefetch=1,
            grid=(tiles,),
            in_specs=[block] * 4 + [mine, whole_block(vectors.shape)],
            out_specs=[block] * 3 + [whole_block((8, D))],
        ),
        out_shape=[
            jax.ShapeDtypeStruct((rows, D), bf16),
            jax.ShapeDtypeStruct((rows, D), f32),
            jax.ShapeDtypeStruct((rows, D), bf16),
            jax.ShapeDtypeStruct((8, D), f32),
        ],
        compiler_params=params_of(6),
        cost_estimate=cost(40 * rows * D, 20 * rows * D),
        name="second_norm",
    )(turns, x1, keep, sent, got, cot, vectors)


def first_back_kernel(
    hid_ref, dmix_ref, keep_ref, sent_ref, got_ref, vec_ref, dhid_ref, low_ref, sums_ref
):
    @pl.when(pl.program_id(0) == 0)
    def _():
        sums_ref[...] = jnp.zeros(sums_ref.shape, f32)

    grad = dmix_ref[...] + summed(keep_ref, sent_ref, got_ref)
    unit, factor = normalized(hid_ref[...])
    d_hidden = norm_back(grad, vec_ref[2:3, :], unit, factor)
    dhid_ref[...] = d_hidden
    low = d_hidden.astype(bf16)
    low_ref[...] = low
    sums_ref[0:1, :] += column_sum(grad * unit)
    sums_ref[1:2, :] += column_sum(grad)
    sums_ref[2:3, :] += column_sum(low.astype(f32))


def first_back(hidden, d_mixed, keep, sent, got, vectors):
    rows = hidden.shape[0]
    tiles = norm_tiles(rows)
    block = pl.BlockSpec((rows // tiles, D), lambda i: (i, 0))
    return pl.pallas_call(
        first_back_kernel,
        grid=(tiles,),
        in_specs=[block] * 5 + [whole_block(vectors.shape)],
        out_specs=[block] * 2 + [whole_block((8, D))],
        out_shape=[
            jax.ShapeDtypeStruct((rows, D), f32),
            jax.ShapeDtypeStruct((rows, D), bf16),
            jax.ShapeDtypeStruct((8, D), f32),
        ],
        compiler_params=params_of(6),
        cost_estimate=cost(40 * rows * D, 20 * rows * D),
        name="first_back",
    )(hidden, d_mixed, keep, sent, got, vectors)


def assemble_kernel(turn_ref, near_ref, far_ref, up_ref, down_ref, sem):
    near = near_ref.shape[0]
    copies = []
    for p in range(WIDE):
        source = near_ref.at[p] if p < near else far_ref.at[p - near]
        start = pl.multiple_of(turn_ref[2 * WIDE + p] * PB, PB)
        for n, target in enumerate((up_ref, down_ref)):
            copies.append(
                copy_in(source.at[pl.ds(PB * n, PB)], target.at[pl.ds(start, PB)], sem)
            )
    for copy in copies:
        copy.wait()


def assemble(turns, near, far):
    return pl.pallas_call(
        assemble_kernel,
        grid_spec=pltpu.PrefetchScalarGridSpec(
            num_scalar_prefetch=1,
            grid=(1,),
            in_specs=[in_place()] * 2,
            out_specs=[whole_block((D, D), single=True)] * 2,
            scratch_shapes=[pltpu.SemaphoreType.DMA],
        ),
        out_shape=[jax.ShapeDtypeStruct((D, D), bf16)] * 2,
        compiler_params=params_of(5),
        cost_estimate=cost(0, 8 * D * D),
        name="assemble",
    )(turns, near, far)


def feed_kernel(
    xa_ref, xb_ref, wu_ref, wd_ref, b_ref, x_ref, gate_ref, act_ref, keep_ref, send_ref, sem
):
    i = pl.program_id(0)
    rows = xa_ref.shape[0]

    first = pltpu.make_async_copy(xa_ref, x_ref.at[pl.ds(0, rows)], sem.at[0])
    second = pltpu.make_async_copy(xb_ref, x_ref.at[pl.ds(rows, rows)], sem.at[1])

    @pl.when(i == 0)
    def _():
        first.start()
        second.start()
        first.wait()

    @pl.when(i == 1)
    def _():
        second.wait()

    mine = pl.ds(pl.multiple_of(i * rows, rows), rows)
    gate = dot32(x_ref[mine, :], wu_ref[...]) + b_ref[...]
    gate_ref[...] = gate
    _, tanh = gelu_parts(gate)
    act = (0.5 * gate * (1.0 + tanh)).astype(bf16)
    act_ref[...] = act

    split_store(i, dot32(act, wd_ref[...]).astype(bf16), keep_ref, send_ref)


def feed_forward(piece_a, piece_b, w_up, w_down, up_bias):
    rows = piece_a.shape[0]
    step = pl.BlockSpec((rows, D), lambda i, *_: (i, 0))
    one = whole_block((rows, D))
    return pl.pallas_call(
        feed_kernel,
        grid_spec=pltpu.PrefetchScalarGridSpec(num_scalar_prefetch=0, grid=(2,),
        in_specs=[in_place()] * 2 + [whole_block((D, D))] * 2 + [whole_block(up_bias.shape)],
        out_specs=[whole_block((2 * rows, D)), step, step, one, one],
        scratch_shapes=[pltpu.SemaphoreType.DMA((2,))],
        ),
        out_shape=[
            jax.ShapeDtypeStruct((2 * rows, D), bf16),
            jax.ShapeDtypeStruct((2 * rows, D), f32),
            jax.ShapeDtypeStruct((2 * rows, D), bf16),
            jax.ShapeDtypeStruct((rows, D), bf16),
            jax.ShapeDtypeStruct((rows, D), bf16),
        ],
        compiler_params=params_of(13),
        cost_estimate=cost(8 * rows * D * D, 24 * rows * D),
        name="feed_forward",
    )(piece_a, piece_b, w_up, w_down, up_bias)


def feed_back_kernel(
    da_ref, db_ref, wu_ref, wd_ref, gate_ref, d_ref, dgate_ref, keep_ref, send_ref, sums_ref, sem
):
    i = pl.program_id(0)
    rows = da_ref.shape[0]

    first = pltpu.make_async_copy(da_ref, d_ref.at[pl.ds(0, rows)], sem.at[0])
    second = pltpu.make_async_copy(db_ref, d_ref.at[pl.ds(rows, rows)], sem.at[1])

    @pl.when(i == 0)
    def _():
        first.start()
        second.start()
        sums_ref[...] = jnp.zeros(sums_ref.shape, f32)
        first.wait()

    @pl.when(i == 1)
    def _():
        second.wait()

    mine = pl.ds(pl.multiple_of(i * rows, rows), rows)
    d_act = dot32(d_ref[mine, :], wd_ref[...], ((1,), (1,)))
    gate = gate_ref[...]
    _, tanh = gelu_parts(gate)
    slope = GELU * (1.0 + 3.0 * 0.044715 * gate * gate)
    d_gate = (d_act * (0.5 * (1.0 + tanh) + 0.5 * gate * (1.0 - tanh * tanh) * slope)).astype(bf16)
    dgate_ref[...] = d_gate
    sums_ref[0:1, :] += column_sum(d_gate.astype(f32))

    split_store(i, dot32(d_gate, wu_ref[...], ((1,), (1,))).astype(bf16), keep_ref, send_ref)


def feed_back(piece_a, piece_b, w_up, w_down, gate):
    rows = piece_a.shape[0]
    step = pl.BlockSpec((rows, D), lambda i, *_: (i, 0))
    one = whole_block((rows, D))
    return pl.pallas_call(
        feed_back_kernel,
        grid_spec=pltpu.PrefetchScalarGridSpec(num_scalar_prefetch=0, grid=(2,),
        in_specs=[in_place()] * 2 + [whole_block((D, D))] * 2 + [step],
        out_specs=[whole_block((2 * rows, D)), step, one, one, whole_block((8, D))],
        scratch_shapes=[pltpu.SemaphoreType.DMA((2,))],
        ),
        out_shape=[
            jax.ShapeDtypeStruct((2 * rows, D), bf16),
            jax.ShapeDtypeStruct((2 * rows, D), bf16),
            jax.ShapeDtypeStruct((rows, D), bf16),
            jax.ShapeDtypeStruct((rows, D), bf16),
            jax.ShapeDtypeStruct((8, D), f32),
        ],
        compiler_params=params_of(13),
        cost_estimate=cost(8 * rows * D * D, 24 * rows * D),
        name="feed_back",
    )(piece_a, piece_b, w_up, w_down, gate)


def group_kernel(turn_ref, left_n, left_f, right_n, right_f, keep_ref, send_ref, all_ref):
    i = pl.program_id(0)
    value = dot32(left_n[...], right_n[...], ((0,), (0,)))
    value = (value + dot32(left_f[...], right_f[...], ((0,), (0,)))).astype(bf16)
    per = value.shape[0] // PB
    for k in range(per):
        all_ref[turn_ref[WIDE + i * per + k]] = value[PB * k : PB * (k + 1)]

    @pl.when(i == pl.num_programs(0) - 1)
    def _():
        near = keep_ref.shape[0]
        keep_ref[...] = all_ref[:near]
        send_ref[...] = all_ref[near:]


def group_grads(turns, left, right, near):
    rows = left[0].shape[0]
    wide = D // 2
    tile = pl.BlockSpec((rows, wide), lambda i, *_: (0, i))
    full = whole_block((rows, D))
    shapes = [(near, PB, D), (WIDE - near, PB, D)]
    return pl.pallas_call(
        group_kernel,
        grid_spec=pltpu.PrefetchScalarGridSpec(
            num_scalar_prefetch=1,
            grid=(2,),
            in_specs=[tile] * 2 + [full] * 2,
            out_specs=[whole_block(shape) for shape in shapes],
            scratch_shapes=[pltpu.VMEM((WIDE, PB, D), bf16)],
        ),
        out_shape=[jax.ShapeDtypeStruct(shape, bf16) for shape in shapes],
        compiler_params=params_of(12),
        cost_estimate=cost(4 * rows * D * D, 12 * rows * D),
    )(turns, *left, *right)


def dx_kernel(dkv_ref, w_ref, *refs, with_q):
    keep_ref, send_ref = refs[-2:]
    i = pl.program_id(0)
    part = dot32(dkv_ref[...], w_ref[...], ((1,), (1,)))
    if with_q:

        @pl.when(i >= pl.num_programs(0) - 4)
        def _():
            more = part + dot32(refs[0][...], refs[1][...], ((1,), (1,)))
            split_store(i, more.astype(bf16), keep_ref, send_ref)

        @pl.when(i < pl.num_programs(0) - 4)
        def _():
            split_store(i, part.astype(bf16), keep_ref, send_ref)

    else:
        split_store(i, part.astype(bf16), keep_ref, send_ref)


def dx_part(d_kv, w_kv, steps, tokens, d_query, w_q):
    rows = tokens // 4
    count = len(steps)
    with_q = steps[-1] == 0
    half = pl.BlockSpec((rows, D), lambda i: (i // 2, 0))
    shape = jax.ShapeDtypeStruct((count * tokens // 2, D), bf16)
    cols = w_kv.shape[1]

    def chunk_row(i):
        step = steps[-1]
        for n in range(count - 1):
            step = jnp.where(i // 4 == n, steps[n], step)
        return 4 * step + i % 4, 0

    args = [d_kv, w_kv]
    specs = [pl.BlockSpec((rows, cols), chunk_row), whole_block(w_kv.shape)]
    if with_q:
        args += [d_query, w_q]
        specs += [
            pl.BlockSpec((rows, w_q.shape[1]), lambda i: (i % 4, 0)),
            whole_block(w_q.shape),
        ]
    return pl.pallas_call(
        functools.partial(dx_kernel, with_q=with_q),
        grid=(4 * count,),
        in_specs=specs,
        out_specs=[half, half],
        out_shape=[shape, shape],
        compiler_params=params_of(7),
        cost_estimate=cost(2 * count * tokens * cols * D, 2 * count * tokens * (cols + D)),
    )(*args)


def late_kernel(
    turn_ref, x_ref, dkv_ref, dq_ref, att_ref, db_ref, s1_ref, s2_ref, sa_ref, bn_ref, bf_ref, top_ref,
    keep_ref, send_ref, acc_kv, acc_q, acc_o, turn_kv, turn_q, inner_ref, vec_ref, all_ref,
    *, cols, steps_q, heads, owners
):
    i = pl.program_id(0)

    @pl.when(i == 0)
    def _():
        acc_kv[...] = jnp.zeros(acc_kv.shape, f32)
        acc_q[...] = jnp.zeros(acc_q.shape, f32)
        acc_o[...] = jnp.zeros(acc_o.shape, f32)

    x = x_ref[...]
    acc_kv[...] += dot32(dkv_ref[...], x, ((0,), (0,)))

    @pl.when(i < steps_q)
    def _():
        acc_q[...] += dot32(dq_ref[...], x, ((0,), (0,)))
        acc_o[...] += dot32(att_ref[...], db_ref[...], ((0,), (0,)))

    @pl.when(i == pl.num_programs(0) - 1)
    def _():
        turn_kv[...] = acc_kv[...].T.astype(bf16)
        turn_q[...] = acc_q[...].T.astype(bf16)
        pad = acc_o.shape[0] - cols
        for k in range(D // PB):
            for c in range(3):
                unit = 3 * k + c
                rows = slice(PB * k, PB * (k + 1))
                piece = turn_q[rows, :cols] if c == 0 else turn_kv[rows, cols * (c - 1) : cols * c]
                all_ref[
                    turn_ref[WIDE + unit // 4], :PB, cols * (unit % 4) : cols * (unit % 4 + 1)
                ] = piece
        for k in range(cols // PB):
            all_ref[turn_ref[WIDE + 3 * cols // PB + k], :PB, :] = acc_o[
                pad + PB * k : pad + PB * (k + 1), :
            ].astype(bf16)
        inner_ref[0:1, :cols] = sa_ref[0:1, :cols]
        inner_ref[0:1, cols : 2 * cols] = sa_ref[1:2, pad : pad + cols]
        inner_ref[0:1, 2 * cols :] = bn_ref[0:1, :] + bf_ref[0:1, :]
        outer_cols = D // owners
        inner_cols = inner_ref.shape[1] // owners
        lane = lax.broadcasted_iota(jnp.int32, (1, D), 1)
        slots = jnp.zeros((1, D), f32)
        base = turn_ref[3 * WIDE] * 3 * heads
        for h in range(heads):
            left = top_ref[h : h + 1, :1]
            for part in range(3):
                piece = left.astype(bf16).astype(f32)
                slots = jnp.where(lane == base + part * heads + h, piece, slots)
                left = left - piece
        vec_ref[...] = jnp.zeros(vec_ref.shape, f32)
        vec_ref[7:8, :] = slots
        outer_rows = [(s1_ref, 2), (s2_ref, 2), (s1_ref, 0), (s1_ref, 1), (s2_ref, 0), (s2_ref, 1)]
        for k in range(owners):
            for n, (ref, row) in enumerate(outer_rows):
                vec_ref[n : n + 1, :outer_cols] = ref[
                    row : row + 1, outer_cols * k : outer_cols * (k + 1)
                ]
            vec_ref[6:7, :inner_cols] = inner_ref[0:1, inner_cols * k : inner_cols * (k + 1)]
            all_ref[turn_ref[WIDE + k], PB:, :] = vec_ref[...].astype(bf16)
        near = keep_ref.shape[0]
        keep_ref[...] = all_ref[:near]
        send_ref[...] = all_ref[near:]


def late_grads(turns, in_all, d_kv, d_query, att, d_branch, s1, s2, sa, bn, bf, tops, cols, heads, near):
    tokens, wide = d_query.shape
    tile = min(512, tokens)
    steps_q = tokens // tile
    owners = WIDE
    under = 16

    def rows_of(width, last):
        return pl.BlockSpec((tile, width), lambda i, *_: (jnp.minimum(i, last), 0))

    steps = in_all.shape[0] // tile
    small = [s1, s2, sa, bn, bf, tops]
    return pl.pallas_call(
        functools.partial(late_kernel, cols=cols, steps_q=steps_q, heads=heads, owners=owners),
        grid_spec=pltpu.PrefetchScalarGridSpec(
            num_scalar_prefetch=1,
            grid=(steps,),
            in_specs=[
                rows_of(D, steps - 1),
                rows_of(2 * cols, steps - 1),
                rows_of(wide, steps_q - 1),
                rows_of(wide, steps_q - 1),
                rows_of(D, steps_q - 1),
            ]
            + [whole_block(v.shape) for v in small],
            out_specs=[
                whole_block((near, PB + under, D)),
                whole_block((owners - near, PB + under, D)),
            ],
            scratch_shapes=[
                pltpu.VMEM((2 * cols, D), f32),
                pltpu.VMEM((wide, D), f32),
                pltpu.VMEM((wide, D), f32),
                pltpu.VMEM((D, 2 * cols), bf16),
                pltpu.VMEM((D, wide), bf16),
                pltpu.VMEM((1, 2 * cols + D), f32),
                pltpu.VMEM((under, D), f32),
                pltpu.VMEM((owners, PB + under, D), bf16),
            ],
        ),
        out_shape=[
            jax.ShapeDtypeStruct((near, PB + under, D), bf16),
            jax.ShapeDtypeStruct((owners - near, PB + under, D), bf16),
        ],
        compiler_params=params_of(20),
        cost_estimate=cost(2 * in_all.shape[0] * D * 2 * cols, 2 * in_all.shape[0] * (D + 2 * cols)),
        name="late_grads",
    )(turns, in_all, d_kv, d_query, att, d_branch, *small)


def head_masks(wide, heads, first):
    lane = lax.broadcasted_iota(jnp.int32, (BLOCK, wide), 1) // HEAD
    return [lane == h + first for h in range(heads)]


def spread(block, masks):
    zero = jnp.zeros_like(block)
    return jnp.concatenate([jnp.where(mask, block, zero) for mask in masks], axis=0)


def fold(stacked, masks):
    total = None
    for h, mask in enumerate(masks):
        part = jnp.where(mask, stacked[BLOCK * h : BLOCK * (h + 1)], 0.0)
        total = part if total is None else total + part
    return total


def listed_rows(addr_ref, kv_ref, i):
    return jnp.concatenate(
        [
            kv_ref[pl.ds(pl.multiple_of(addr_ref[i * LIST + e] * BLOCK, BLOCK), BLOCK), :]
            for e in range(LIST)
        ],
        axis=0,
    )


def fwd_kernel(
    addr_ref, valid_ref, query_ref, q_ref, kv_src, att_ref, p_ref, top_ref, kv_ref, sem, *, heads, group
):
    i = pl.program_id(0)
    wide = q_ref.shape[1]
    start = kv_ref.shape[1] - wide

    @pl.when(i == 0)
    def _():
        load = copy_in(kv_src, kv_ref, sem)
        top_ref[...] = jnp.full(top_ref.shape, neg_large, f32)
        load.wait()

    scale = jnp.asarray(HEAD ** (-0.5), bf16)
    q_masks = head_masks(wide, heads, 0)
    v_masks = head_masks(wide, heads, (heads * HEAD - start) // HEAD)
    lane = lax.broadcasted_iota(jnp.int32, (1, LIST * BLOCK), 1)
    for u in range(group):
        block = i * group + u
        mine = slice(u * BLOCK, (u + 1) * BLOCK)
        q_all = spread(q_ref[mine] * scale, q_masks)
        listed = listed_rows(addr_ref, kv_ref, block)
        scores = dot32(q_all, listed[:, :wide], ((1,), (1,)))
        limit = jnp.zeros((1, LIST * BLOCK), jnp.int32)
        for e in range(LIST):
            limit = jnp.where(lane // BLOCK == e, valid_ref[block * LIST + e], limit)
        scores = jnp.where(lane % BLOCK < limit, scores, neg_large)
        row_top = jnp.max(scores, axis=1, keepdims=True)
        shifted = jnp.exp(scores - row_top)
        probs = shifted * (1.0 / jnp.sum(shifted, axis=1, keepdims=True))
        probs_low = probs.astype(bf16)
        p_ref[u] = probs_low
        out = dot32(probs_low, listed[:, start:])
        att_ref[mine] = fold(out, v_masks).astype(bf16)
        row = lax.broadcasted_iota(jnp.int32, row_top.shape, 0) % BLOCK
        seen = jnp.where(row < query_ref[block], row_top, neg_large)
        for h in range(heads):
            best = jnp.max(seen[BLOCK * h : BLOCK * (h + 1)], axis=0, keepdims=True)
            top_ref[h : h + 1, :] = jnp.maximum(top_ref[h : h + 1, :], best)


def attention_forward(queries, kv_all, addr, valid, query_valid, heads, group=2):
    tokens, wide = queries.shape
    blocks = tokens // BLOCK
    rows = heads * BLOCK
    cols = LIST * BLOCK
    return pl.pallas_call(
        functools.partial(fwd_kernel, heads=heads, group=group),
        grid_spec=pltpu.PrefetchScalarGridSpec(
            num_scalar_prefetch=3,
            grid=(blocks // group,),
            in_specs=[pl.BlockSpec((group * BLOCK, wide), lambda i, *_: (i, 0)), in_place()],
            out_specs=[
                pl.BlockSpec((group * BLOCK, wide), lambda i, *_: (i, 0)),
                pl.BlockSpec((group, rows, cols), lambda i, *_: (i, 0, 0)),
                whole_block((8, 128)),
            ],
            scratch_shapes=[pltpu.VMEM(kv_all.shape, bf16), pltpu.SemaphoreType.DMA],
        ),
        out_shape=(
            jax.ShapeDtypeStruct((tokens, wide), bf16),
            jax.ShapeDtypeStruct((blocks, rows, cols), bf16),
            jax.ShapeDtypeStruct((8, 128), f32),
        ),
        compiler_params=params_of(11),
        cost_estimate=cost(
            4 * blocks * rows * cols * wide,
            2 * (kv_all.size + 2 * queries.size + blocks * rows * cols),
            blocks * rows * cols,
        ),
        name="attention_forward",
    )(addr, valid, query_valid, queries, kv_all)


def bwd_kernel(addr_ref, q_ref, p_ref, w_ref, kv_src, *refs, heads, group):
    pieces = refs[:4]
    dq_ref, dkv_ref, sums_ref, db_ref, kv_ref, acc_ref, sem, piece_sem = refs[4:]
    i = pl.program_id(0)
    wide = q_ref.shape[1]
    start = kv_ref.shape[1] - wide

    @pl.when(i == 0)
    def _():
        rows = pieces[0].shape[0]
        loads = [
            copy_in(ref, db_ref.at[pl.ds(r * rows, rows)], piece_sem.at[r])
            for r, ref in enumerate(pieces)
        ]
        loads.append(copy_in(kv_src, kv_ref, sem))
        acc_ref[...] = jnp.zeros(acc_ref.shape, f32)
        sums_ref[...] = jnp.zeros(sums_ref.shape, f32)
        for load in loads:
            load.wait()

    scale = jnp.asarray(HEAD ** (-0.5), bf16)
    q_masks = head_masks(wide, heads, 0)
    v_masks = head_masks(wide, heads, (heads * HEAD - start) // HEAD)
    span = group * BLOCK
    d_branch = db_ref[pl.ds(pl.multiple_of(i * span, span), span), :]
    d_out = dot32(d_branch, w_ref[...], ((1,), (1,))).astype(bf16)
    for u in range(group):
        block = i * group + u
        mine = slice(u * BLOCK, (u + 1) * BLOCK)
        q_all = spread(q_ref[mine] * scale, q_masks)
        do_all = spread(d_out[mine], v_masks)
        listed = listed_rows(addr_ref, kv_ref, block)
        probs_low = p_ref[u]
        probs = probs_low.astype(f32)
        d_probs = dot32(do_all, listed[:, start:], ((1,), (1,)))
        delta = jnp.sum(probs * d_probs, axis=1, keepdims=True)
        d_scores = (probs * (d_probs - delta)).astype(bf16)
        d_query = (fold(dot32(d_scores, listed[:, :wide]), q_masks) * HEAD ** (-0.5)).astype(bf16)
        dq_ref[mine] = d_query
        sums_ref[0:1, :] += column_sum(d_query.astype(f32))
        d_key = dot32(d_scores, q_all, ((0,), (0,)))
        d_value = dot32(probs_low, do_all, ((0,), (0,)))
        sums_ref[1:2, :] += column_sum(d_value)
        for e in range(LIST):
            rows = pl.ds(pl.multiple_of(addr_ref[block * LIST + e] * BLOCK, BLOCK), BLOCK)
            part = slice(BLOCK * e, BLOCK * (e + 1))
            acc_ref[rows, :start] += d_key[part, :start]
            acc_ref[rows, start:wide] += d_key[part, start:] + d_value[part, : wide - start]
            acc_ref[rows, wide:] += d_value[part, wide - start :]

    @pl.when(i == pl.num_programs(0) - 1)
    def _():
        dkv_ref[...] = acc_ref[...].astype(bf16)


def attention_backward(queries, pieces, w_out, probs, kv_all, addr, heads, group=2):
    tokens, wide = queries.shape
    blocks = tokens // BLOCK
    rows = heads * BLOCK
    cols = LIST * BLOCK
    return pl.pallas_call(
        functools.partial(bwd_kernel, heads=heads, group=group),
        grid_spec=pltpu.PrefetchScalarGridSpec(
            num_scalar_prefetch=1,
            grid=(blocks // group,),
            in_specs=[
                pl.BlockSpec((group * BLOCK, wide), lambda i, *_: (i, 0)),
                pl.BlockSpec((group, rows, cols), lambda i, *_: (i, 0, 0)),
                whole_block(w_out.shape),
            ]
            + [in_place()] * 5,
            out_specs=[
                pl.BlockSpec((group * BLOCK, wide), lambda i, *_: (i, 0)),
                whole_block(kv_all.shape, single=True),
                whole_block((8, wide)),
                whole_block((tokens, D), single=True),
            ],
            scratch_shapes=[
                pltpu.VMEM(kv_all.shape, bf16),
                pltpu.VMEM(kv_all.shape, f32),
                pltpu.SemaphoreType.DMA,
                pltpu.SemaphoreType.DMA((4,)),
            ],
        ),
        out_shape=(
            jax.ShapeDtypeStruct((tokens, wide), bf16),
            jax.ShapeDtypeStruct(kv_all.shape, bf16),
            jax.ShapeDtypeStruct((8, wide), f32),
            jax.ShapeDtypeStruct((tokens, D), bf16),
        ),
        compiler_params=params_of(24),
        cost_estimate=cost(
            8 * blocks * rows * cols * wide,
            2 * (2 * kv_all.size + 3 * queries.size + blocks * rows * cols),
        ),
        name="attention_backward",
    )(addr, queries, probs, w_out, kv_all, *pieces)


def two_parts(values):
    high = values.astype(bf16)
    return high, (values - high.astype(f32)).astype(bf16)


def shampoo_kernel(turn_ref, *refs, width, groups, heads):
    g_refs = refs[: 3 if groups else 1]
    tail_ref, mb_ref, ls_ref, rs_ref, lr_ref, rr_ref = refs[len(g_refs) : len(g_refs) + 6]
    bg_ref, ln_ref, rn_ref, nb_ref, max_ref, g_ref = refs[len(g_refs) + 6 :]
    i = pl.program_id(0)
    if groups:
        for n in range(3):

            @pl.when(i == n)
            def _():
                g_ref[...] = g_refs[n][...]
    else:
        g_ref[...] = g_refs[0][...]
    slots = tail_ref[0:8, :128]
    lanes = slots.shape[1]
    slots = slots + pltpu.roll(slots, lanes - heads, 1) + pltpu.roll(slots, lanes - 2 * heads, 1)
    lane = lax.broadcasted_iota(jnp.int32, slots.shape, 1)
    row = lax.broadcasted_iota(jnp.int32, slots.shape, 0)
    largest = jnp.zeros(slots.shape, f32)
    scales = []
    for h in range(heads):
        chosen = (row == 7) & (lane % (3 * heads) == h) & (lane < 3 * heads * WIDE)
        best = jnp.max(jnp.where(chosen, slots, neg_large), axis=1, keepdims=True)
        best = jnp.max(best, axis=0, keepdims=True)
        largest = jnp.where(lane == h, best, largest)
        scales.append(jnp.sqrt(tau_clip / jnp.maximum(best, tau_clip)))
    max_ref[...] = largest
    per_row = 3 * heads * HEAD // PB
    column = lax.broadcasted_iota(jnp.int32, (1, PB), 1)
    for j in range(width):
        cut = slice(PB * j, PB * (j + 1))
        grad = g_ref[:, cut]
        bg_ref[j] = grad.astype(f32)
        ln_ref[j] = 0.5 * ls_ref[j] + 0.5 * dot32(grad, grad, ((1,), (1,)))
        rn_ref[j] = 0.5 * rs_ref[j] + 0.5 * dot32(grad, grad, ((0,), (0,)))
        left_hi, left_lo = two_parts(lr_ref[j])
        applied_hi, applied_lo = two_parts(dot32(left_hi, grad) + dot32(left_lo, grad))
        right_hi, right_lo = two_parts(rr_ref[j])
        step_val = (
            dot32(applied_hi, right_hi) + dot32(applied_hi, right_lo) + dot32(applied_lo, right_hi)
        )
        index = (turn_ref[3 * WIDE] * pl.num_programs(0) + i) * width + j
        head_of = (lax.rem(index, per_row) * PB + column) // HEAD
        factor = jnp.ones((1, PB), f32)
        for h in range(heads):
            hit = (head_of == h) | (head_of == heads + h)
            factor = jnp.where(hit & (index < D // PB * per_row), scales[h], factor)
        nb_ref[j] = (mb_ref[j] - rate_matrix * step_val) * factor


def shampoo(turns, grads, groups, tail, master, left_s, right_s, left_r, right_r, heads):
    count = master.shape[0]
    width = WIDE if groups else 1
    block = pl.BlockSpec((width, PB, PB), lambda i, *_: (i, 0, 0))
    shape = jax.ShapeDtypeStruct((count, PB, PB), f32)
    if groups:
        specs = [whole_block(part.shape) for part in grads]
    else:
        specs = [pl.BlockSpec((PB, PB), lambda i, *_: (i, 0))]
    return pl.pallas_call(
        functools.partial(shampoo_kernel, width=width, groups=groups, heads=heads),
        grid_spec=pltpu.PrefetchScalarGridSpec(
            num_scalar_prefetch=1,
            grid=(count // width,),
            in_specs=specs + [whole_block(tail.shape)] + [block] * 5,
            out_specs=[block] * 4 + [whole_block((8, 128))],
            scratch_shapes=[pltpu.VMEM((PB, PB * width), bf16)],
        ),
        out_shape=[shape] * 4 + [jax.ShapeDtypeStruct((8, 128), f32)],
        compiler_params=params_of(16),
        cost_estimate=cost(16 * count * PB**3, 40 * count * PB * PB),
        name="shampoo",
    )(turns, *grads, tail, master, left_s, right_s, left_r, right_r)


def gather_quarters(own):
    side = swap(own, 1)
    across = swap(own, 2)
    return own, side, across, swap(across, 1)


def cross_sum(keep_far, send_far):
    mine = keep_far.astype(f32) + swap(send_far, 1).astype(f32)
    return swap(mine.astype(bf16), 2)


def slot_pairs(slot):
    return [(d, (3 * d + slot) % WIDE) for d in range(WIDE)]


def spread_group(held):
    count = lax.axis_size("ctx")
    near = jnp.stack([held] + [shift_ctx(held, step) for step in range(1, count)], axis=0)
    far = [shift_shard(near, u) for u in range(1, lax.axis_size("shard"))]
    return near, far[0] if len(far) == 1 else jnp.concatenate(far, axis=0)


def reduce_group(near, far):
    count = lax.axis_size("ctx")
    back = [
        shift_shard(far[count * (u - 1) : count * u], u)
        for u in range(1, lax.axis_size("shard"))
    ]
    halves = []
    for step in range(count):
        value = near[step].astype(f32)
        for part in back:
            value = value + part[step].astype(f32)
        halves.append(value)
    return halves[0], [shift_ctx(halves[step].astype(bf16), step) for step in near_first(count)]


def total_of(first, others, *wait):
    if wait:
        others = lax.optimization_barrier(tuple(others) + wait)[: len(others)]
    for other in others:
        first = first + other.astype(f32)
    return first


def per_device(
    inputs,
    lengths,
    global_blocks,
    random_blocks,
    master_blocks,
    outer_vectors,
    inner_biases,
    left_stats,
    right_stats,
    left_roots,
    right_roots,
    cotangent,
):
    tensor_count = lax.axis_size("tp")
    owner_count = lax.axis_size(OWN)
    ctx_count = lax.axis_size("ctx")
    shard_count = lax.axis_size("shard")
    heads_here = HEADS // tensor_count
    cols = heads_here * HEAD
    wide = 256
    pad = wide - cols
    tokens = inputs.shape[1]
    quarter = tokens // 4
    rows_blocks = tokens // BLOCK
    blocks_here = master_blocks.shape[0]
    packed = owner_count == WIDE and blocks_here == 3 * WIDE
    me = lax.axis_index("tp")
    z = lax.axis_index("ctx")
    y = lax.axis_index("shard")
    owner = lax.axis_index(OWN)
    ids = jnp.stack([me, y, z, owner]).astype(jnp.int32)
    addr, valid, query_valid, turns = index_tables(
        ids,
        lengths,
        global_blocks,
        random_blocks.reshape(rows_blocks, 3),
        rows_blocks,
        ctx_count,
        shard_count,
    )
    inner_row = inner_biases[0:1]
    q_bias = jnp.pad(inner_row[:, :cols], ((0, 0), (0, pad)))
    kv_bias = jnp.pad(inner_row[:, cols : 2 * cols], ((0, 0), (cols, 0)))
    up_bias = inner_row[:, 2 * cols :]
    flat_in = inputs.reshape(tokens, D)
    own_in = pick_quarter(ids, flat_in)

    if packed:
        own_packed = after(pack_rows(master_blocks), turns, up_bias, q_bias, kv_bias)
        held = [
            owner_move(own_packed[PB * slot : PB * (slot + 1)], slot_pairs(slot))
            for slot in range(3)
        ]
        held_first, held_rest = sort_held(turns, held)
        first_near, first_far = spread_group(held_first)
        rest_near, rest_far = spread_group(held_rest)
    else:
        weights = pack_rows(lax.all_gather(master_blocks.astype(bf16), OWN, axis=0, tiled=True))
        weights = weights.reshape(3, WIDE, PB, D)
        first_near, first_far = weights[0, : WIDE // 2], weights[0, WIDE // 2 :]
        rest = jnp.concatenate([weights[1], weights[2]], axis=1)
        rest_near, rest_far = rest[: WIDE // 2], rest[WIDE // 2 :]
        order = jnp.arange(WIDE, dtype=jnp.int32)
        turns = jnp.concatenate([order, order, order, turns[3 * WIDE :]])
    w_q, w_kv, w_out = unpack_first(turns, first_near, first_far, cols, wide)

    in_all, kv_all, queries = project_chunk(
        ids, [flat_in], 0, ctx_count, w_kv, kv_bias, w_q, q_bias, None
    )
    moved = []
    for n, step in enumerate(near_first(ctx_count)):
        source = own_in if n < 2 else after(own_in, moved[n - 2])
        moved.append(shift_ctx(source, step))
        pieces = gather_quarters(moved[n])
        in_all, kv_all = project_chunk(
            ids, pieces, step, ctx_count, w_kv, kv_bias, None, None, (in_all, kv_all)
        )

    att, probs, tops = attention_forward(queries, kv_all, addr, valid, query_valid, heads_here)
    keep, send = out_project(att, w_out)
    sent = swap(send, 1)
    got = swap((keep[quarter:].astype(f32) + sent[quarter:].astype(f32)).astype(bf16), 2)
    w_up, w_down = assemble(turns, rest_near, rest_far)
    hidden, x_first, x_own = first_norm(ids, flat_in, keep, sent, got, outer_vectors)
    x_own, x_side, x_across, x_diag = gather_quarters(x_own)
    x_n, gate_n, act_n, keep_n, send_n = feed_forward(x_own, x_side, w_up, w_down, up_bias)
    x_f, gate_f, act_f, keep_f, send_f = feed_forward(
        x_across, x_diag, w_up, w_down, up_bias
    )
    out_own, d_mixed, d_own, sums2 = second_norm(
        turns,
        x_first,
        keep_n,
        swap(send_n, 1),
        cross_sum(keep_f, send_f),
        cotangent.reshape(tokens, D),
        outer_vectors,
    )

    near = ctx_count if packed else WIDE // 2
    d_own, d_side, d_across, d_diag = gather_quarters(d_own)
    d_n, dg_n, keep_n, send_n, up_n = feed_back(d_own, d_side, w_up, w_down, gate_n)
    d_f, dg_f, keep_f, send_f, up_f = feed_back(d_across, d_diag, w_up, w_down, gate_f)
    d_hidden, b_own, sums1 = first_back(
        hidden, d_mixed, keep_n, swap(send_n, 1), cross_sum(keep_f, send_f), outer_vectors
    )
    b_pieces = gather_quarters(b_own)
    g_down = group_grads(turns, (act_n, act_f), (d_n, d_f), near)
    g_up = group_grads(turns, (x_n, x_f), (dg_n, dg_f), near)
    if packed:
        down_own = reduce_group(*g_down)
        up_own = reduce_group(*g_up)
    out_quarters = gather_quarters(after(out_own, b_pieces[3]))
    d_query, d_kv, sums_a, d_branch = attention_backward(
        queries, b_pieces, w_out, probs, kv_all, addr, heads_here
    )

    total = d_hidden
    order = near_first(ctx_count)[::-1] + [0]
    half = len(order) // 2
    d_kv_late = d_kv
    for steps in (order[:half], order[half:]):
        keep, send = dx_part(d_kv, w_kv, steps, tokens, d_query, w_q)
        sent = swap(send, 1)
        keep = keep.reshape(len(steps), 2, quarter, D)
        sent = sent.reshape(len(steps), 2, quarter, D)
        across = (keep[:, 1].astype(f32) + sent[:, 1].astype(f32)).astype(bf16)
        across = swap(across, 2)
        for c, step in enumerate(steps):
            mine = keep[c, 0].astype(f32) + sent[c, 0].astype(f32) + across[c].astype(f32)
            if step:
                mine = shift_ctx(mine.astype(bf16), ctx_count - step).astype(f32)
            total = total + mine
    grad_quarters = gather_quarters(total.astype(bf16))

    near_rows, far_rows = late_grads(
        turns,
        in_all,
        d_kv_late,
        d_query,
        att,
        d_branch,
        sums1,
        sums2,
        sums_a,
        up_n,
        up_f,
        tops,
        cols,
        heads_here,
        near,
    )
    outer_cols = D // owner_count
    inner_cols = inner_biases.shape[1] // owner_count
    if packed:
        down_own = total_of(*down_own, near_rows).astype(bf16)
        up_own = total_of(*up_own, near_rows).astype(bf16)
        late_own = total_of(*reduce_group(near_rows, far_rows))
        dealt = deal_rows(turns, late_own, up_own, down_own)
        tail = late_own[PB:]
        outer_own = tail[:6, :outer_cols]
        inner_own = tail[6:7, :inner_cols]
        grads = [
            owner_move(dealt[slot], [(holder, d) for d, holder in slot_pairs(slot)])
            for slot in range(3)
        ]
        groups = 3
    else:
        rows_of = jnp.concatenate([near_rows, far_rows], axis=0)[:, :PB]
        whole = jnp.concatenate([rows_of, *g_up, *g_down], axis=0).reshape(-1, D)
        blocks = whole.reshape(-1, PB, WIDE, PB).transpose(0, 2, 1, 3).reshape(-1, PB, PB)
        own_grads = lax.psum_scatter(blocks, OWN, scatter_dimension=0, tiled=True)
        grads, groups = [own_grads.reshape(blocks_here * PB, PB)], 0
        outer_part = jnp.stack([sums1[2], sums2[2], sums1[0], sums1[1], sums2[0], sums2[1]], axis=0)
        inner_part = jnp.concatenate([sums_a[0, :cols], sums_a[1, pad:], up_n[0] + up_f[0]])
        outer_own = lax.psum_scatter(outer_part, OWN, scatter_dimension=1, tiled=True)
        inner_own = lax.psum_scatter(inner_part[None, :], OWN, scatter_dimension=1, tiled=True)
        largest = lax.pmax(tops[:heads_here, 0], OWN)
        slots = jnp.tile(jnp.concatenate([largest, jnp.zeros((2 * heads_here,), f32)]), WIDE)
        tail = jnp.zeros((16, D), f32).at[7, : slots.shape[0]].set(slots)
    outer_own = outer_own + swap(outer_own, 1)
    outer_own = outer_own + swap(outer_own, 2)

    block_sum, left_new, right_new, new_blocks, largest = shampoo(
        turns,
        grads,
        groups,
        tail,
        master_blocks,
        left_stats,
        right_stats,
        left_roots,
        right_roots,
        heads_here,
    )
    maxima = largest[0, :heads_here]
    own_outer = lax.dynamic_slice_in_dim(outer_vectors, owner * outer_cols, outer_cols, 1)
    new_outer = own_outer - rate_vector * outer_own
    own_inner = lax.dynamic_slice_in_dim(inner_biases, owner * inner_cols, inner_cols, 1)
    head_of = (owner * inner_cols + jnp.arange(inner_cols, dtype=jnp.int32)) // HEAD
    factor = jnp.ones((inner_cols,), f32)
    for h in range(heads_here):
        scale = jnp.sqrt(tau_clip / jnp.maximum(largest[0, h], tau_clip))
        factor = jnp.where(head_of == h, scale, factor)
    new_inner = (own_inner - rate_vector * inner_own) * factor[None, :]

    return (
        place_quarters(ids, out_quarters).reshape(inputs.shape),
        place_quarters(ids, grad_quarters).reshape(inputs.shape),
        block_sum,
        outer_own,
        inner_own,
        maxima,
        left_new,
        right_new,
        new_blocks,
        new_outer,
        new_inner,
    )


def solution(mesh):
    return jax.shard_map(
        per_device,
        mesh=mesh,
        in_specs=(
            P("shard", "ctx", None),
            P("shard"),
            P("shard", None),
            P("shard", "ctx", None),
            P(("shard", "ctx", "tp"), None, None),
            P(),
            P("tp", None),
            P(("shard", "ctx", "tp"), None, None),
            P(("shard", "ctx", "tp"), None, None),
            P(("shard", "ctx", "tp"), None, None),
            P(("shard", "ctx", "tp"), None, None),
            P("shard", "ctx", None),
        ),
        out_specs=(
            P("shard", "ctx", None),
            P("shard", "ctx", None),
            P(("shard", "ctx", "tp"), None, None),
            P(None, ("shard", "ctx")),
            P("tp", ("shard", "ctx")),
            P("tp"),
            P(("shard", "ctx", "tp"), None, None),
            P(("shard", "ctx", "tp"), None, None),
            P(("shard", "ctx", "tp"), None, None),
            P(None, ("shard", "ctx")),
            P("tp", ("shard", "ctx")),
        ),
        check_vma=False,
    )
```

time: 382 us -> 406 us (1.063)
  Pallas kernels: 33.8 us -> 93.4 us
  matrix products: 43 us -> 0 us
  waiting for transfers between devices: 138 us -> 176 us
  starting transfers between devices: 71.6 us -> 95.3 us
  other arithmetic: 33.9 us -> 12.8 us
  local copies, waits for them, and re-layouts: 39.1 us -> 19.8 us
  between operations: 16.7 us -> 4.56 us
    pallas_call x4 -> x27, Pallas kernels: 28.1 us -> 92.2 us  [the longest x1 14.4 us: attention_backward(): pl.pallas_call(functools.partial(bwd_kernel, heads=heads, group=group), g...]
    ppermute x12 -> x21, waiting for transfers between devices: 41.9 us -> 94.5 us  [shift_ctx(): lax.ppermute(rows, 'ctx', [(i, (i + step) % count) for i in range(count)])]
    dot_general x21 -> x0, matrix products: 43 us -> none  [dot32(): lax.dot_general(left, right, (dims, ((), ())), preferred_element_type=f32)]
    ppermute x12 -> x21, starting transfers between devices: 14 us -> 32.7 us  [shift_ctx(): lax.ppermute(rows, 'ctx', [(i, (i + step) % count) for i in range(count)])]
    ppermute x40 -> x38, waiting for transfers between devices: 62.4 us -> 50.9 us  [swap(): return lax.ppermute(rows, 'tp', [(i, i ^ mask) for i in range(count)])]
    concatenate x12 -> x0, other arithmetic: 8.5 us -> none  [the longest x1 4.5 us: per_device(): early = jnp.concatenate([jnp.zeros((edge, D), bf16), g_up, g_down], axis=0)]
    concatenate x8 -> x0, local copies, waits for them, and re-layouts: 4.74 us -> none  [the longest x1 2.1 us: per_device(): inner_part = jnp.concatenate([sums[0, :cols], sums[1, pad:], d_upbias])]
    unnamed x209 -> x96, local copies, waits for them, and re-layouts: 23 us -> 18.4 us
  transfers between devices with their start and end apart: 62 -> 70, of which waited for: 28 -> 30; matrix products, arithmetic and copies ran while one was open for 24% -> 3% of each run, Pallas kernels for 7% -> 14%
where the time goes in v1:
time: 406 us; the launch traced here: 402 us
  waiting for transfers between devices  176 us (43%)
  starting transfers between devices  95.3 us (23%)
  Pallas kernels  93.4 us (23%)
  local copies, waits for them, and re-layouts  19.8 us (5%)
  other arithmetic  12.8 us (3%)
  between operations  4.56 us (1%)
    ppermute x21, waiting for transfers between devices, shift_ctx(): lax.ppermute(rows, 'ctx', [(i, (i + step) % count) for i in range(count)])  94.5 us
    ppermute x38, waiting for transfers between devices, swap(): return lax.ppermute(rows, 'tp', [(i, i ^ mask) for i in range(count)])  50.9 us
    ppermute x38, starting transfers between devices, swap(): return lax.ppermute(rows, 'tp', [(i, i ^ mask) for i in range(count)])  45.4 us
    ppermute x21, starting transfers between devices, shift_ctx(): lax.ppermute(rows, 'ctx', [(i, (i + step) % count) for i in range(count)])  32.7 us
    ppermute x5, waiting for transfers between devices, shift_shard(): lax.ppermute(rows, 'shard', [(i, (i + step) % count) for i in range(count)])  21.1 us
    unnamed x96, local copies, waits for them, and re-layouts  18.4 us
    pallas_call x1, Pallas kernels, attention_backward(): pl.pallas_call(functools.partial(bwd_kernel, heads=heads, group=group), g...  14.4 us
    ppermute x6, starting transfers between devices, owner_move(): return lax.ppermute(rows, OWN, pairs)  12.7 us
  transfers between devices with their start and end apart: 70, of which 30 were waited for; matrix products, arithmetic and copies ran while one was open for 3% of the time, Pallas kernels for 14%

profile of v1, /device:TPU:9, one launch (start us, length us, event | category | flops | bytes accessed | tf_op | source)
XLA Modules:
  0.0 402.0 jit_solution(12100549234759109079)
XLA Ops:
  27.7 6.6 %collective-permute-done.4 = bf16[96,768]{1,0:T(8,128)(2,1)S(1)} collective-permute-done((bf16[96,768]{1,0:T(8,128)(2,1)S(1)}, bf16[96,768]{1,0:T(8,128)(2,1)S(1)}, u32[]{:S(2)}, u32[]{:S(2)}) %collective-permute-start.4) | collective-permute-done | bytes 147488 | tf_op jit(solution)/shard_map/ppermute | solution.py:89
  34.3 19.2 %collective-permute-done.3 = bf16[96,768]{1,0:T(8,128)(2,1)S(1)} collective-permute-done((bf16[96,768]{1,0:T(8,128)(2,1)S(1)}, bf16[96,768]{1,0:T(8,128)(2,1)S(1)}, u32[]{:S(2)}, u32[]{:S(2)}) %collective-permute-start.3) | collective-permute-done | bytes 147488 | tf_op jit(solution)/shard_map/ppermute | solution.py:89
  63.2 4.6 %collective-permute-start.18 = (bf16[256,768]{1,0:T(8,128)(2,1)S(1)}, bf16[256,768]{1,0:T(8,128)(2,1)S(1)}, u32[]{:S(2)}, u32[]{:S(2)}) collective-permute-start(bf16[256,768]{1,0:T(8,128)(2,1)S(1)} %collective-permute-done.17.refs_2_), channel_id=1, source_target_pairs={{0,1},{1,0},{2,3},{3,2},{4,5},{5,4},{6,7},{7,6},{8,9},{9,8},{10,11... | collective-permute-start | bytes 1179656 | tf_op jit(solution)/shard_map/ppermute | solution.py:84
  70.9 5.3 %collective-permute-start.13 = (bf16[256,768]{1,0:T(8,128)(2,1)S(1)}, bf16[256,768]{1,0:T(8,128)(2,1)S(1)}, u32[]{:S(2)}, u32[]{:S(2)}) collective-permute-start(bf16[256,768]{1,0:T(8,128)(2,1)S(1)} %collective-permute-done.12.refs_0_), channel_id=1, source_target_pairs={{0,1},{1,0},{2,3},{3,2},{4,5},{5,4},{6,7},{7,6},{8,9},{9,8},{10,11... | collective-permute-start | bytes 1179656 | tf_op jit(solution)/shard_map/ppermute | solution.py:84
  98.2 6.7 %attention_forward.1 = (bf16[1024,256]{1,0:T(8,128)(2,1)S(1)}, bf16[16,192,512]{2,1,0:T(8,128)(2,1)S(1)}, f32[8,128]{1,0:T(8,128)S(1)}) custom-call(s32[128]{0:T(128)S(1)} %get-tuple-element.98.addr_ref, s32[128]{0:T(128)S(1)} %get-tuple-element.99.valid_ref, s32[16]{0:T(128)S(1)} %get-tuple-element.100.query_ref, ...), custom_call_target="tpu_custom_call" | custom-call | flops 1610612736 | bytes 7340032 | tf_op jit(solution)/shard_map/attention_forward/pallas_call | solution.py:990
  115.5 7.3 %collective-permute-done.23 = bf16[192,768]{1,0:T(8,128)(2,1)S(1)} collective-permute-done((bf16[192,768]{1,0:T(8,128)(2,1)S(1)}, bf16[192,768]{1,0:T(8,128)(2,1)S(1)}, u32[]{:S(2)}, u32[]{:S(2)}) %collective-permute-start.23) | collective-permute-done | bytes 294944 | tf_op jit(solution)/shard_map/ppermute | solution.py:89
  122.7 6.1 %collective-permute-done.22 = bf16[192,768]{1,0:T(8,128)(2,1)S(1)} collective-permute-done((bf16[192,768]{1,0:T(8,128)(2,1)S(1)}, bf16[192,768]{1,0:T(8,128)(2,1)S(1)}, u32[]{:S(2)}, u32[]{:S(2)}) %collective-permute-start.22) | collective-permute-done | bytes 294944 | tf_op jit(solution)/shard_map/ppermute | solution.py:89
  133.3 8.7 %collective-permute-done.27.xa_ref = bf16[256,768]{1,0:T(8,128)(2,1)S(1)} collective-permute-done((bf16[256,768]{1,0:T(8,128)(2,1)S(1)}, bf16[256,768]{1,0:T(8,128)(2,1)S(1)}, u32[]{:S(2)}, u32[]{:S(2)}) %collective-permute-start.27) | collective-permute-done | bytes 393248 | tf_op jit(solution)/shard_map/ppermute | solution.py:84
  143.6 12.5 %collective-permute-done.25.far_ref = bf16[4,192,768]{2,1,0:T(8,128)(2,1)S(1)} collective-permute-done((bf16[4,192,768]{2,1,0:T(8,128)(2,1)S(1)}, bf16[4,192,768]{2,1,0:T(8,128)(2,1)S(1)}, u32[]{:S(2)}, u32[]{:S(2)}) %collective-permute-start.25) | collective-permute-done | bytes 1179680 | tf_op jit(solution)/shard_map/ppermute | solution.py:94
  168.0 9.4 %collective-permute-done.30.got_ref = bf16[256,768]{1,0:T(8,128)(2,1)S(1)} collective-permute-done((bf16[256,768]{1,0:T(8,128)(2,1)S(1)}, bf16[256,768]{1,0:T(8,128)(2,1)S(1)}, u32[]{:S(2)}, u32[]{:S(2)}) %collective-permute-start.30) | collective-permute-done | bytes 393248 | tf_op jit(solution)/shard_map/ppermute | solution.py:84
  181.3 8.5 %collective-permute-done.33.da_ref = bf16[256,768]{1,0:T(8,128)(2,1)S(1)} collective-permute-done((bf16[256,768]{1,0:T(8,128)(2,1)S(1)}, bf16[256,768]{1,0:T(8,128)(2,1)S(1)}, u32[]{:S(2)}, u32[]{:S(2)}) %collective-permute-start.33) | collective-permute-done | bytes 393248 | tf_op jit(solution)/shard_map/ppermute | solution.py:84
  203.1 8.9 %collective-permute-done.36.got_ref = bf16[256,768]{1,0:T(8,128)(2,1)S(1)} collective-permute-done((bf16[256,768]{1,0:T(8,128)(2,1)S(1)}, bf16[256,768]{1,0:T(8,128)(2,1)S(1)}, u32[]{:S(2)}, u32[]{:S(2)}) %collective-permute-start.36) | collective-permute-done | bytes 393248 | tf_op jit(solution)/shard_map/ppermute | solution.py:84
  216.9 6.7 %collective-permute-done.37.refs_2_ = bf16[256,768]{1,0:T(8,128)(2,1)S(1)} collective-permute-done((bf16[256,768]{1,0:T(8,128)(2,1)S(1)}, bf16[256,768]{1,0:T(8,128)(2,1)S(1)}, u32[]{:S(2)}, u32[]{:S(2)}) %collective-permute-start.37) | collective-permute-done | bytes 393248 | tf_op jit(solution)/shard_map/ppermute | solution.py:84
  227.1 14.4 %attention_backward.1 = (bf16[1024,256]{1,0:T(8,128)(2,1)S(1)}, bf16[4096,384]{1,0:T(8,128)(2,1)S(1)}, f32[8,256]{1,0:T(8,128)S(1)}, bf16[1024,768]{1,0:T(8,128)(2,1)S(1)}) custom-call(s32[128]{0:T(128)S(1)} %get-tuple-element.98.addr_ref, bf16[1024,256]{1,0:T(8,128)(2,1)S(1)} %get-tuple-element.105.q_ref, ...), custom_call_target="tpu_custom_call" | custom-call | flops 3221225472 | bytes 11010048 | tf_op jit(solution)/shard_map/attention_backward/pallas_call | solution.py:1078
  241.5 5.3 %shard_map.208 = (bf16[1024,768]{1,0:T(8,128)(2,1)S(1)}, bf16[1024,768]{1,0:T(8,128)(2,1)}) custom-call(bf16[4096,384]{1,0:T(8,128)(2,1)S(1)} %get-tuple-element.141.dkv_ref, bf16[768,384]{1,0:T(8,128)(2,1)S(1)} %get-tuple-element.103.refs_1_.refs_4_.w_ref), custom_call_target="tpu_custom_call" | custom-call | flops 1207959552 | bytes 4718592 | tf_op jit(solution)/shard_map/pallas_call | solution.py:788
  248.3 5.8 %shard_map.209 = (bf16[1024,768]{1,0:T(8,128)(2,1)S(1)}, bf16[1024,768]{1,0:T(8,128)(2,1)}) custom-call(bf16[4096,384]{1,0:T(8,128)(2,1)S(1)} %get-tuple-element.141.dkv_ref, bf16[768,384]{1,0:T(8,128)(2,1)S(1)} %get-tuple-element.103.refs_1_.refs_4_.w_ref, bf16[1024,256]{1,0:T(8,128)(2,1)S(1)} %get-tuple-element.144.refs_0_.dq_ref, ...), custom_call_target="tpu_custom_call" | custom-call | flops 1207959552 | bytes 4718592 | tf_op jit(solution)/shard_map/pallas_call | solution.py:788
  271.0 7.3 %late_grads.1 = (bf16[4,112,768]{2,1,0:T(8,128)(2,1)S(1)}, bf16[4,112,768]{2,1,0:T(8,128)(2,1)S(1)}) custom-call(s32[32]{0:T(128)S(1)} %get-tuple-element.97.turn_ref, bf16[4096,768]{1,0:T(8,128)(2,1)S(1)} %copy-done.1, bf16[4096,384]{1,0:T(8,128)(2,1)S(1)} %get-tuple-element.141.dkv_ref, bf16[1024,256]{1,0:T(8,128)(2,1)S(1)} %copy-done.7, ...), custom_call_target="tpu_custom_call" | custom-call | flops 2415919104 | bytes 9437184 | tf_op jit(solution)/shard_map/late_grads/pallas_call | solution.py:878
  281.2 6.8 %collective-permute-start.59 = (bf16[96,768]{1,0:T(8,128)(2,1)S(1)}, bf16[96,768]{1,0:T(8,128)(2,1)S(1)}, u32[]{:S(2)}, u32[]{:S(2)}) collective-permute-start(bf16[96,768]{1,0:T(8,128)(2,1)S(1)} %get-tuple-element.196), channel_id=1, source_target_pairs={{0,12},{4,0},{8,4},{12,8},{1,13},{5,1},{9,5},{13,9},{2,14},{6,2},{... | collective-permute-start | bytes 442376 | tf_op jit(solution)/shard_map/ppermute | solution.py:89
  293.1 8.6 %collective-permute-done.53 = bf16[4,112,768]{2,1,0:T(8,128)(2,1)S(1)} collective-permute-done((bf16[4,112,768]{2,1,0:T(8,128)(2,1)S(1)}, bf16[4,112,768]{2,1,0:T(8,128)(2,1)S(1)}, u32[]{:S(2)}, u32[]{:S(2)}) %collective-permute-start.53) | collective-permute-done | bytes 688160 | tf_op jit(solution)/shard_map/ppermute | solution.py:94
  303.0 4.9 %collective-permute-start.54 = (bf16[112,768]{1,0:T(8,128)(2,1)S(1)}, bf16[112,768]{1,0:T(8,128)(2,1)S(1)}, u32[]{:S(2)}, u32[]{:S(2)}) collective-permute-start(bf16[112,768]{1,0:T(8,128)(2,1)S(1)} %get-tuple-element.189), channel_id=1, source_target_pairs={{0,4},{4,8},{8,12},{12,0},{1,5},{5,9},{9,13},{13,1},{2,6},{6,10},{... | collective-permute-start | bytes 516104 | tf_op jit(solution)/shard_map/ppermute | solution.py:89
  314.3 11.0 %collective-permute-done.56 = bf16[112,768]{1,0:T(8,128)(2,1)S(1)} collective-permute-done((bf16[112,768]{1,0:T(8,128)(2,1)S(1)}, bf16[112,768]{1,0:T(8,128)(2,1)S(1)}, u32[]{:S(2)}, u32[]{:S(2)}) %collective-permute-start.56) | collective-permute-done | bytes 172064 | tf_op jit(solution)/shard_map/ppermute | solution.py:89
  347.6 16.7 %collective-permute-done.45 = bf16[256,768]{1,0:T(8,128)(2,1)S(1)} collective-permute-done((bf16[256,768]{1,0:T(8,128)(2,1)S(1)}, bf16[256,768]{1,0:T(8,128)(2,1)S(1)}, u32[]{:S(2)}, u32[]{:S(2)}) %collective-permute-start.45) | collective-permute-done | bytes 393248 | tf_op jit(solution)/shard_map/ppermute | solution.py:89
  364.2 8.4 %collective-permute-done.46 = bf16[256,768]{1,0:T(8,128)(2,1)S(1)} collective-permute-done((bf16[256,768]{1,0:T(8,128)(2,1)S(1)}, bf16[256,768]{1,0:T(8,128)(2,1)S(1)}, u32[]{:S(2)}, u32[]{:S(2)}) %collective-permute-start.46) | collective-permute-done | bytes 393248 | tf_op jit(solution)/shard_map/ppermute | solution.py:89
  384.8 4.5 %collective-permute-done.67.refs_2_ = bf16[96,768]{1,0:T(8,128)(2,1)S(1)} collective-permute-done((bf16[96,768]{1,0:T(8,128)(2,1)S(1)}, bf16[96,768]{1,0:T(8,128)(2,1)S(1)}, u32[]{:S(2)}, u32[]{:S(2)}) %collective-permute-start.67) | collective-permute-done | bytes 147488 | tf_op jit(solution)/shard_map/ppermute | solution.py:98
  (271 shorter events, 193.2 us)
Async XLA Ops:
  2.8 22.7 %collective-permute-start.7 = (bf16[256,768]{1,0:T(8,128)(2,1)S(1)}, bf16[256,768]{1,0:T(8,128)(2,1)S(1)}, u32[]{:S(2)}, u32[]{:S(2)}) collective-permute-start(bf16[256,768]{1,0:T(8,128)(2,1)S(1)} %pick_quarter.1), channel_id=1, source_target_pairs={{0,4},{4,8},{8,12},{12,0},{1,5},{5,9},{9,13},{13,1},{2,6},{6,10},{... | collective-permute-start | bytes 1179656 | tf_op jit(solution)/shard_map/ppermute | solution.py:89
  23.8 29.7 %collective-permute-start.3 = (bf16[96,768]{1,0:T(8,128)(2,1)S(1)}, bf16[96,768]{1,0:T(8,128)(2,1)S(1)}, u32[]{:S(2)}, u32[]{:S(2)}) collective-permute-start(bf16[96,768]{1,0:T(8,128)(2,1)S(1)} %get-tuple-element.102), channel_id=1, source_target_pairs={{0,4},{4,8},{8,12},{12,0},{1,5},{5,9},{9,13},{13,1},{2,6},{6,10},{... | collective-permute-start | bytes 442376 | tf_op jit(solution)/shard_map/ppermute | solution.py:89
  25.5 29.5 %collective-permute-start.12 = (bf16[256,768]{1,0:T(8,128)(2,1)S(1)}, bf16[256,768]{1,0:T(8,128)(2,1)S(1)}, u32[]{:S(2)}, u32[]{:S(2)}) collective-permute-start(bf16[256,768]{1,0:T(8,128)(2,1)S(1)} %pick_quarter.1), channel_id=1, source_target_pairs={{0,12},{4,0},{8,4},{12,8},{1,13},{5,1},{9,5},{13,9},{2,14},{6,2},{... | collective-permute-start | bytes 1179656 | tf_op jit(solution)/shard_map/ppermute | solution.py:89
  25.5 36.5 %collective-permute-start.8 = (bf16[256,768]{1,0:T(8,128)(2,1)S(1)}, bf16[256,768]{1,0:T(8,128)(2,1)S(1)}, u32[]{:S(2)}, u32[]{:S(2)}) collective-permute-start(bf16[256,768]{1,0:T(8,128)(2,1)S(1)} %pick_quarter.1), channel_id=1, source_target_pairs={{0,8},{4,12},{8,0},{12,4},{1,9},{5,13},{9,1},{13,5},{2,10},{6,14},... | collective-permute-start | bytes 1179656 | tf_op jit(solution)/shard_map/ppermute | solution.py:89
  53.6 22.6 %collective-permute-start.6 = (bf16[4,96,768]{2,1,0:T(8,128)(2,1)S(1)}, bf16[4,96,768]{2,1,0:T(8,128)(2,1)S(1)}, u32[]{:S(2)}, u32[]{:S(2)}) collective-permute-start(bf16[4,96,768]{2,1,0:T(8,128)(2,1)S(1)} %pad_maximum_fusion.1.near_ref), channel_id=1, source_target_pairs={{0,16},{16,0},{1,17},{17,1},{2,18},{18,2},{3,19},{19,3},{4,20},{20... | collective-permute-start | bytes 1769480 | tf_op jit(solution)/shard_map/ppermute | solution.py:94
  55.2 20.9 %collective-permute-start.16 = (bf16[256,768]{1,0:T(8,128)(2,1)S(1)}, bf16[256,768]{1,0:T(8,128)(2,1)S(1)}, u32[]{:S(2)}, u32[]{:S(2)}) collective-permute-start(bf16[256,768]{1,0:T(8,128)(2,1)S(1)} %collective-permute-done.7.refs_0_), channel_id=1, source_target_pairs={{0,1},{1,0},{2,3},{3,2},{4,5},{5,4},{6,7},{7,6},{8,9},{9,8},{10,11... | collective-permute-start | bytes 1179656 | tf_op jit(solution)/shard_map/ppermute | solution.py:84
  63.2 23.3 %collective-permute-start.18 = (bf16[256,768]{1,0:T(8,128)(2,1)S(1)}, bf16[256,768]{1,0:T(8,128)(2,1)S(1)}, u32[]{:S(2)}, u32[]{:S(2)}) collective-permute-start(bf16[256,768]{1,0:T(8,128)(2,1)S(1)} %collective-permute-done.17.refs_2_), channel_id=1, source_target_pairs={{0,1},{1,0},{2,3},{3,2},{4,5},{5,4},{6,7},{7,6},{8,9},{9,8},{10,11... | collective-permute-start | bytes 1179656 | tf_op jit(solution)/shard_map/ppermute | solution.py:84
  109.8 20.7 %collective-permute-start.20 = (bf16[256,768]{1,0:T(8,128)(2,1)S(1)}, bf16[256,768]{1,0:T(8,128)(2,1)S(1)}, u32[]{:S(2)}, u32[]{:S(2)}) collective-permute-start(bf16[256,768]{1,0:T(8,128)(2,1)S(1)} %add_convert_fusion.4), channel_id=1, source_target_pairs={{0,2},{1,3},{2,0},{3,1},{4,6},{5,7},{6,4},{7,5},{8,10},{9,11},{10,... | collective-permute-start | bytes 1179656 | tf_op jit(solution)/shard_map/ppermute | solution.py:84
  129.0 27.1 %collective-permute-start.25 = (bf16[4,192,768]{2,1,0:T(8,128)(2,1)S(1)}, bf16[4,192,768]{2,1,0:T(8,128)(2,1)S(1)}, u32[]{:S(2)}, u32[]{:S(2)}) collective-permute-start(bf16[4,192,768]{2,1,0:T(8,128)(2,1)S(1)} %pad_maximum_fusion.near_ref), channel_id=1, source_target_pairs={{0,16},{16,0},{1,17},{17,1},{2,18},{18,2},{3,19},{19,3},{4,20},{20... | collective-permute-start | bytes 3538952 | tf_op jit(solution)/shard_map/ppermute | solution.py:94
  247.9 33.2 %collective-permute-start.43 = (bf16[1024,768]{1,0:T(8,128)(2,1)}, bf16[1024,768]{1,0:T(8,128)(2,1)}, u32[]{:S(2)}, u32[]{:S(2)}) collective-permute-start(bf16[1024,768]{1,0:T(8,128)(2,1)} %get-tuple-element.143), channel_id=1, source_target_pairs={{0,1},{1,0},{2,3},{3,2},{4,5},{5,4},{6,7},{7,6},{8,9},{9,8},{10,11... | collective-permute-start | bytes 4718600 | tf_op jit(solution)/shard_map/ppermute | solution.py:84
  255.3 34.0 %collective-permute-start.47 = (bf16[1024,768]{1,0:T(8,128)(2,1)}, bf16[1024,768]{1,0:T(8,128)(2,1)}, u32[]{:S(2)}, u32[]{:S(2)}) collective-permute-start(bf16[1024,768]{1,0:T(8,128)(2,1)} %get-tuple-element.146), channel_id=1, source_target_pairs={{0,1},{1,0},{2,3},{3,2},{4,5},{5,4},{6,7},{7,6},{8,9},{9,8},{10,11... | collective-permute-start | bytes 4718600 | tf_op jit(solution)/shard_map/ppermute | solution.py:84
  268.1 23.9 %collective-permute-start.61 = (bf16[4,96,768]{2,1,0:T(8,128)(2,1)S(1)}, bf16[4,96,768]{2,1,0:T(8,128)(2,1)S(1)}, u32[]{:S(2)}, u32[]{:S(2)}) collective-permute-start(bf16[4,96,768]{2,1,0:T(8,128)(2,1)S(1)} %get-tuple-element.171), channel_id=1, source_target_pairs={{0,16},{16,0},{1,17},{17,1},{2,18},{18,2},{3,19},{19,3},{4,20},{20... | collective-permute-start | bytes 1769480 | tf_op jit(solution)/shard_map/ppermute | solution.py:94
  278.3 23.4 %collective-permute-start.53 = (bf16[4,112,768]{2,1,0:T(8,128)(2,1)S(1)}, bf16[4,112,768]{2,1,0:T(8,128)(2,1)S(1)}, u32[]{:S(2)}, u32[]{:S(2)}) collective-permute-start(bf16[4,112,768]{2,1,0:T(8,128)(2,1)S(1)} %get-tuple-element.156), channel_id=1, source_target_pairs={{0,16},{16,0},{1,17},{17,1},{2,18},{18,2},{3,19},{19,3},{4,20},{20... | collective-permute-start | bytes 2064392 | tf_op jit(solution)/shard_map/ppermute | solution.py:94
  281.1 22.0 %collective-permute-start.60 = (bf16[96,768]{1,0:T(8,128)(2,1)S(1)}, bf16[96,768]{1,0:T(8,128)(2,1)S(1)}, u32[]{:S(2)}, u32[]{:S(2)}) collective-permute-start(bf16[96,768]{1,0:T(8,128)(2,1)S(1)} %get-tuple-element.195), channel_id=1, source_target_pairs={{0,8},{4,12},{8,0},{12,4},{1,9},{5,13},{9,1},{13,5},{2,10},{6,14},... | collective-permute-start | bytes 442376 | tf_op jit(solution)/shard_map/ppermute | solution.py:89
  281.2 26.8 %collective-permute-start.59 = (bf16[96,768]{1,0:T(8,128)(2,1)S(1)}, bf16[96,768]{1,0:T(8,128)(2,1)S(1)}, u32[]{:S(2)}, u32[]{:S(2)}) collective-permute-start(bf16[96,768]{1,0:T(8,128)(2,1)S(1)} %get-tuple-element.196), channel_id=1, source_target_pairs={{0,12},{4,0},{8,4},{12,8},{1,13},{5,1},{9,5},{13,9},{2,14},{6,2},{... | collective-permute-start | bytes 442376 | tf_op jit(solution)/shard_map/ppermute | solution.py:89
  289.3 40.2 %collective-permute-start.44 = (bf16[2,256,768]{2,1,0:T(8,128)(2,1)S(1)}, bf16[2,256,768]{2,1,0:T(8,128)(2,1)S(1)}, u32[]{:S(2)}, u32[]{:S(2)}) collective-permute-start(bf16[2,256,768]{2,1,0:T(8,128)(2,1)S(1)} %fusion), channel_id=1, source_target_pairs={{0,2},{1,3},{2,0},{3,1},{4,6},{5,7},{6,4},{7,5},{8,10},{9,11},{10,... | collective-permute-start | bytes 2359304 | tf_op jit(solution)/shard_map/ppermute | solution.py:84
  301.7 29.6 %collective-permute-start.48 = (bf16[2,256,768]{2,1,0:T(8,128)(2,1)S(1)}, bf16[2,256,768]{2,1,0:T(8,128)(2,1)S(1)}, u32[]{:S(2)}, u32[]{:S(2)}) collective-permute-start(bf16[2,256,768]{2,1,0:T(8,128)(2,1)S(1)} %fusion.1), channel_id=1, source_target_pairs={{0,2},{1,3},{2,0},{3,1},{4,6},{5,7},{6,4},{7,5},{8,10},{9,11},{10,... | collective-permute-start | bytes 2359304 | tf_op jit(solution)/shard_map/ppermute | solution.py:84
  313.1 21.9 %collective-permute-start.64 = (bf16[96,768]{1,0:T(8,128)(2,1)S(1)}, bf16[96,768]{1,0:T(8,128)(2,1)S(1)}, u32[]{:S(2)}, u32[]{:S(2)}) collective-permute-start(bf16[96,768]{1,0:T(8,128)(2,1)S(1)} %get-tuple-element.192), channel_id=1, source_target_pairs={{0,8},{4,12},{8,0},{12,4},{1,9},{5,13},{9,1},{13,5},{2,10},{6,14},... | collective-permute-start | bytes 442376 | tf_op jit(solution)/shard_map/ppermute | solution.py:89
  338.9 25.3 %collective-permute-start.45 = (bf16[256,768]{1,0:T(8,128)(2,1)S(1)}, bf16[256,768]{1,0:T(8,128)(2,1)S(1)}, u32[]{:S(2)}, u32[]{:S(2)}) collective-permute-start(bf16[256,768]{1,0:T(8,128)(2,1)S(1)} %get-tuple-element.187), channel_id=1, source_target_pairs={{0,8},{4,12},{8,0},{12,4},{1,9},{5,13},{9,1},{13,5},{2,10},{6,14},... | collective-permute-start | bytes 1179656 | tf_op jit(solution)/shard_map/ppermute | solution.py:89
  338.9 33.8 %collective-permute-start.46 = (bf16[256,768]{1,0:T(8,128)(2,1)S(1)}, bf16[256,768]{1,0:T(8,128)(2,1)S(1)}, u32[]{:S(2)}, u32[]{:S(2)}) collective-permute-start(bf16[256,768]{1,0:T(8,128)(2,1)S(1)} %get-tuple-element.188), channel_id=1, source_target_pairs={{0,4},{4,8},{8,12},{12,0},{1,5},{5,9},{9,13},{13,1},{2,6},{6,10},{... | collective-permute-start | bytes 1179656 | tf_op jit(solution)/shard_map/ppermute | solution.py:89
  341.8 32.9 %collective-permute-start.39 = (bf16[256,768]{1,0:T(8,128)(2,1)S(1)}, bf16[256,768]{1,0:T(8,128)(2,1)S(1)}, u32[]{:S(2)}, u32[]{:S(2)}) collective-permute-start(bf16[256,768]{1,0:T(8,128)(2,1)S(1)} %get-tuple-element.138.refs_0_), channel_id=1, source_target_pairs={{0,1},{1,0},{2,3},{3,2},{4,5},{5,4},{6,7},{7,6},{8,9},{9,8},{10,11... | collective-permute-start | bytes 1179656 | tf_op jit(solution)/shard_map/ppermute | solution.py:84
  342.8 32.0 %collective-permute-start.41 = (bf16[256,768]{1,0:T(8,128)(2,1)S(1)}, bf16[256,768]{1,0:T(8,128)(2,1)S(1)}, u32[]{:S(2)}, u32[]{:S(2)}) collective-permute-start(bf16[256,768]{1,0:T(8,128)(2,1)S(1)} %collective-permute-done.40.refs_2_), channel_id=1, source_target_pairs={{0,1},{1,0},{2,3},{3,2},{4,5},{5,4},{6,7},{7,6},{8,9},{9,8},{10,11... | collective-permute-start | bytes 1179656 | tf_op jit(solution)/shard_map/ppermute | solution.py:84
  347.3 35.9 %collective-permute-start.69 = (f32[6,96]{1,0:T(8,128)S(1)}, f32[6,96]{1,0:T(8,128)S(1)}, u32[]{:S(2)}, u32[]{:S(2)}) collective-permute-start(f32[6,96]{1,0:T(8,128)S(1)} %slice_add_fusion), channel_id=1, source_target_pairs={{0,2},{1,3},{2,0},{3,1},{4,6},{5,7},{6,4},{7,5},{8,10},{9,11},{10,... | collective-permute-start | bytes 6920 | tf_op jit(solution)/shard_map/ppermute | solution.py:84
  374.1 23.3 %collective-permute-start.51 = (bf16[256,768]{1,0:T(8,128)(2,1)S(1)}, bf16[256,768]{1,0:T(8,128)(2,1)S(1)}, u32[]{:S(2)}, u32[]{:S(2)}) collective-permute-start(bf16[256,768]{1,0:T(8,128)(2,1)S(1)} %fusion.3.refs_0_), channel_id=1, source_target_pairs={{0,2},{1,3},{2,0},{3,1},{4,6},{5,7},{6,4},{7,5},{8,10},{9,11},{10,... | collective-permute-start | bytes 1179656 | tf_op jit(solution)/shard_map/ppermute | solution.py:84
  (94 other events, 885.0 us)

commit v2 on v1

--- a/solution.py
+++ b/solution.py
@@ -26,7 +26,8 @@
 ANY = pl.ANY
 bf16 = jnp.bfloat16
 f32 = jnp.float32
-OWN = ("shard", "ctx")
+SHARD, CTX, TP = "shard", "ctx", "tp"
+OWN = (SHARD, CTX)
 
 
 def params_of(mib, **more):
@@ -35,6 +36,14 @@
 
 def in_place():
     return pl.BlockSpec(memory_space=ANY)
+
+
+def direct():
+    return pl.BlockSpec(memory_space=pltpu.VMEM)
+
+
+def scalars():
+    return pl.BlockSpec(memory_space=pltpu.SMEM)
 
 
 def whole_block(shape, single=False):
@@ -80,18 +89,30 @@
 
 
 def swap(rows, mask):
-    count = lax.axis_size("tp")
-    return lax.ppermute(rows, "tp", [(i, i ^ mask) for i in range(count)])
+    count = lax.axis_size(TP)
+    return lax.ppermute(rows, TP, [(i, i ^ mask) for i in range(count)])
 
 
 def shift_ctx(rows, step):
-    count = lax.axis_size("ctx")
-    return lax.ppermute(rows, "ctx", [(i, (i + step) % count) for i in range(count)])
+    count = lax.axis_size(CTX)
+    return lax.ppermute(rows, CTX, [(i, (i + step) % count) for i in range(count)])
+
+
+def forward_two(from_left, from_right):
+    right = lax.ppermute(from_left, CTX, [(1, 2), (2, 3)])
+    left = lax.ppermute(from_right, CTX, [(1, 0), (2, 1)])
+    return right + left
+
+
+def back_two(rows):
+    right = lax.ppermute(rows, CTX, [(0, 1), (1, 2)])
+    left = lax.ppermute(rows, CTX, [(2, 1), (3, 2)])
+    return right, left
 
 
 def shift_shard(rows, step):
-    count = lax.axis_size("shard")
-    return lax.ppermute(rows, "shard", [(i, (i + step) % count) for i in range(count)])
+    count = lax.axis_size(SHARD)
+    return lax.ppermute(rows, SHARD, [(i, (i + step) % count) for i in range(count)])
 
 
 def owner_move(rows, pairs):
@@ -120,7 +141,7 @@
         out_specs=pl.BlockSpec((PB, PB * WIDE), lambda i: (i, 0)),
         out_shape=jax.ShapeDtypeStruct((rows * PB, PB * WIDE), bf16),
         compiler_params=params_of(3),
-        name="pack_rows",
+        name="pack",
     )(blocks)
 
 
@@ -156,7 +177,7 @@
         ),
         scratch_shapes=[pltpu.VMEM((near.shape[0] + far.shape[0], PB, D), bf16)],
         compiler_params=params_of(8),
-        name="unpack_first",
+        name="unpack",
     )(turns, near, far)
 
 
@@ -217,7 +238,7 @@
         out_specs=[smem] * 4,
         out_shape=[jax.ShapeDtypeStruct(shape, jnp.int32) for shape in shapes],
         compiler_params=params_of(2),
-        name="index_tables",
+        name="tables",
     )(ids, lengths, global_blocks, random_blocks)
 
 
@@ -237,7 +258,7 @@
         ),
         out_shape=jax.ShapeDtypeStruct((rows, D), bf16),
         compiler_params=params_of(3),
-        name="pick_quarter",
+        name="pick",
     )(ids, values)
 
 
@@ -256,15 +277,11 @@
     rows = pieces[0].shape[0]
     return pl.pallas_call(
         place_kernel,
-        grid_spec=pltpu.PrefetchScalarGridSpec(
-            num_scalar_prefetch=1,
-            grid=(1,),
-            in_specs=[in_place()] * 4,
-            out_specs=whole_block((4 * rows, D), single=True),
-            scratch_shapes=[pltpu.SemaphoreType.DMA((4,))],
-        ),
+        in_specs=[scalars()] + [in_place()] * 4,
+        out_specs=in_place(),
+        scratch_shapes=[pltpu.SemaphoreType.DMA((4,))],
         out_shape=jax.ShapeDtypeStruct((4 * rows, D), bf16),
-        compiler_params=params_of(4),
+        compiler_params=params_of(2),
     )(ids, *pieces)
 
 
@@ -292,7 +309,7 @@
             jax.ShapeDtypeStruct((2 * PB, D), bf16),
         ],
         compiler_params=params_of(4),
-        name="sort_held",
+        name="sort",
     )(turns, *held)
 
 
@@ -316,51 +333,33 @@
         ),
         out_shape=[jax.ShapeDtypeStruct((PB, D), bf16)] * 3,
         compiler_params=params_of(6),
-        name="deal_rows",
+        name="dealt",
     )(turns, first, up, down)
 
 
-def project_kernel(ids_ref, *refs, step, heads_q, chained):
-    count = 1 if heads_q else 4
-    pieces = refs[:count]
-    rest = list(refs[count:])
+def project_kernel(ids_ref, *refs, step, with_q, chained):
+    pieces = refs[: 1 if with_q else 4]
+    rest = list(refs[len(pieces) :])
     wkv_ref, bkv_ref = rest[:2]
     rest = rest[2:]
-    if heads_q:
+    if with_q:
         wq_ref, bq_ref = rest[:2]
         rest = rest[2:]
     if chained:
         rest = rest[2:]
     in_all, kv_all = rest[:2]
-    rest = rest[2:]
-    if heads_q:
-        q_ref = rest[0]
-        rest = rest[1:]
-    x_ref, kv_ref, sem, out_sem = rest
-    tokens = x_ref.shape[0]
+    tokens = pieces[0].shape[0] * len(pieces)
     rows = tokens // 4
-    loads = []
     for r in range(4):
-        if heads_q:
-            source = pieces[0].at[pl.ds(pl.multiple_of((ids_ref[0] ^ r) * rows, rows), rows)]
+        if with_q:
+            x = pieces[0][pl.ds(pl.multiple_of((ids_ref[0] ^ r) * rows, rows), rows), :]
         else:
-            source = pieces[r]
-        loads.append(copy_in(source, x_ref.at[pl.ds(r * rows, rows)], sem.at[r]))
-    for load in loads:
-        load.wait()
-    saves = [copy_in(x_ref, in_all.at[pl.ds(step * tokens, tokens)], out_sem.at[0])]
-
-    def body(r, carry):
-        mine = pl.ds(pl.multiple_of(r * rows, rows), rows)
-        kv_ref[mine, :] = (dot32(x_ref[mine, :], wkv_ref[...]) + bkv_ref[...]).astype(bf16)
-        if heads_q:
-            q_ref[mine, :] = (dot32(x_ref[mine, :], wq_ref[...]) + bq_ref[...]).astype(bf16)
-        return carry
-
-    lax.fori_loop(0, 4, body, 0)
-    saves.append(copy_in(kv_ref, kv_all.at[pl.ds(step * tokens, tokens)], out_sem.at[1]))
-    for save in saves:
-        save.wait()
+            x = pieces[r][...]
+        mine = slice(step * tokens + r * rows, step * tokens + (r + 1) * rows)
+        in_all[mine, :] = x
+        kv_all[mine, :] = (dot32(x, wkv_ref[...]) + bkv_ref[...]).astype(bf16)
+        if with_q:
+            rest[2][r * rows : (r + 1) * rows, :] = (dot32(x, wq_ref[...]) + bq_ref[...]).astype(bf16)
 
 
 def project_chunk(ids, pieces, step, count, w_kv, b_kv, w_q, b_q, carried):
@@ -370,37 +369,22 @@
     with_q = w_q is not None
     chained = carried is not None
     args = list(pieces) + [w_kv, b_kv]
-    specs = [in_place()] * len(pieces) + [whole_block(w_kv.shape), whole_block(b_kv.shape)]
     if with_q:
         args += [w_q, b_q]
-        specs += [whole_block(w_q.shape), whole_block(b_q.shape)]
     aliases = {}
     if chained:
         aliases = {len(args) + 1: 0, len(args) + 2: 1}
         args += list(carried)
-        specs += [in_place()] * 2
     shapes = [
         jax.ShapeDtypeStruct((count * tokens, width), bf16),
         jax.ShapeDtypeStruct((count * tokens, kv_cols), bf16),
     ]
-    outs = [in_place()] * 2
     if with_q:
         shapes.append(jax.ShapeDtypeStruct((tokens, w_q.shape[1]), bf16))
-        outs.append(whole_block((tokens, w_q.shape[1])))
-    return pl.pallas_call(
-        functools.partial(project_kernel, step=step, heads_q=with_q, chained=chained),
-        grid_spec=pltpu.PrefetchScalarGridSpec(
-            num_scalar_prefetch=1,
-            grid=(1,),
-            in_specs=specs,
-            out_specs=outs,
-            scratch_shapes=[
-                pltpu.VMEM((tokens, width), bf16),
-                pltpu.VMEM((tokens, kv_cols), bf16),
-                pltpu.SemaphoreType.DMA((4,)),
-                pltpu.SemaphoreType.DMA((2,)),
-            ],
-        ),
+    return pl.pallas_call(
+        functools.partial(project_kernel, step=step, with_q=with_q, chained=chained),
+        in_specs=[scalars()] + [direct()] * len(args),
+        out_specs=[direct()] * len(shapes),
         out_shape=shapes,
         input_output_aliases=aliases,
         compiler_params=params_of(8),
@@ -437,7 +421,7 @@
         out_shape=[shape, shape],
         compiler_params=params_of(4),
         cost_estimate=cost(2 * tokens * wide * D, 2 * tokens * (wide + D)),
-        name="out_project",
+        name="oproj",
     )(att, w_out)
 
 
@@ -478,7 +462,7 @@
         ],
         compiler_params=params_of(5),
         cost_estimate=cost(20 * rows * D, 20 * rows * D),
-        name="first_norm",
+        name="norm1",
     )(ids, values, keep, sent, got, vectors)
 
 
@@ -526,7 +510,7 @@
         ],
         compiler_params=params_of(6),
         cost_estimate=cost(40 * rows * D, 20 * rows * D),
-        name="second_norm",
+        name="norm2",
     )(turns, x1, keep, sent, got, cot, vectors)
 
 
@@ -564,36 +548,26 @@
         ],
         compiler_params=params_of(6),
         cost_estimate=cost(40 * rows * D, 20 * rows * D),
-        name="first_back",
+        name="back1",
     )(hidden, d_mixed, keep, sent, got, vectors)
 
 
-def assemble_kernel(turn_ref, near_ref, far_ref, up_ref, down_ref, sem):
+def assemble_kernel(turn_ref, near_ref, far_ref, up_ref, down_ref):
     near = near_ref.shape[0]
-    copies = []
     for p in range(WIDE):
-        source = near_ref.at[p] if p < near else far_ref.at[p - near]
         start = pl.multiple_of(turn_ref[2 * WIDE + p] * PB, PB)
         for n, target in enumerate((up_ref, down_ref)):
-            copies.append(
-                copy_in(source.at[pl.ds(PB * n, PB)], target.at[pl.ds(start, PB)], sem)
-            )
-    for copy in copies:
-        copy.wait()
+            cut = slice(PB * n, PB * (n + 1))
+            target[pl.ds(start, PB), :] = near_ref[p, cut] if p < near else far_ref[p - near, cut]
 
 
 def assemble(turns, near, far):
     return pl.pallas_call(
         assemble_kernel,
-        grid_spec=pltpu.PrefetchScalarGridSpec(
-            num_scalar_prefetch=1,
-            grid=(1,),
-            in_specs=[in_place()] * 2,
-            out_specs=[whole_block((D, D), single=True)] * 2,
-            scratch_shapes=[pltpu.SemaphoreType.DMA],
-        ),
+        in_specs=[scalars(), direct(), direct()],
+        out_specs=[direct()] * 2,
         out_shape=[jax.ShapeDtypeStruct((D, D), bf16)] * 2,
-        compiler_params=params_of(5),
+        compiler_params=params_of(6),
         cost_estimate=cost(0, 8 * D * D),
         name="assemble",
     )(turns, near, far)
@@ -648,7 +622,7 @@
         ],
         compiler_params=params_of(13),
         cost_estimate=cost(8 * rows * D * D, 24 * rows * D),
-        name="feed_forward",
+        name="feed",
     )(piece_a, piece_b, w_up, w_down, up_bias)
 
 
@@ -704,7 +678,7 @@
         ],
         compiler_params=params_of(13),
         cost_estimate=cost(8 * rows * D * D, 24 * rows * D),
-        name="feed_back",
+        name="fback",
     )(piece_a, piece_b, w_up, w_down, gate)
 
 
@@ -750,17 +724,8 @@
     part = dot32(dkv_ref[...], w_ref[...], ((1,), (1,)))
     if with_q:
 
-        @pl.when(i >= pl.num_programs(0) - 4)
-        def _():
-            more = part + dot32(refs[0][...], refs[1][...], ((1,), (1,)))
-            split_store(i, more.astype(bf16), keep_ref, send_ref)
-
-        @pl.when(i < pl.num_programs(0) - 4)
-        def _():
-            split_store(i, part.astype(bf16), keep_ref, send_ref)
-
-    else:
-        split_store(i, part.astype(bf16), keep_ref, send_ref)
+        part = part + dot32(refs[0][...], refs[1][...], ((1,), (1,)))
+    split_store(i, part.astype(bf16), keep_ref, send_ref)
 
 
 def dx_part(d_kv, w_kv, steps, tokens, d_query, w_q):
@@ -799,117 +764,92 @@
 def late_kernel(
     turn_ref, x_ref, dkv_ref, dq_ref, att_ref, db_ref, s1_ref, s2_ref, sa_ref, bn_ref, bf_ref, top_ref,
     keep_ref, send_ref, acc_kv, acc_q, acc_o, turn_kv, turn_q, inner_ref, vec_ref, all_ref,
-    *, cols, steps_q, heads, owners
+    *, cols, tile, heads, owners
 ):
-    i = pl.program_id(0)
-
-    @pl.when(i == 0)
-    def _():
-        acc_kv[...] = jnp.zeros(acc_kv.shape, f32)
-        acc_q[...] = jnp.zeros(acc_q.shape, f32)
-        acc_o[...] = jnp.zeros(acc_o.shape, f32)
-
-    x = x_ref[...]
-    acc_kv[...] += dot32(dkv_ref[...], x, ((0,), (0,)))
-
-    @pl.when(i < steps_q)
-    def _():
-        acc_q[...] += dot32(dq_ref[...], x, ((0,), (0,)))
-        acc_o[...] += dot32(att_ref[...], db_ref[...], ((0,), (0,)))
-
-    @pl.when(i == pl.num_programs(0) - 1)
-    def _():
-        turn_kv[...] = acc_kv[...].T.astype(bf16)
-        turn_q[...] = acc_q[...].T.astype(bf16)
-        pad = acc_o.shape[0] - cols
-        for k in range(D // PB):
-            for c in range(3):
-                unit = 3 * k + c
-                rows = slice(PB * k, PB * (k + 1))
-                piece = turn_q[rows, :cols] if c == 0 else turn_kv[rows, cols * (c - 1) : cols * c]
-                all_ref[
-                    turn_ref[WIDE + unit // 4], :PB, cols * (unit % 4) : cols * (unit % 4 + 1)
-                ] = piece
-        for k in range(cols // PB):
-            all_ref[turn_ref[WIDE + 3 * cols // PB + k], :PB, :] = acc_o[
-                pad + PB * k : pad + PB * (k + 1), :
-            ].astype(bf16)
-        inner_ref[0:1, :cols] = sa_ref[0:1, :cols]
-        inner_ref[0:1, cols : 2 * cols] = sa_ref[1:2, pad : pad + cols]
-        inner_ref[0:1, 2 * cols :] = bn_ref[0:1, :] + bf_ref[0:1, :]
-        outer_cols = D // owners
-        inner_cols = inner_ref.shape[1] // owners
-        lane = lax.broadcasted_iota(jnp.int32, (1, D), 1)
-        slots = jnp.zeros((1, D), f32)
-        base = turn_ref[3 * WIDE] * 3 * heads
-        for h in range(heads):
-            left = top_ref[h : h + 1, :1]
-            for part in range(3):
-                piece = left.astype(bf16).astype(f32)
-                slots = jnp.where(lane == base + part * heads + h, piece, slots)
-                left = left - piece
-        vec_ref[...] = jnp.zeros(vec_ref.shape, f32)
-        vec_ref[7:8, :] = slots
-        outer_rows = [(s1_ref, 2), (s2_ref, 2), (s1_ref, 0), (s1_ref, 1), (s2_ref, 0), (s2_ref, 1)]
-        for k in range(owners):
-            for n, (ref, row) in enumerate(outer_rows):
-                vec_ref[n : n + 1, :outer_cols] = ref[
-                    row : row + 1, outer_cols * k : outer_cols * (k + 1)
-                ]
-            vec_ref[6:7, :inner_cols] = inner_ref[0:1, inner_cols * k : inner_cols * (k + 1)]
-            all_ref[turn_ref[WIDE + k], PB:, :] = vec_ref[...].astype(bf16)
-        near = keep_ref.shape[0]
-        keep_ref[...] = all_ref[:near]
-        send_ref[...] = all_ref[near:]
+
+    acc_kv[...] = jnp.zeros(acc_kv.shape, f32)
+
+    def step(i, carry):
+        mine = pl.ds(pl.multiple_of(i * tile, tile), tile)
+        acc_kv[...] += dot32(dkv_ref[mine, :], x_ref[mine, :], ((0,), (0,)))
+        return carry
+
+    lax.fori_loop(0, x_ref.shape[0] // tile, step, 0)
+    own = slice(0, dq_ref.shape[0])
+    acc_q[...] = dot32(dq_ref[...], x_ref[own, :], ((0,), (0,)))
+    acc_o[...] = dot32(att_ref[...], db_ref[...], ((0,), (0,)))
+    turn_kv[...] = acc_kv[...].T.astype(bf16)
+    turn_q[...] = acc_q[...].T.astype(bf16)
+    pad = acc_o.shape[0] - cols
+    for k in range(D // PB):
+        for c in range(3):
+            unit = 3 * k + c
+            rows = slice(PB * k, PB * (k + 1))
+            piece = turn_q[rows, :cols] if c == 0 else turn_kv[rows, cols * (c - 1) : cols * c]
+            all_ref[
+                turn_ref[WIDE + unit // 4], :PB, cols * (unit % 4) : cols * (unit % 4 + 1)
+            ] = piece
+    for k in range(cols // PB):
+        all_ref[turn_ref[WIDE + 3 * cols // PB + k], :PB, :] = acc_o[
+            pad + PB * k : pad + PB * (k + 1), :
+        ].astype(bf16)
+    inner_ref[0:1, :cols] = sa_ref[0:1, :cols]
+    inner_ref[0:1, cols : 2 * cols] = sa_ref[1:2, pad : pad + cols]
+    inner_ref[0:1, 2 * cols :] = bn_ref[0:1, :] + bf_ref[0:1, :]
+    outer_cols = D // owners
+    inner_cols = inner_ref.shape[1] // owners
+    lane = lax.broadcasted_iota(jnp.int32, (1, D), 1)
+    slots = jnp.zeros((1, D), f32)
+    base = turn_ref[3 * WIDE] * 3 * heads
+    for h in range(heads):
+        left = top_ref[h : h + 1, :1]
+        for part in range(3):
+            piece = left.astype(bf16).astype(f32)
+            slots = jnp.where(lane == base + part * heads + h, piece, slots)
+            left = left - piece
+    vec_ref[...] = jnp.zeros(vec_ref.shape, f32)
+    vec_ref[7:8, :] = slots
+    outer_rows = [(s1_ref, 2), (s2_ref, 2), (s1_ref, 0), (s1_ref, 1), (s2_ref, 0), (s2_ref, 1)]
+    for k in range(owners):
+        for n, (ref, row) in enumerate(outer_rows):
+            vec_ref[n : n + 1, :outer_cols] = ref[
+                row : row + 1, outer_cols * k : outer_cols * (k + 1)
+            ]
+        vec_ref[6:7, :inner_cols] = inner_ref[0:1, inner_cols * k : inner_cols * (k + 1)]
+        all_ref[turn_ref[WIDE + k], PB:, :] = vec_ref[...].astype(bf16)
+    near = keep_ref.shape[0]
+    keep_ref[...] = all_ref[:near]
+    send_ref[...] = all_ref[near:]
 
 
 def late_grads(turns, in_all, d_kv, d_query, att, d_branch, s1, s2, sa, bn, bf, tops, cols, heads, near):
-    tokens, wide = d_query.shape
-    tile = min(512, tokens)
-    steps_q = tokens // tile
+    _, wide = d_query.shape
+    tile = 1024
     owners = WIDE
     under = 16
 
-    def rows_of(width, last):
-        return pl.BlockSpec((tile, width), lambda i, *_: (jnp.minimum(i, last), 0))
-
-    steps = in_all.shape[0] // tile
     small = [s1, s2, sa, bn, bf, tops]
     return pl.pallas_call(
-        functools.partial(late_kernel, cols=cols, steps_q=steps_q, heads=heads, owners=owners),
-        grid_spec=pltpu.PrefetchScalarGridSpec(
-            num_scalar_prefetch=1,
-            grid=(steps,),
-            in_specs=[
-                rows_of(D, steps - 1),
-                rows_of(2 * cols, steps - 1),
-                rows_of(wide, steps_q - 1),
-                rows_of(wide, steps_q - 1),
-                rows_of(D, steps_q - 1),
-            ]
-            + [whole_block(v.shape) for v in small],
-            out_specs=[
-                whole_block((near, PB + under, D)),
-                whole_block((owners - near, PB + under, D)),
-            ],
-            scratch_shapes=[
-                pltpu.VMEM((2 * cols, D), f32),
-                pltpu.VMEM((wide, D), f32),
-                pltpu.VMEM((wide, D), f32),
-                pltpu.VMEM((D, 2 * cols), bf16),
-                pltpu.VMEM((D, wide), bf16),
-                pltpu.VMEM((1, 2 * cols + D), f32),
-                pltpu.VMEM((under, D), f32),
-                pltpu.VMEM((owners, PB + under, D), bf16),
-            ],
-        ),
+        functools.partial(late_kernel, cols=cols, tile=tile, heads=heads, owners=owners),
+        in_specs=[scalars()] + [direct()] * (5 + len(small)),
+        out_specs=[direct()] * 2,
+        scratch_shapes=[
+            pltpu.VMEM((2 * cols, D), f32),
+            pltpu.VMEM((wide, D), f32),
+            pltpu.VMEM((wide, D), f32),
+            pltpu.VMEM((D, 2 * cols), bf16),
+            pltpu.VMEM((D, wide), bf16),
+            pltpu.VMEM((1, 2 * cols + D), f32),
+            pltpu.VMEM((under, D), f32),
+            pltpu.VMEM((owners, PB + under, D), bf16),
+        ],
         out_shape=[
             jax.ShapeDtypeStruct((near, PB + under, D), bf16),
             jax.ShapeDtypeStruct((owners - near, PB + under, D), bf16),
         ],
         compiler_params=params_of(20),
         cost_estimate=cost(2 * in_all.shape[0] * D * 2 * cols, 2 * in_all.shape[0] * (D + 2 * cols)),
-        name="late_grads",
+        name="late",
     )(turns, in_all, d_kv, d_query, att, d_branch, *small)
 
 
@@ -942,44 +882,42 @@
 
 
 def fwd_kernel(
-    addr_ref, valid_ref, query_ref, q_ref, kv_src, att_ref, p_ref, top_ref, kv_ref, sem, *, heads, group
+    addr_ref, valid_ref, query_ref, q_ref, kv_ref, att_ref, p_ref, top_ref, *, heads, group
 ):
-    i = pl.program_id(0)
     wide = q_ref.shape[1]
     start = kv_ref.shape[1] - wide
-
-    @pl.when(i == 0)
-    def _():
-        load = copy_in(kv_src, kv_ref, sem)
-        top_ref[...] = jnp.full(top_ref.shape, neg_large, f32)
-        load.wait()
-
+    top_ref[...] = jnp.full(top_ref.shape, neg_large, f32)
     scale = jnp.asarray(HEAD ** (-0.5), bf16)
     q_masks = head_masks(wide, heads, 0)
     v_masks = head_masks(wide, heads, (heads * HEAD - start) // HEAD)
     lane = lax.broadcasted_iota(jnp.int32, (1, LIST * BLOCK), 1)
-    for u in range(group):
-        block = i * group + u
-        mine = slice(u * BLOCK, (u + 1) * BLOCK)
-        q_all = spread(q_ref[mine] * scale, q_masks)
-        listed = listed_rows(addr_ref, kv_ref, block)
-        scores = dot32(q_all, listed[:, :wide], ((1,), (1,)))
-        limit = jnp.zeros((1, LIST * BLOCK), jnp.int32)
-        for e in range(LIST):
-            limit = jnp.where(lane // BLOCK == e, valid_ref[block * LIST + e], limit)
-        scores = jnp.where(lane % BLOCK < limit, scores, neg_large)
-        row_top = jnp.max(scores, axis=1, keepdims=True)
-        shifted = jnp.exp(scores - row_top)
-        probs = shifted * (1.0 / jnp.sum(shifted, axis=1, keepdims=True))
-        probs_low = probs.astype(bf16)
-        p_ref[u] = probs_low
-        out = dot32(probs_low, listed[:, start:])
-        att_ref[mine] = fold(out, v_masks).astype(bf16)
-        row = lax.broadcasted_iota(jnp.int32, row_top.shape, 0) % BLOCK
-        seen = jnp.where(row < query_ref[block], row_top, neg_large)
-        for h in range(heads):
-            best = jnp.max(seen[BLOCK * h : BLOCK * (h + 1)], axis=0, keepdims=True)
-            top_ref[h : h + 1, :] = jnp.maximum(top_ref[h : h + 1, :], best)
+
+    def step(i, carry):
+        for u in range(group):
+            block = i * group + u
+            mine = pl.ds(pl.multiple_of(block * BLOCK, BLOCK), BLOCK)
+            q_all = spread(q_ref[mine, :] * scale, q_masks)
+            listed = listed_rows(addr_ref, kv_ref, block)
+            scores = dot32(q_all, listed[:, :wide], ((1,), (1,)))
+            limit = jnp.zeros((1, LIST * BLOCK), jnp.int32)
+            for e in range(LIST):
+                limit = jnp.where(lane // BLOCK == e, valid_ref[block * LIST + e], limit)
+            scores = jnp.where(lane % BLOCK < limit, scores, neg_large)
+            row_top = jnp.max(scores, axis=1, keepdims=True)
+            shifted = jnp.exp(scores - row_top)
+            probs = shifted * (1.0 / jnp.sum(shifted, axis=1, keepdims=True))
+            probs_low = probs.astype(bf16)
+            p_ref[block] = probs_low
+            out = dot32(probs_low, listed[:, start:])
+            att_ref[mine, :] = fold(out, v_masks).astype(bf16)
+            row = lax.broadcasted_iota(jnp.int32, row_top.shape, 0) % BLOCK
+            seen = jnp.where(row < query_ref[block], row_top, neg_large)
+            for h in range(heads):
+                best = jnp.max(seen[BLOCK * h : BLOCK * (h + 1)], axis=0, keepdims=True)
+                top_ref[h : h + 1, :] = jnp.maximum(top_ref[h : h + 1, :], best)
+        return carry
+
+    lax.fori_loop(0, q_ref.shape[0] // (group * BLOCK), step, 0)
 
 
 def attention_forward(queries, kv_all, addr, valid, query_valid, heads, group=2):
@@ -989,17 +927,8 @@
     cols = LIST * BLOCK
     return pl.pallas_call(
         functools.partial(fwd_kernel, heads=heads, group=group),
-        grid_spec=pltpu.PrefetchScalarGridSpec(
-            num_scalar_prefetch=3,
-            grid=(blocks // group,),
-            in_specs=[pl.BlockSpec((group * BLOCK, wide), lambda i, *_: (i, 0)), in_place()],
-            out_specs=[
-                pl.BlockSpec((group * BLOCK, wide), lambda i, *_: (i, 0)),
-                pl.BlockSpec((group, rows, cols), lambda i, *_: (i, 0, 0)),
-                whole_block((8, 128)),
-            ],
-            scratch_shapes=[pltpu.VMEM(kv_all.shape, bf16), pltpu.SemaphoreType.DMA],
-        ),
+        in_specs=[scalars()] * 3 + [direct()] * 2,
+        out_specs=[direct()] * 3,
         out_shape=(
             jax.ShapeDtypeStruct((tokens, wide), bf16),
             jax.ShapeDtypeStruct((blocks, rows, cols), bf16),
@@ -1011,63 +940,56 @@
             2 * (kv_all.size + 2 * queries.size + blocks * rows * cols),
             blocks * rows * cols,
         ),
-        name="attention_forward",
+        name="afwd",
     )(addr, valid, query_valid, queries, kv_all)
 
 
-def bwd_kernel(addr_ref, q_ref, p_ref, w_ref, kv_src, *refs, heads, group):
+def bwd_kernel(addr_ref, q_ref, p_ref, w_ref, kv_ref, *refs, heads, group):
     pieces = refs[:4]
-    dq_ref, dkv_ref, sums_ref, db_ref, kv_ref, acc_ref, sem, piece_sem = refs[4:]
-    i = pl.program_id(0)
+    dq_ref, dkv_ref, sums_ref, db_ref, acc_ref = refs[4:]
     wide = q_ref.shape[1]
     start = kv_ref.shape[1] - wide
-
-    @pl.when(i == 0)
-    def _():
-        rows = pieces[0].shape[0]
-        loads = [
-            copy_in(ref, db_ref.at[pl.ds(r * rows, rows)], piece_sem.at[r])
-            for r, ref in enumerate(pieces)
-        ]
-        loads.append(copy_in(kv_src, kv_ref, sem))
-        acc_ref[...] = jnp.zeros(acc_ref.shape, f32)
-        sums_ref[...] = jnp.zeros(sums_ref.shape, f32)
-        for load in loads:
-            load.wait()
-
+    rows = pieces[0].shape[0]
+    for r, piece in enumerate(pieces):
+        db_ref[r * rows : (r + 1) * rows, :] = piece[...]
+    acc_ref[...] = jnp.zeros(acc_ref.shape, f32)
+    sums_ref[...] = jnp.zeros(sums_ref.shape, f32)
     scale = jnp.asarray(HEAD ** (-0.5), bf16)
     q_masks = head_masks(wide, heads, 0)
     v_masks = head_masks(wide, heads, (heads * HEAD - start) // HEAD)
-    span = group * BLOCK
-    d_branch = db_ref[pl.ds(pl.multiple_of(i * span, span), span), :]
-    d_out = dot32(d_branch, w_ref[...], ((1,), (1,))).astype(bf16)
-    for u in range(group):
-        block = i * group + u
-        mine = slice(u * BLOCK, (u + 1) * BLOCK)
-        q_all = spread(q_ref[mine] * scale, q_masks)
-        do_all = spread(d_out[mine], v_masks)
-        listed = listed_rows(addr_ref, kv_ref, block)
-        probs_low = p_ref[u]
-        probs = probs_low.astype(f32)
-        d_probs = dot32(do_all, listed[:, start:], ((1,), (1,)))
-        delta = jnp.sum(probs * d_probs, axis=1, keepdims=True)
-        d_scores = (probs * (d_probs - delta)).astype(bf16)
-        d_query = (fold(dot32(d_scores, listed[:, :wide]), q_masks) * HEAD ** (-0.5)).astype(bf16)
-        dq_ref[mine] = d_query
-        sums_ref[0:1, :] += column_sum(d_query.astype(f32))
-        d_key = dot32(d_scores, q_all, ((0,), (0,)))
-        d_value = dot32(probs_low, do_all, ((0,), (0,)))
-        sums_ref[1:2, :] += column_sum(d_value)
-        for e in range(LIST):
-            rows = pl.ds(pl.multiple_of(addr_ref[block * LIST + e] * BLOCK, BLOCK), BLOCK)
-            part = slice(BLOCK * e, BLOCK * (e + 1))
-            acc_ref[rows, :start] += d_key[part, :start]
-            acc_ref[rows, start:wide] += d_key[part, start:] + d_value[part, : wide - start]
-            acc_ref[rows, wide:] += d_value[part, wide - start :]
-
-    @pl.when(i == pl.num_programs(0) - 1)
-    def _():
-        dkv_ref[...] = acc_ref[...].astype(bf16)
+
+    def step(i, carry):
+        span = group * BLOCK
+        d_branch = db_ref[pl.ds(pl.multiple_of(i * span, span), span), :]
+        d_out = dot32(d_branch, w_ref[...], ((1,), (1,))).astype(bf16)
+        for u in range(group):
+            block = i * group + u
+            here = slice(u * BLOCK, (u + 1) * BLOCK)
+            mine = pl.ds(pl.multiple_of(block * BLOCK, BLOCK), BLOCK)
+            q_all = spread(q_ref[mine, :] * scale, q_masks)
+            do_all = spread(d_out[here], v_masks)
+            listed = listed_rows(addr_ref, kv_ref, block)
+            probs_low = p_ref[block]
+            probs = probs_low.astype(f32)
+            d_probs = dot32(do_all, listed[:, start:], ((1,), (1,)))
+            delta = jnp.sum(probs * d_probs, axis=1, keepdims=True)
+            d_scores = (probs * (d_probs - delta)).astype(bf16)
+            d_query = (fold(dot32(d_scores, listed[:, :wide]), q_masks) * HEAD ** (-0.5)).astype(bf16)
+            dq_ref[mine, :] = d_query
+            sums_ref[0:1, :] += column_sum(d_query.astype(f32))
+            d_key = dot32(d_scores, q_all, ((0,), (0,)))
+            d_value = dot32(probs_low, do_all, ((0,), (0,)))
+            sums_ref[1:2, :] += column_sum(d_value)
+            for e in range(LIST):
+                rows = pl.ds(pl.multiple_of(addr_ref[block * LIST + e] * BLOCK, BLOCK), BLOCK)
+                part = slice(BLOCK * e, BLOCK * (e + 1))
+                acc_ref[rows, :start] += d_key[part, :start]
+                acc_ref[rows, start:wide] += d_key[part, start:] + d_value[part, : wide - start]
+                acc_ref[rows, wide:] += d_value[part, wide - start :]
+        return carry
+
+    lax.fori_loop(0, q_ref.shape[0] // (group * BLOCK), step, 0)
+    dkv_ref[...] = acc_ref[...].astype(bf16)
 
 
 def attention_backward(queries, pieces, w_out, probs, kv_all, addr, heads, group=2):
@@ -1077,28 +999,9 @@
     cols = LIST * BLOCK
     return pl.pallas_call(
         functools.partial(bwd_kernel, heads=heads, group=group),
-        grid_spec=pltpu.PrefetchScalarGridSpec(
-            num_scalar_prefetch=1,
-            grid=(blocks // group,),
-            in_specs=[
-                pl.BlockSpec((group * BLOCK, wide), lambda i, *_: (i, 0)),
-                pl.BlockSpec((group, rows, cols), lambda i, *_: (i, 0, 0)),
-                whole_block(w_out.shape),
-            ]
-            + [in_place()] * 5,
-            out_specs=[
-                pl.BlockSpec((group * BLOCK, wide), lambda i, *_: (i, 0)),
-                whole_block(kv_all.shape, single=True),
-                whole_block((8, wide)),
-                whole_block((tokens, D), single=True),
-            ],
-            scratch_shapes=[
-                pltpu.VMEM(kv_all.shape, bf16),
-                pltpu.VMEM(kv_all.shape, f32),
-                pltpu.SemaphoreType.DMA,
-                pltpu.SemaphoreType.DMA((4,)),
-            ],
-        ),
+        in_specs=[scalars()] + [direct()] * 8,
+        out_specs=[direct()] * 4,
+        scratch_shapes=[pltpu.VMEM(kv_all.shape, f32)],
         out_shape=(
             jax.ShapeDtypeStruct((tokens, wide), bf16),
             jax.ShapeDtypeStruct(kv_all.shape, bf16),
@@ -1110,7 +1013,7 @@
             8 * blocks * rows * cols * wide,
             2 * (2 * kv_all.size + 3 * queries.size + blocks * rows * cols),
         ),
-        name="attention_backward",
+        name="abwd",
     )(addr, queries, probs, w_out, kv_all, *pieces)
 
 
@@ -1209,18 +1112,24 @@
     return [(d, (3 * d + slot) % WIDE) for d in range(WIDE)]
 
 
-def spread_group(held):
-    count = lax.axis_size("ctx")
-    near = jnp.stack([held] + [shift_ctx(held, step) for step in range(1, count)], axis=0)
-    far = [shift_shard(near, u) for u in range(1, lax.axis_size("shard"))]
+def spread_group(held, group):
+    count = lax.axis_size(CTX)
+    pieces = [held] + [None] * (count - 1)
+    for step in near_first(count):
+        if count == 4 and step == 2 and group:
+            pieces[2] = forward_two(pieces[1], pieces[3])
+        else:
+            pieces[step] = shift_ctx(held, step)
+    near = jnp.stack(pieces, axis=0)
+    far = [shift_shard(near, u) for u in range(1, lax.axis_size(SHARD))]
     return near, far[0] if len(far) == 1 else jnp.concatenate(far, axis=0)
 
 
 def reduce_group(near, far):
-    count = lax.axis_size("ctx")
+    count = lax.axis_size(CTX)
     back = [
         shift_shard(far[count * (u - 1) : count * u], u)
-        for u in range(1, lax.axis_size("shard"))
+        for u in range(1, lax.axis_size(SHARD))
     ]
     halves = []
     for step in range(count):
@@ -1253,10 +1162,10 @@
     right_roots,
     cotangent,
 ):
-    tensor_count = lax.axis_size("tp")
+    tensor_count = lax.axis_size(TP)
     owner_count = lax.axis_size(OWN)
-    ctx_count = lax.axis_size("ctx")
-    shard_count = lax.axis_size("shard")
+    ctx_count = lax.axis_size(CTX)
+    shard_count = lax.axis_size(SHARD)
     heads_here = HEADS // tensor_count
     cols = heads_here * HEAD
     wide = 256
@@ -1266,9 +1175,9 @@
     rows_blocks = tokens // BLOCK
     blocks_here = master_blocks.shape[0]
     packed = owner_count == WIDE and blocks_here == 3 * WIDE
-    me = lax.axis_index("tp")
-    z = lax.axis_index("ctx")
-    y = lax.axis_index("shard")
+    me = lax.axis_index(TP)
+    z = lax.axis_index(CTX)
+    y = lax.axis_index(SHARD)
     owner = lax.axis_index(OWN)
     ids = jnp.stack([me, y, z, owner]).astype(jnp.int32)
     addr, valid, query_valid, turns = index_tables(
@@ -1294,8 +1203,8 @@
             for slot in range(3)
         ]
         held_first, held_rest = sort_held(turns, held)
-        first_near, first_far = spread_group(held_first)
-        rest_near, rest_far = spread_group(held_rest)
+        first_near, first_far = spread_group(held_first, 0)
+        rest_near, rest_far = spread_group(held_rest, 1)
     else:
         weights = pack_rows(lax.all_gather(master_blocks.astype(bf16), OWN, axis=0, tiled=True))
         weights = weights.reshape(3, WIDE, PB, D)
@@ -1311,8 +1220,11 @@
     )
     moved = []
     for n, step in enumerate(near_first(ctx_count)):
-        source = own_in if n < 2 else after(own_in, moved[n - 2])
-        moved.append(shift_ctx(source, step))
+        if ctx_count == 4 and n == 2:
+            moved.append(forward_two(moved[0], moved[1]))
+        else:
+            source = own_in if n < 2 else after(own_in, moved[n - 2])
+            moved.append(shift_ctx(source, step))
         pieces = gather_quarters(moved[n])
         in_all, kv_all = project_chunk(
             ids, pieces, step, ctx_count, w_kv, kv_bias, None, None, (in_all, kv_all)
@@ -1358,21 +1270,22 @@
     )
 
     total = d_hidden
-    order = near_first(ctx_count)[::-1] + [0]
-    half = len(order) // 2
     d_kv_late = d_kv
-    for steps in (order[:half], order[half:]):
-        keep, send = dx_part(d_kv, w_kv, steps, tokens, d_query, w_q)
+    extra = {}
+    for step in near_first(ctx_count)[::-1] + [0]:
+        keep, send = dx_part(d_kv, w_kv, [step], tokens, d_query, w_q)
         sent = swap(send, 1)
-        keep = keep.reshape(len(steps), 2, quarter, D)
-        sent = sent.reshape(len(steps), 2, quarter, D)
-        across = (keep[:, 1].astype(f32) + sent[:, 1].astype(f32)).astype(bf16)
+        across = (keep[quarter:].astype(f32) + sent[quarter:].astype(f32)).astype(bf16)
         across = swap(across, 2)
-        for c, step in enumerate(steps):
-            mine = keep[c, 0].astype(f32) + sent[c, 0].astype(f32) + across[c].astype(f32)
-            if step:
-                mine = shift_ctx(mine.astype(bf16), ctx_count - step).astype(f32)
-            total = total + mine
+        mine = keep[:quarter].astype(f32) + sent[:quarter].astype(f32) + across.astype(f32)
+        if step in extra:
+            mine = mine + extra[step].astype(f32)
+        if step == 2 and ctx_count == 4:
+            extra[3], extra[1] = back_two(mine.astype(bf16))
+            continue
+        if step:
+            mine = shift_ctx(mine.astype(bf16), ctx_count - step).astype(f32)
+        total = total + mine
     grad_quarters = gather_quarters(total.astype(bf16))
 
     near_rows, far_rows = late_grads(
@@ -1466,31 +1379,31 @@
         per_device,
         mesh=mesh,
         in_specs=(
-            P("shard", "ctx", None),
-            P("shard"),
-            P("shard", None),
-            P("shard", "ctx", None),
-            P(("shard", "ctx", "tp"), None, None),
+            P(SHARD, CTX, None),
+            P(SHARD),
+            P(SHARD, None),
+            P(SHARD, CTX, None),
+            P((SHARD, CTX, TP), None, None),
             P(),
-            P("tp", None),
-            P(("shard", "ctx", "tp"), None, None),
-            P(("shard", "ctx", "tp"), None, None),
-            P(("shard", "ctx", "tp"), None, None),
-            P(("shard", "ctx", "tp"), None, None),
-            P("shard", "ctx", None),
+            P(TP, None),
+            P((SHARD, CTX, TP), None, None),
+            P((SHARD, CTX, TP), None, None),
+            P((SHARD, CTX, TP), None, None),
+            P((SHARD, CTX, TP), None, None),
+            P(SHARD, CTX, None),
         ),
         out_specs=(
-            P("shard", "ctx", None),
-            P("shard", "ctx", None),
-            P(("shard", "ctx", "tp"), None, None),
-            P(None, ("shard", "ctx")),
-            P("tp", ("shard", "ctx")),
-            P("tp"),
-            P(("shard", "ctx", "tp"), None, None),
-            P(("shard", "ctx", "tp"), None, None),
-            P(("shard", "ctx", "tp"), None, None),
-            P(None, ("shard", "ctx")),
-            P("tp", ("shard", "ctx")),
+            P(SHARD, CTX, None),
+            P(SHARD, CTX, None),
+            P((SHARD, CTX, TP), None, None),
+            P(None, (SHARD, CTX)),
+            P(TP, (SHARD, CTX)),
+            P(TP),
+            P((SHARD, CTX, TP), None, None),
+            P((SHARD, CTX, TP), None, None),
+            P((SHARD, CTX, TP), None, None),
+            P(None, (SHARD, CTX)),
+            P(TP, (SHARD, CTX)),
         ),
         check_vma=False,
     )

time: 406 us -> 343 us (0.84)
  waiting for transfers between devices: 176 us -> 135 us
  Pallas kernels: 93.4 us -> 78 us
  local copies, waits for them, and re-layouts: 19.8 us -> 8.4 us
  starting transfers between devices: 95.3 us -> 102 us
    ppermute x64 -> x71, waiting for transfers between devices: 167 us -> 116 us  [the longest x42 72.8 us: swap(): return lax.ppermute(rows, TP, [(i, i ^ mask) for i in range(count)])]
    pallas_call x10, Pallas kernels: 49.5 us -> 36.5 us  [the longest x1 13.2 us: attention_backward(): pl.pallas_call(functools.partial(bwd_kernel, heads=heads, group=group), i...]
    unnamed x96 -> x64, local copies, waits for them, and re-layouts: 18.4 us -> 7.04 us
    ppermute x6, waiting for transfers between devices: 9.62 us -> 18.8 us  [owner_move(): return lax.ppermute(rows, OWN, pairs)]
    ppermute x64 -> x71, starting transfers between devices: 82.6 us -> 86.3 us  [the longest x42 48.7 us: swap(): return lax.ppermute(rows, TP, [(i, i ^ mask) for i in range(count)])]
    pallas_call x2 -> x4, Pallas kernels: 11.1 us -> 8.45 us  [dx_part(): pl.pallas_call(functools.partial(dx_kernel, with_q=with_q), grid=(4 * cou...]
  transfers between devices with their start and end apart: 70 -> 77, of which waited for: 30 -> 30; matrix products, arithmetic and copies ran while one was open for 3% -> 4% of each run, Pallas kernels for 14% -> 21%
where the time goes in v2:
time: 343 us; the launch traced here: 341 us
  waiting for transfers between devices  135 us (39%)
  starting transfers between devices  102 us (30%)
  Pallas kernels  78 us (23%)
  other arithmetic  12.7 us (4%)
  local copies, waits for them, and re-layouts  8.4 us (2%)
  between operations  4.51 us (1%)
    ppermute x42, waiting for transfers between devices, swap(): return lax.ppermute(rows, TP, [(i, i ^ mask) for i in range(count)])  72.8 us
    ppermute x42, starting transfers between devices, swap(): return lax.ppermute(rows, TP, [(i, i ^ mask) for i in range(count)])  48.7 us
    ppermute x18, waiting for transfers between devices, shift_ctx(): lax.ppermute(rows, CTX, [(i, (i + step) % count) for i in range(count)])  22.4 us
    ppermute x18, starting transfers between devices, shift_ctx(): lax.ppermute(rows, CTX, [(i, (i + step) % count) for i in range(count)])  19.2 us
    ppermute x6, waiting for transfers between devices, owner_move(): return lax.ppermute(rows, OWN, pairs)  18.8 us
    ppermute x6, starting transfers between devices, owner_move(): return lax.ppermute(rows, OWN, pairs)  15.5 us
    pallas_call x1, Pallas kernels, attention_backward(): pl.pallas_call(functools.partial(bwd_kernel, heads=heads, group=group), i...  13.2 us
    ppermute x2, waiting for transfers between devices, forward_two(): left = lax.ppermute(from_right, CTX, [(1, 0), (2, 1)])  11 us
  transfers between devices with their start and end apart: 77, of which 30 were waited for; matrix products, arithmetic and copies ran while one was open for 4% of the time, Pallas kernels for 21%

profile of v2, /device:TPU:9, one launch (start us, length us, event | category | flops | bytes accessed | tf_op | source)
XLA Modules:
  0.0 340.7 jit_solution(129435162024223783)
XLA Ops:
  17.0 12.7 %collective-permute-done.1.b_ref = bf16[96,768]{1,0:T(8,128)(2,1)S(1)} collective-permute-done((bf16[96,768]{1,0:T(8,128)(2,1)S(1)}, bf16[96,768]{1,0:T(8,128)(2,1)S(1)}, u32[]{:S(2)}, u32[]{:S(2)}) %collective-permute-start.1) | collective-permute-done | bytes 147488 | tf_op jit(solution)/shard_map/ppermute | solution.py:119
  46.1 6.1 %collective-permute-done.10 = bf16[256,768]{1,0:T(8,128)(2,1)S(1)} collective-permute-done((bf16[256,768]{1,0:T(8,128)(2,1)S(1)}, bf16[256,768]{1,0:T(8,128)(2,1)S(1)}, u32[]{:S(2)}, u32[]{:S(2)}) %collective-permute-start.10) | collective-permute-done | bytes 393248 | tf_op jit(solution)/shard_map/ppermute | solution.py:103
  58.4 3.6 %collective-permute-done.15.refs_2_ = bf16[256,768]{1,0:T(8,128)(2,1)S(1)} collective-permute-done((bf16[256,768]{1,0:T(8,128)(2,1)S(1)}, bf16[256,768]{1,0:T(8,128)(2,1)S(1)}, u32[]{:S(2)}, u32[]{:S(2)}) %collective-permute-start.15) | collective-permute-done | bytes 393248 | tf_op jit(solution)/shard_map/ppermute | solution.py:93
  62.0 4.8 %collective-permute-start.14 = (bf16[256,768]{1,0:T(8,128)(2,1)S(1)}, bf16[256,768]{1,0:T(8,128)(2,1)S(1)}, u32[]{:S(2)}, u32[]{:S(2)}) collective-permute-start(bf16[256,768]{1,0:T(8,128)(2,1)S(1)} %collective-permute-done.9.refs_0_), channel_id=1, source_target_pairs={{0,1},{1,0},{2,3},{3,2},{4,5},{5,4},{6,7},{7,6},{8,9},{9,8},{10,11... | collective-permute-start | bytes 1179656 | tf_op jit(solution)/shard_map/ppermute | solution.py:93
  82.9 6.6 %afwd.1 = (bf16[1024,256]{1,0:T(8,128)(2,1)S(1)}, bf16[16,192,512]{2,1,0:T(8,128)(2,1)S(1)}, f32[8,128]{1,0:T(8,128)S(1)}) custom-call(s32[128]{0:T(128)S(1)} %get-tuple-element.101.addr_ref, s32[128]{0:T(128)S(1)} %get-tuple-element.102.valid_ref, s32[16]{0:T(128)S(1)} %get-tuple-element.103.query_ref, bf16[1024,256]{1,0:T(8,128)(2,1)S(1)} %get-tuple-element.108.q_ref, ...), custom_call_target="tpu_custom_call" | custom-call | flops 1610612736 | bytes 7340032 | tf_op jit(solution)/shard_map/afwd/pallas_call | solution.py:928
  96.5 4.9 %collective-permute-done.26 = bf16[192,768]{1,0:T(8,128)(2,1)S(1)} collective-permute-done((bf16[192,768]{1,0:T(8,128)(2,1)S(1)}, bf16[192,768]{1,0:T(8,128)(2,1)S(1)}, u32[]{:S(2)}, u32[]{:S(2)}) %collective-permute-start.26) | collective-permute-done | bytes 294944 | tf_op jit(solution)/shard_map/ppermute | solution.py:103
  105.2 6.6 %collective-permute-done.21.got_ref = bf16[256,768]{1,0:T(8,128)(2,1)S(1)} collective-permute-done((bf16[256,768]{1,0:T(8,128)(2,1)S(1)}, bf16[256,768]{1,0:T(8,128)(2,1)S(1)}, u32[]{:S(2)}, u32[]{:S(2)}) %collective-permute-start.21) | collective-permute-done | bytes 393248 | tf_op jit(solution)/shard_map/ppermute | solution.py:93
  114.8 7.3 %collective-permute-done.29.xa_ref = bf16[256,768]{1,0:T(8,128)(2,1)S(1)} collective-permute-done((bf16[256,768]{1,0:T(8,128)(2,1)S(1)}, bf16[256,768]{1,0:T(8,128)(2,1)S(1)}, u32[]{:S(2)}, u32[]{:S(2)}) %collective-permute-start.29) | collective-permute-done | bytes 393248 | tf_op jit(solution)/shard_map/ppermute | solution.py:93
  125.1 4.7 %collective-permute-done.27.far_ref = bf16[4,192,768]{2,1,0:T(8,128)(2,1)S(1)} collective-permute-done((bf16[4,192,768]{2,1,0:T(8,128)(2,1)S(1)}, bf16[4,192,768]{2,1,0:T(8,128)(2,1)S(1)}, u32[]{:S(2)}, u32[]{:S(2)}) %collective-permute-start.27) | collective-permute-done | bytes 1179680 | tf_op jit(solution)/shard_map/ppermute | solution.py:115
  139.8 9.4 %collective-permute-done.32.got_ref = bf16[256,768]{1,0:T(8,128)(2,1)S(1)} collective-permute-done((bf16[256,768]{1,0:T(8,128)(2,1)S(1)}, bf16[256,768]{1,0:T(8,128)(2,1)S(1)}, u32[]{:S(2)}, u32[]{:S(2)}) %collective-permute-start.32) | collective-permute-done | bytes 393248 | tf_op jit(solution)/shard_map/ppermute | solution.py:93
  152.4 9.5 %collective-permute-done.35.da_ref = bf16[256,768]{1,0:T(8,128)(2,1)S(1)} collective-permute-done((bf16[256,768]{1,0:T(8,128)(2,1)S(1)}, bf16[256,768]{1,0:T(8,128)(2,1)S(1)}, u32[]{:S(2)}, u32[]{:S(2)}) %collective-permute-start.35) | collective-permute-done | bytes 393248 | tf_op jit(solution)/shard_map/ppermute | solution.py:93
  172.9 8.9 %collective-permute-done.38.got_ref = bf16[256,768]{1,0:T(8,128)(2,1)S(1)} collective-permute-done((bf16[256,768]{1,0:T(8,128)(2,1)S(1)}, bf16[256,768]{1,0:T(8,128)(2,1)S(1)}, u32[]{:S(2)}, u32[]{:S(2)}) %collective-permute-start.38) | collective-permute-done | bytes 393248 | tf_op jit(solution)/shard_map/ppermute | solution.py:93
  185.8 7.7 %collective-permute-done.39.refs_2_ = bf16[256,768]{1,0:T(8,128)(2,1)S(1)} collective-permute-done((bf16[256,768]{1,0:T(8,128)(2,1)S(1)}, bf16[256,768]{1,0:T(8,128)(2,1)S(1)}, u32[]{:S(2)}, u32[]{:S(2)}) %collective-permute-start.39) | collective-permute-done | bytes 393248 | tf_op jit(solution)/shard_map/ppermute | solution.py:93
  203.6 13.2 %abwd.1 = (bf16[1024,256]{1,0:T(8,128)(2,1)S(1)}, bf16[4096,384]{1,0:T(8,128)(2,1)S(1)}, f32[8,256]{1,0:T(8,128)S(1)}, bf16[1024,768]{1,0:T(8,128)(2,1)S(1)}) custom-call(s32[128]{0:T(128)S(1)} %get-tuple-element.101.addr_ref, bf16[1024,256]{1,0:T(8,128)(2,1)S(1)} %get-tuple-element.108.q_ref, bf16[16,192,512]{2,1,0:T(8,128)(2,1)S(1)} %get-tuple-element.142.p_ref, ...), custom_call_target="tpu_custom_call" | custom-call | flops 3221225472 | bytes 11010048 | tf_op jit(solution)/shard_map/abwd/pallas_call | solution.py:1000
  216.9 6.0 %late.1 = (bf16[4,112,768]{2,1,0:T(8,128)(2,1)S(1)}, bf16[4,112,768]{2,1,0:T(8,128)(2,1)}) custom-call(s32[32]{0:T(128)S(1)} %get-tuple-element.100.turn_ref, bf16[4096,768]{1,0:T(8,128)(2,1)S(1)} %get-tuple-element.153.x_ref, bf16[4096,384]{1,0:T(8,128)(2,1)S(1)} %get-tuple-element.143.dkv_ref, bf16[1024,256]{1,0:T(8,128)(2,1)S(1)} %get-tuple-element.150.refs_0_.dq_ref, ...), custom_call_target="tpu_custom_call" | custom-call | flops 2415919104 | bytes 9437184 | tf_op jit(solution)/shard_map/late/pallas_call | solution.py:832
  237.8 4.0 %collective-permute-done.67 = bf16[96,768]{1,0:T(8,128)(2,1)} collective-permute-done((bf16[96,768]{1,0:T(8,128)(2,1)}, bf16[96,768]{1,0:T(8,128)(2,1)}, u32[]{:S(2)}, u32[]{:S(2)}) %collective-permute-start.67) | collective-permute-done | bytes 147488 | tf_op jit(solution)/shard_map/ppermute | solution.py:98
  256.9 8.0 %collective-permute-done.48 = bf16[256,768]{1,0:T(8,128)(2,1)S(1)} collective-permute-done((bf16[256,768]{1,0:T(8,128)(2,1)S(1)}, bf16[256,768]{1,0:T(8,128)(2,1)S(1)}, u32[]{:S(2)}, u32[]{:S(2)}) %collective-permute-start.48) | collective-permute-done | bytes 393248 | tf_op jit(solution)/shard_map/ppermute | solution.py:93
  277.9 4.6 %collective-permute-done.46 = bf16[256,768]{1,0:T(8,128)(2,1)S(1)} collective-permute-done((bf16[256,768]{1,0:T(8,128)(2,1)S(1)}, bf16[256,768]{1,0:T(8,128)(2,1)S(1)}, u32[]{:S(2)}, u32[]{:S(2)}) %collective-permute-start.46) | collective-permute-done | bytes 393248 | tf_op jit(solution)/shard_map/ppermute | solution.py:93
  286.6 5.0 %collective-permute-start.75 = (f32[6,96]{1,0:T(8,128)S(1)}, f32[6,96]{1,0:T(8,128)S(1)}, u32[]{:S(2)}, u32[]{:S(2)}) collective-permute-start(f32[6,96]{1,0:T(8,128)S(1)} %slice.245), channel_id=1, source_target_pairs={{0,1},{1,0},{2,3},{3,2},{4,5},{5,4},{6,7},{7,6},{8,9},{9,8},{10,11... | collective-permute-start | bytes 6920 | tf_op jit(solution)/shard_map/ppermute | solution.py:93
  298.6 4.3 %collective-permute-done.54 = bf16[256,768]{1,0:T(8,128)(2,1)S(1)} collective-permute-done((bf16[256,768]{1,0:T(8,128)(2,1)S(1)}, bf16[256,768]{1,0:T(8,128)(2,1)S(1)}, u32[]{:S(2)}, u32[]{:S(2)}) %collective-permute-start.54) | collective-permute-done | bytes 393248 | tf_op jit(solution)/shard_map/ppermute | solution.py:98
  302.9 6.2 %collective-permute-done.50 = bf16[256,768]{1,0:T(8,128)(2,1)S(1)} collective-permute-done((bf16[256,768]{1,0:T(8,128)(2,1)S(1)}, bf16[256,768]{1,0:T(8,128)(2,1)S(1)}, u32[]{:S(2)}, u32[]{:S(2)}) %collective-permute-start.50) | collective-permute-done | bytes 393248 | tf_op jit(solution)/shard_map/ppermute | solution.py:98
  314.2 5.1 %collective-permute-start.72 = (bf16[96,768]{1,0:T(8,128)(2,1)S(1)}, bf16[96,768]{1,0:T(8,128)(2,1)S(1)}, u32[]{:S(2)}, u32[]{:S(2)}) collective-permute-start(bf16[96,768]{1,0:T(8,128)(2,1)S(1)} %get-tuple-element.181), channel_id=1, source_target_pairs={{0,0},{12,4},{24,8},{4,12},{16,16},{28,20},{8,24},{20,28},{1,1},{1... | collective-permute-start | bytes 442376 | tf_op jit(solution)/shard_map/ppermute | solution.py:119
  324.6 4.4 %collective-permute-done.74.refs_2_ = bf16[96,768]{1,0:T(8,128)(2,1)S(1)} collective-permute-done((bf16[96,768]{1,0:T(8,128)(2,1)S(1)}, bf16[96,768]{1,0:T(8,128)(2,1)S(1)}, u32[]{:S(2)}, u32[]{:S(2)}) %collective-permute-start.74) | collective-permute-done | bytes 147488 | tf_op jit(solution)/shard_map/ppermute | solution.py:119
  328.9 4.4 %shampoo.1 = (f32[24,96,96]{2,1,0:T(8,128)}, f32[24,96,96]{2,1,0:T(8,128)}, f32[24,96,96]{2,1,0:T(8,128)}, f32[24,96,96]{2,1,0:T(8,128)}, f32[8,128]{1,0:T(8,128)S(1)}) custom-call(s32[32]{0:T(128)S(1)} %get-tuple-element.100.turn_ref, bf16[96,768]{1,0:T(8,128)(2,1)S(1)} %collective-permute-done.72.refs_0_, ...), custom_call_target="tpu_custom_call" | custom-call | flops 339738624 | bytes 8847360 | tf_op jit(solution)/shard_map/shampoo/pallas_call | solution.py:1084
  (260 shorter events, 178.3 us)
Async XLA Ops:
  2.8 30.0 %collective-permute-start.9 = (bf16[256,768]{1,0:T(8,128)(2,1)S(1)}, bf16[256,768]{1,0:T(8,128)(2,1)S(1)}, u32[]{:S(2)}, u32[]{:S(2)}) collective-permute-start(bf16[256,768]{1,0:T(8,128)(2,1)S(1)} %pick.1), channel_id=1, source_target_pairs={{0,12},{4,0},{8,4},{12,8},{1,13},{5,1},{9,5},{13,9},{2,14},{6,2},{... | collective-permute-start | bytes 1179656 | tf_op jit(solution)/shard_map/ppermute | solution.py:98
  2.8 32.1 %collective-permute-start.7 = (bf16[256,768]{1,0:T(8,128)(2,1)S(1)}, bf16[256,768]{1,0:T(8,128)(2,1)S(1)}, u32[]{:S(2)}, u32[]{:S(2)}) collective-permute-start(bf16[256,768]{1,0:T(8,128)(2,1)S(1)} %pick.1), channel_id=1, source_target_pairs={{0,4},{4,8},{8,12},{12,0},{1,5},{5,9},{9,13},{13,1},{2,6},{6,10},{... | collective-permute-start | bytes 1179656 | tf_op jit(solution)/shard_map/ppermute | solution.py:98
  11.9 17.8 %collective-permute-start.1 = (bf16[96,768]{1,0:T(8,128)(2,1)S(1)}, bf16[96,768]{1,0:T(8,128)(2,1)S(1)}, u32[]{:S(2)}, u32[]{:S(2)}) collective-permute-start(bf16[96,768]{1,0:T(8,128)(2,1)S(1)} %get-tuple-element.203), channel_id=1, source_target_pairs={{0,4},{4,16},{8,28},{12,8},{16,20},{20,0},{24,12},{28,24},{1,5},{5... | collective-permute-start | bytes 442376 | tf_op jit(solution)/shard_map/ppermute | solution.py:119
  32.8 19.5 %collective-permute-start.10 = (bf16[256,768]{1,0:T(8,128)(2,1)S(1)}, bf16[256,768]{1,0:T(8,128)(2,1)S(1)}, u32[]{:S(2)}, u32[]{:S(2)}) collective-permute-start(bf16[256,768]{1,0:T(8,128)(2,1)S(1)} %collective-permute-done.9.refs_0_), channel_id=1, source_target_pairs={{4,0},{8,4},{5,1},{9,5},{6,2},{10,6},{7,3},{11,7},{20,16},{24,20},... | collective-permute-start | bytes 1179656 | tf_op jit(solution)/shard_map/ppermute | solution.py:103
  35.0 19.6 %collective-permute-start.8 = (bf16[256,768]{1,0:T(8,128)(2,1)S(1)}, bf16[256,768]{1,0:T(8,128)(2,1)S(1)}, u32[]{:S(2)}, u32[]{:S(2)}) collective-permute-start(bf16[256,768]{1,0:T(8,128)(2,1)S(1)} %collective-permute-done.7.refs_0_), channel_id=1, source_target_pairs={{4,8},{8,12},{5,9},{9,13},{6,10},{10,14},{7,11},{11,15},{20,24},{2... | collective-permute-start | bytes 1179656 | tf_op jit(solution)/shard_map/ppermute | solution.py:102
  44.4 22.4 %collective-permute-start.6 = (bf16[4,96,768]{2,1,0:T(8,128)(2,1)S(1)}, bf16[4,96,768]{2,1,0:T(8,128)(2,1)S(1)}, u32[]{:S(2)}, u32[]{:S(2)}) collective-permute-start(bf16[4,96,768]{2,1,0:T(8,128)(2,1)S(1)} %pad_maximum_fusion.1.near_ref), channel_id=1, source_target_pairs={{0,16},{16,0},{1,17},{17,1},{2,18},{18,2},{3,19},{19,3},{4,20},{20... | collective-permute-start | bytes 1769480 | tf_op jit(solution)/shard_map/ppermute | solution.py:115
  45.9 16.1 %collective-permute-start.15 = (bf16[256,768]{1,0:T(8,128)(2,1)S(1)}, bf16[256,768]{1,0:T(8,128)(2,1)S(1)}, u32[]{:S(2)}, u32[]{:S(2)}) collective-permute-start(bf16[256,768]{1,0:T(8,128)(2,1)S(1)} %collective-permute-done.9.refs_0_), channel_id=1, source_target_pairs={{0,2},{1,3},{2,0},{3,1},{4,6},{5,7},{6,4},{7,5},{8,10},{9,11},{10,... | collective-permute-start | bytes 1179656 | tf_op jit(solution)/shard_map/ppermute | solution.py:93
  56.0 20.0 %collective-permute-start.19 = (bf16[256,768]{1,0:T(8,128)(2,1)S(1)}, bf16[256,768]{1,0:T(8,128)(2,1)S(1)}, u32[]{:S(2)}, u32[]{:S(2)}) collective-permute-start(bf16[256,768]{1,0:T(8,128)(2,1)S(1)} %collective-permute-done.18.refs_2_), channel_id=1, source_target_pairs={{0,1},{1,0},{2,3},{3,2},{4,5},{5,4},{6,7},{7,6},{8,9},{9,8},{10,11... | collective-permute-start | bytes 1179656 | tf_op jit(solution)/shard_map/ppermute | solution.py:93
  62.0 17.3 %collective-permute-start.14 = (bf16[256,768]{1,0:T(8,128)(2,1)S(1)}, bf16[256,768]{1,0:T(8,128)(2,1)S(1)}, u32[]{:S(2)}, u32[]{:S(2)}) collective-permute-start(bf16[256,768]{1,0:T(8,128)(2,1)S(1)} %collective-permute-done.9.refs_0_), channel_id=1, source_target_pairs={{0,1},{1,0},{2,3},{3,2},{4,5},{5,4},{6,7},{7,6},{8,9},{9,8},{10,11... | collective-permute-start | bytes 1179656 | tf_op jit(solution)/shard_map/ppermute | solution.py:93
  103.9 25.9 %collective-permute-start.27 = (bf16[4,192,768]{2,1,0:T(8,128)(2,1)S(1)}, bf16[4,192,768]{2,1,0:T(8,128)(2,1)S(1)}, u32[]{:S(2)}, u32[]{:S(2)}) collective-permute-start(bf16[4,192,768]{2,1,0:T(8,128)(2,1)S(1)} %pad_maximum_fusion.near_ref), channel_id=1, source_target_pairs={{0,16},{16,0},{1,17},{17,1},{2,18},{18,2},{3,19},{19,3},{4,20},{20... | collective-permute-start | bytes 3538952 | tf_op jit(solution)/shard_map/ppermute | solution.py:115
  184.2 19.4 %collective-permute-start.44 = (bf16[256,768]{1,0:T(8,128)(2,1)S(1)}, bf16[256,768]{1,0:T(8,128)(2,1)S(1)}, u32[]{:S(2)}, u32[]{:S(2)}) collective-permute-start(bf16[256,768]{1,0:T(8,128)(2,1)S(1)} %get-tuple-element.139.refs_0_), channel_id=1, source_target_pairs={{0,1},{1,0},{2,3},{3,2},{4,5},{5,4},{6,7},{7,6},{8,9},{9,8},{10,11... | collective-permute-start | bytes 1179656 | tf_op jit(solution)/shard_map/ppermute | solution.py:93
  198.0 30.7 %collective-permute-start.64 = (bf16[4,96,768]{2,1,0:T(8,128)(2,1)S(1)}, bf16[4,96,768]{2,1,0:T(8,128)(2,1)S(1)}, u32[]{:S(2)}, u32[]{:S(2)}) collective-permute-start(bf16[4,96,768]{2,1,0:T(8,128)(2,1)S(1)} %get-tuple-element.168), channel_id=1, source_target_pairs={{0,16},{16,0},{1,17},{17,1},{2,18},{18,2},{3,19},{19,3},{4,20},{20... | collective-permute-start | bytes 1769480 | tf_op jit(solution)/shard_map/ppermute | solution.py:115
  203.5 34.0 %collective-permute-start.68 = (bf16[4,96,768]{2,1,0:T(8,128)(2,1)}, bf16[4,96,768]{2,1,0:T(8,128)(2,1)}, u32[]{:S(2)}, u32[]{:S(2)}) collective-permute-start(bf16[4,96,768]{2,1,0:T(8,128)(2,1)} %get-tuple-element.177), channel_id=1, source_target_pairs={{0,16},{16,0},{1,17},{17,1},{2,18},{18,2},{3,19},{19,3},{4,20},{20... | collective-permute-start | bytes 1769480 | tf_op jit(solution)/shard_map/ppermute | solution.py:115
  222.9 27.2 %collective-permute-start.60 = (bf16[4,112,768]{2,1,0:T(8,128)(2,1)}, bf16[4,112,768]{2,1,0:T(8,128)(2,1)}, u32[]{:S(2)}, u32[]{:S(2)}) collective-permute-start(bf16[4,112,768]{2,1,0:T(8,128)(2,1)} %get-tuple-element.162), channel_id=1, source_target_pairs={{0,16},{16,0},{1,17},{17,1},{2,18},{18,2},{3,19},{19,3},{4,20},{20... | collective-permute-start | bytes 2064392 | tf_op jit(solution)/shard_map/ppermute | solution.py:115
  227.9 25.0 %collective-permute-start.47 = (bf16[512,768]{1,0:T(8,128)(2,1)}, bf16[512,768]{1,0:T(8,128)(2,1)}, u32[]{:S(2)}, u32[]{:S(2)}) collective-permute-start(bf16[512,768]{1,0:T(8,128)(2,1)} %get-tuple-element.147), channel_id=1, source_target_pairs={{0,1},{1,0},{2,3},{3,2},{4,5},{5,4},{6,7},{7,6},{8,9},{9,8},{10,11... | collective-permute-start | bytes 2359304 | tf_op jit(solution)/shard_map/ppermute | solution.py:93
  250.0 16.4 %collective-permute-start.45 = (bf16[512,768]{1,0:T(8,128)(2,1)S(1)}, bf16[512,768]{1,0:T(8,128)(2,1)S(1)}, u32[]{:S(2)}, u32[]{:S(2)}) collective-permute-start(bf16[512,768]{1,0:T(8,128)(2,1)S(1)} %get-tuple-element.145), channel_id=1, source_target_pairs={{0,1},{1,0},{2,3},{3,2},{4,5},{5,4},{6,7},{7,6},{8,9},{9,8},{10,11... | collective-permute-start | bytes 2359304 | tf_op jit(solution)/shard_map/ppermute | solution.py:93
  251.4 16.4 %collective-permute-start.61 = (bf16[112,768]{1,0:T(8,128)(2,1)S(1)}, bf16[112,768]{1,0:T(8,128)(2,1)S(1)}, u32[]{:S(2)}, u32[]{:S(2)}) collective-permute-start(bf16[112,768]{1,0:T(8,128)(2,1)S(1)} %get-tuple-element.193), channel_id=1, source_target_pairs={{0,4},{4,8},{8,12},{12,0},{1,5},{5,9},{9,13},{13,1},{2,6},{6,10},{... | collective-permute-start | bytes 516104 | tf_op jit(solution)/shard_map/ppermute | solution.py:98
  252.9 16.8 %collective-permute-start.63 = (bf16[112,768]{1,0:T(8,128)(2,1)S(1)}, bf16[112,768]{1,0:T(8,128)(2,1)S(1)}, u32[]{:S(2)}, u32[]{:S(2)}) collective-permute-start(bf16[112,768]{1,0:T(8,128)(2,1)S(1)} %get-tuple-element.194), channel_id=1, source_target_pairs={{0,8},{4,12},{8,0},{12,4},{1,9},{5,13},{9,1},{13,5},{2,10},{6,14},... | collective-permute-start | bytes 516104 | tf_op jit(solution)/shard_map/ppermute | solution.py:98
  267.8 18.8 %collective-permute-start.71 = (bf16[96,768]{1,0:T(8,128)(2,1)S(1)}, bf16[96,768]{1,0:T(8,128)(2,1)S(1)}, u32[]{:S(2)}, u32[]{:S(2)}) collective-permute-start(bf16[96,768]{1,0:T(8,128)(2,1)S(1)} %get-tuple-element.196), channel_id=1, source_target_pairs={{0,8},{4,12},{8,0},{12,4},{1,9},{5,13},{9,1},{13,5},{2,10},{6,14},... | collective-permute-start | bytes 442376 | tf_op jit(solution)/shard_map/ppermute | solution.py:98
  274.2 17.4 %collective-permute-start.70 = (bf16[96,768]{1,0:T(8,128)(2,1)S(1)}, bf16[96,768]{1,0:T(8,128)(2,1)S(1)}, u32[]{:S(2)}, u32[]{:S(2)}) collective-permute-start(bf16[96,768]{1,0:T(8,128)(2,1)S(1)} %get-tuple-element.197), channel_id=1, source_target_pairs={{0,12},{4,0},{8,4},{12,8},{1,13},{5,1},{9,5},{13,9},{2,14},{6,2},{... | collective-permute-start | bytes 442376 | tf_op jit(solution)/shard_map/ppermute | solution.py:98
  292.1 17.0 %collective-permute-start.50 = (bf16[256,768]{1,0:T(8,128)(2,1)S(1)}, bf16[256,768]{1,0:T(8,128)(2,1)S(1)}, u32[]{:S(2)}, u32[]{:S(2)}) collective-permute-start(bf16[256,768]{1,0:T(8,128)(2,1)S(1)} %add_convert_fusion.4), channel_id=1, source_target_pairs={{0,4},{4,8},{8,12},{12,0},{1,5},{5,9},{9,13},{13,1},{2,6},{6,10},{... | collective-permute-start | bytes 1179656 | tf_op jit(solution)/shard_map/ppermute | solution.py:98
  295.0 16.7 %collective-permute-start.41 = (bf16[256,768]{1,0:T(8,128)(2,1)S(1)}, bf16[256,768]{1,0:T(8,128)(2,1)S(1)}, u32[]{:S(2)}, u32[]{:S(2)}) collective-permute-start(bf16[256,768]{1,0:T(8,128)(2,1)S(1)} %copy-done.24), channel_id=1, source_target_pairs={{0,1},{1,0},{2,3},{3,2},{4,5},{5,4},{6,7},{7,6},{8,9},{9,8},{10,11... | collective-permute-start | bytes 1179656 | tf_op jit(solution)/shard_map/ppermute | solution.py:93
  298.3 23.2 %collective-permute-start.76 = (f32[6,96]{1,0:T(8,128)S(1)}, f32[6,96]{1,0:T(8,128)S(1)}, u32[]{:S(2)}, u32[]{:S(2)}) collective-permute-start(f32[6,96]{1,0:T(8,128)S(1)} %slice_add_fusion), channel_id=1, source_target_pairs={{0,2},{1,3},{2,0},{3,1},{4,6},{5,7},{6,4},{7,5},{8,10},{9,11},{10,... | collective-permute-start | bytes 6920 | tf_op jit(solution)/shard_map/ppermute | solution.py:93
  309.4 27.4 %collective-permute-start.58 = (bf16[256,768]{1,0:T(8,128)(2,1)S(1)}, bf16[256,768]{1,0:T(8,128)(2,1)S(1)}, u32[]{:S(2)}, u32[]{:S(2)}) collective-permute-start(bf16[256,768]{1,0:T(8,128)(2,1)S(1)} %add_convert_fusion.refs_0_), channel_id=1, source_target_pairs={{0,2},{1,3},{2,0},{3,1},{4,6},{5,7},{6,4},{7,5},{8,10},{9,11},{10,... | collective-permute-start | bytes 1179656 | tf_op jit(solution)/shard_map/ppermute | solution.py:93
  (85 other events, 951.6 us)

commit v3 on v2

--- a/solution.py
+++ b/solution.py
@@ -313,28 +313,50 @@
     )(turns, *held)
 
 
-def deal_kernel(turn_ref, first_ref, up_ref, down_ref, a_ref, b_ref, c_ref):
-    groups = (first_ref[:PB].astype(bf16), up_ref[...].astype(bf16), down_ref[...].astype(bf16))
-    for slot, out_ref in enumerate((a_ref, b_ref, c_ref)):
+def deal_kernel(turn_ref, *refs, parts, heads):
+    outs = refs[sum(parts) :]
+    groups = []
+    for group in range(3):
+        base = sum(parts[:group])
+        total = refs[base][...]
+        for part in refs[base + 1 : base + parts[group]]:
+            total = total + part[...].astype(f32)
+        groups.append(total)
+    rows = [total[:PB].astype(bf16) for total in groups]
+    for slot in range(3):
         target = lax.rem(3 * (turn_ref[3 * WIDE] + WIDE - slot), WIDE)
         group = lax.div(3 * target + slot, WIDE)
-        out_ref[...] = jnp.where(group == 0, groups[0], jnp.where(group == 1, groups[1], groups[2]))
-
-
-def deal_rows(turns, first, up, down):
-    one = whole_block((PB, D))
-    return pl.pallas_call(
-        deal_kernel,
-        grid_spec=pltpu.PrefetchScalarGridSpec(
-            num_scalar_prefetch=1,
-            grid=(1,),
-            in_specs=[whole_block(first.shape), one, one],
-            out_specs=[one] * 3,
-        ),
-        out_shape=[jax.ShapeDtypeStruct((PB, D), bf16)] * 3,
-        compiler_params=params_of(6),
+        outs[slot][...] = jnp.where(group == 0, rows[0], jnp.where(group == 1, rows[1], rows[2]))
+    outs[3][...] = groups[0][PB:]
+    slots = groups[0][PB : PB + 8, :128]
+    lanes = slots.shape[1]
+    slots = slots + pltpu.roll(slots, lanes - heads, 1) + pltpu.roll(slots, lanes - 2 * heads, 1)
+    lane = lax.broadcasted_iota(jnp.int32, slots.shape, 1)
+    row = lax.broadcasted_iota(jnp.int32, slots.shape, 0)
+    largest = jnp.zeros(slots.shape, f32)
+    for h in range(heads):
+        chosen = (row == 7) & (lane % (3 * heads) == h) & (lane < 3 * heads * WIDE)
+        best = jnp.max(jnp.where(chosen, slots, neg_large), axis=1, keepdims=True)
+        largest = jnp.where(lane == h, jnp.max(best, axis=0, keepdims=True), largest)
+    outs[4][...] = largest
+
+
+def deal_rows(turns, first, up, down, heads):
+    args = [*first, *up, *down]
+    one = jax.ShapeDtypeStruct((PB, D), bf16)
+    under = first[0].shape[0] - PB
+    shapes = [one] * 3 + [
+        jax.ShapeDtypeStruct((under, D), f32),
+        jax.ShapeDtypeStruct((8, 128), f32),
+    ]
+    return pl.pallas_call(
+        functools.partial(deal_kernel, parts=(len(first), len(up), len(down)), heads=heads),
+        in_specs=[scalars()] + [direct()] * len(args),
+        out_specs=[direct()] * 5,
+        out_shape=shapes,
+        compiler_params=params_of(8),
         name="dealt",
-    )(turns, first, up, down)
+    )(turns, *args)
 
 
 def project_kernel(ids_ref, *refs, step, with_q, chained):
@@ -1024,8 +1046,8 @@
 
 def shampoo_kernel(turn_ref, *refs, width, groups, heads):
     g_refs = refs[: 3 if groups else 1]
-    tail_ref, mb_ref, ls_ref, rs_ref, lr_ref, rr_ref = refs[len(g_refs) : len(g_refs) + 6]
-    bg_ref, ln_ref, rn_ref, nb_ref, max_ref, g_ref = refs[len(g_refs) + 6 :]
+    max_ref, mb_ref, ls_ref, rs_ref, lr_ref, rr_ref = refs[len(g_refs) : len(g_refs) + 6]
+    bg_ref, ln_ref, rn_ref, nb_ref, g_ref = refs[len(g_refs) + 6 :]
     i = pl.program_id(0)
     if groups:
         for n in range(3):
@@ -1035,20 +1057,9 @@
                 g_ref[...] = g_refs[n][...]
     else:
         g_ref[...] = g_refs[0][...]
-    slots = tail_ref[0:8, :128]
-    lanes = slots.shape[1]
-    slots = slots + pltpu.roll(slots, lanes - heads, 1) + pltpu.roll(slots, lanes - 2 * heads, 1)
-    lane = lax.broadcasted_iota(jnp.int32, slots.shape, 1)
-    row = lax.broadcasted_iota(jnp.int32, slots.shape, 0)
-    largest = jnp.zeros(slots.shape, f32)
-    scales = []
-    for h in range(heads):
-        chosen = (row == 7) & (lane % (3 * heads) == h) & (lane < 3 * heads * WIDE)
-        best = jnp.max(jnp.where(chosen, slots, neg_large), axis=1, keepdims=True)
-        best = jnp.max(best, axis=0, keepdims=True)
-        largest = jnp.where(lane == h, best, largest)
-        scales.append(jnp.sqrt(tau_clip / jnp.maximum(best, tau_clip)))
-    max_ref[...] = largest
+    scales = [
+        jnp.sqrt(tau_clip / jnp.maximum(max_ref[0:1, h : h + 1], tau_clip)) for h in range(heads)
+    ]
     per_row = 3 * heads * HEAD // PB
     column = lax.broadcasted_iota(jnp.int32, (1, PB), 1)
     for j in range(width):
@@ -1072,7 +1083,7 @@
         nb_ref[j] = (mb_ref[j] - rate_matrix * step_val) * factor
 
 
-def shampoo(turns, grads, groups, tail, master, left_s, right_s, left_r, right_r, heads):
+def shampoo(turns, grads, groups, largest, master, left_s, right_s, left_r, right_r, heads):
     count = master.shape[0]
     width = WIDE if groups else 1
     block = pl.BlockSpec((width, PB, PB), lambda i, *_: (i, 0, 0))
@@ -1086,15 +1097,15 @@
         grid_spec=pltpu.PrefetchScalarGridSpec(
             num_scalar_prefetch=1,
             grid=(count // width,),
-            in_specs=specs + [whole_block(tail.shape)] + [block] * 5,
-            out_specs=[block] * 4 + [whole_block((8, 128))],
+            in_specs=specs + [whole_block(largest.shape)] + [block] * 5,
+            out_specs=[block] * 4,
             scratch_shapes=[pltpu.VMEM((PB, PB * width), bf16)],
         ),
-        out_shape=[shape] * 4 + [jax.ShapeDtypeStruct((8, 128), f32)],
+        out_shape=[shape] * 4,
         compiler_params=params_of(16),
         cost_estimate=cost(16 * count * PB**3, 40 * count * PB * PB),
         name="shampoo",
-    )(turns, *grads, tail, master, left_s, right_s, left_r, right_r)
+    )(turns, *grads, largest, master, left_s, right_s, left_r, right_r)
 
 
 def gather_quarters(own):
@@ -1125,7 +1136,7 @@
     return near, far[0] if len(far) == 1 else jnp.concatenate(far, axis=0)
 
 
-def reduce_group(near, far):
+def reduce_group(near, far, label):
     count = lax.axis_size(CTX)
     back = [
         shift_shard(far[count * (u - 1) : count * u], u)
@@ -1137,15 +1148,13 @@
         for part in back:
             value = value + part[step].astype(f32)
         halves.append(value)
-    return halves[0], [shift_ctx(halves[step].astype(bf16), step) for step in near_first(count)]
-
-
-def total_of(first, others, *wait):
-    if wait:
-        others = lax.optimization_barrier(tuple(others) + wait)[: len(others)]
-    for other in others:
-        first = first + other.astype(f32)
-    return first
+    steps = near_first(count)
+    if count == 4 and label == "0":
+        right, left = back_two(halves[2].astype(bf16))
+        halves[1] = halves[1] + right.astype(f32)
+        halves[3] = halves[3] + left.astype(f32)
+        steps = [1, 3]
+    return [halves[0]] + [shift_ctx(halves[step].astype(bf16), step) for step in steps]
 
 
 def per_device(
@@ -1197,7 +1206,7 @@
     own_in = pick_quarter(ids, flat_in)
 
     if packed:
-        own_packed = after(pack_rows(master_blocks), turns, up_bias, q_bias, kv_bias)
+        own_packed = pack_rows(master_blocks)
         held = [
             owner_move(own_packed[PB * slot : PB * (slot + 1)], slot_pairs(slot))
             for slot in range(3)
@@ -1262,8 +1271,8 @@
     g_down = group_grads(turns, (act_n, act_f), (d_n, d_f), near)
     g_up = group_grads(turns, (x_n, x_f), (dg_n, dg_f), near)
     if packed:
-        down_own = reduce_group(*g_down)
-        up_own = reduce_group(*g_up)
+        down_own = reduce_group(*g_down, "2")
+        up_own = reduce_group(*g_up, "1")
     out_quarters = gather_quarters(after(out_own, b_pieces[3]))
     d_query, d_kv, sums_a, d_branch = attention_backward(
         queries, b_pieces, w_out, probs, kv_all, addr, heads_here
@@ -1308,11 +1317,9 @@
     outer_cols = D // owner_count
     inner_cols = inner_biases.shape[1] // owner_count
     if packed:
-        down_own = total_of(*down_own, near_rows).astype(bf16)
-        up_own = total_of(*up_own, near_rows).astype(bf16)
-        late_own = total_of(*reduce_group(near_rows, far_rows))
-        dealt = deal_rows(turns, late_own, up_own, down_own)
-        tail = late_own[PB:]
+        *dealt, tail, largest = deal_rows(
+            turns, reduce_group(near_rows, far_rows, "0"), up_own, down_own, heads_here
+        )
         outer_own = tail[:6, :outer_cols]
         inner_own = tail[6:7, :inner_cols]
         grads = [
@@ -1331,16 +1338,15 @@
         outer_own = lax.psum_scatter(outer_part, OWN, scatter_dimension=1, tiled=True)
         inner_own = lax.psum_scatter(inner_part[None, :], OWN, scatter_dimension=1, tiled=True)
         largest = lax.pmax(tops[:heads_here, 0], OWN)
-        slots = jnp.tile(jnp.concatenate([largest, jnp.zeros((2 * heads_here,), f32)]), WIDE)
-        tail = jnp.zeros((16, D), f32).at[7, : slots.shape[0]].set(slots)
+        largest = jnp.zeros((8, 128), f32).at[0, :heads_here].set(largest)
     outer_own = outer_own + swap(outer_own, 1)
     outer_own = outer_own + swap(outer_own, 2)
 
-    block_sum, left_new, right_new, new_blocks, largest = shampoo(
+    block_sum, left_new, right_new, new_blocks = shampoo(
         turns,
         grads,
         groups,
-        tail,
+        largest,
         master_blocks,
         left_stats,
         right_stats,

time: 343 us -> 353 us (1.029); the launches traced: 341 us -> 346 us
  starting transfers between devices: 102 us -> 110 us
  other arithmetic: 12.7 us -> 8.31 us
    ppermute x42, waiting for transfers between devices: 72.8 us -> 63 us  [swap(): return lax.ppermute(rows, TP, [(i, i ^ mask) for i in range(count)])]
    ppermute x1 -> x2, starting transfers between devices: 2.18 us -> 10.3 us  [back_two(): right = lax.ppermute(rows, CTX, [(0, 1), (1, 2)])]
    ppermute x18 -> x17, waiting for transfers between devices: 22.4 us -> 30.1 us  [shift_ctx(): lax.ppermute(rows, CTX, [(i, (i + step) % count) for i in range(count)])]
    ppermute x5, waiting for transfers between devices: 4.69 us -> 11.6 us  [shift_shard(): lax.ppermute(rows, SHARD, [(i, (i + step) % count) for i in range(count)])]
    ppermute x6, waiting for transfers between devices: 18.8 us -> 15.2 us  [owner_move(): return lax.ppermute(rows, OWN, pairs)]
    ppermute x18 -> x17, starting transfers between devices: 19.2 us -> 16.4 us  [shift_ctx(): lax.ppermute(rows, CTX, [(i, (i + step) % count) for i in range(count)])]
    unnamed x64 -> x70, local copies, waits for them, and re-layouts: 7.04 us -> 8.86 us
  transfers between devices with their start and end apart: 77 -> 78, of which waited for: 30 -> 27; matrix products, arithmetic and copies ran while one was open for 4% -> 2% of each run, Pallas kernels for 21% -> 20%
where the time goes in v3:
time: 353 us; the launch traced here: 346 us
  waiting for transfers between devices  136 us (39%)
  starting transfers between devices  110 us (31%)
  Pallas kernels  76.2 us (22%)
  local copies, waits for them, and re-layouts  10.2 us (3%)
  other arithmetic  8.31 us (2%)
  between operations  4.54 us (1%)
    ppermute x42, waiting for transfers between devices, swap(): return lax.ppermute(rows, TP, [(i, i ^ mask) for i in range(count)])  63 us
    ppermute x42, starting transfers between devices, swap(): return lax.ppermute(rows, TP, [(i, i ^ mask) for i in range(count)])  51.5 us
    ppermute x17, waiting for transfers between devices, shift_ctx(): lax.ppermute(rows, CTX, [(i, (i + step) % count) for i in range(count)])  30.1 us
    ppermute x17, starting transfers between devices, shift_ctx(): lax.ppermute(rows, CTX, [(i, (i + step) % count) for i in range(count)])  16.4 us
    ppermute x6, waiting for transfers between devices, owner_move(): return lax.ppermute(rows, OWN, pairs)  15.2 us
    ppermute x6, starting transfers between devices, owner_move(): return lax.ppermute(rows, OWN, pairs)  15.1 us
    pallas_call x1, Pallas kernels, attention_backward(): pl.pallas_call(functools.partial(bwd_kernel, heads=heads, group=group), i...  13.3 us
    ppermute x2, waiting for transfers between devices, forward_two(): left = lax.ppermute(from_right, CTX, [(1, 0), (2, 1)])  12.5 us
  transfers between devices with their start and end apart: 78, of which 27 were waited for; matrix products, arithmetic and copies ran while one was open for 2% of the time, Pallas kernels for 20%

profile of v3, /device:TPU:9, one launch (start us, length us, event | category | flops | bytes accessed | tf_op | source)
XLA Modules:
  0.0 346.0 jit_solution(9853880750369331413)
XLA Ops:
  16.8 12.9 %collective-permute-done.1.b_ref = bf16[96,768]{1,0:T(8,128)(2,1)S(1)} collective-permute-done((bf16[96,768]{1,0:T(8,128)(2,1)S(1)}, bf16[96,768]{1,0:T(8,128)(2,1)S(1)}, u32[]{:S(2)}, u32[]{:S(2)}) %collective-permute-start.1) | collective-permute-done | bytes 147488 | tf_op jit(solution)/shard_map/ppermute | solution.py:119
  37.8 5.1 %collective-permute-done.3 = bf16[96,768]{1,0:T(8,128)(2,1)S(1)} collective-permute-done((bf16[96,768]{1,0:T(8,128)(2,1)S(1)}, bf16[96,768]{1,0:T(8,128)(2,1)S(1)}, u32[]{:S(2)}, u32[]{:S(2)}) %collective-permute-start.3) | collective-permute-done | bytes 147488 | tf_op jit(solution)/shard_map/ppermute | solution.py:98
  44.8 8.2 %collective-permute-done.10 = bf16[256,768]{1,0:T(8,128)(2,1)S(1)} collective-permute-done((bf16[256,768]{1,0:T(8,128)(2,1)S(1)}, bf16[256,768]{1,0:T(8,128)(2,1)S(1)}, u32[]{:S(2)}, u32[]{:S(2)}) %collective-permute-start.10) | collective-permute-done | bytes 393248 | tf_op jit(solution)/shard_map/ppermute | solution.py:103
  59.2 7.8 %collective-permute-start.14 = (bf16[256,768]{1,0:T(8,128)(2,1)S(1)}, bf16[256,768]{1,0:T(8,128)(2,1)S(1)}, u32[]{:S(2)}, u32[]{:S(2)}) collective-permute-start(bf16[256,768]{1,0:T(8,128)(2,1)S(1)} %collective-permute-done.9.refs_0_), channel_id=1, source_target_pairs={{0,1},{1,0},{2,3},{3,2},{4,5},{5,4},{6,7},{7,6},{8,9},{9,8},{10,11... | collective-permute-start | bytes 1179656 | tf_op jit(solution)/shard_map/ppermute | solution.py:93
  67.6 4.1 %collective-permute-start.13 = (bf16[256,768]{1,0:T(8,128)(2,1)S(1)}, bf16[256,768]{1,0:T(8,128)(2,1)S(1)}, u32[]{:S(2)}, u32[]{:S(2)}) collective-permute-start(bf16[256,768]{1,0:T(8,128)(2,1)S(1)} %collective-permute-done.12.refs_2_), channel_id=1, source_target_pairs={{0,1},{1,0},{2,3},{3,2},{4,5},{5,4},{6,7},{7,6},{8,9},{9,8},{10,11... | collective-permute-start | bytes 1179656 | tf_op jit(solution)/shard_map/ppermute | solution.py:93
  82.9 6.6 %afwd.1 = (bf16[1024,256]{1,0:T(8,128)(2,1)S(1)}, bf16[16,192,512]{2,1,0:T(8,128)(2,1)S(1)}, f32[8,128]{1,0:T(8,128)S(1)}) custom-call(s32[128]{0:T(128)S(1)} %get-tuple-element.95.addr_ref, s32[128]{0:T(128)S(1)} %get-tuple-element.96.valid_ref, s32[16]{0:T(128)S(1)} %get-tuple-element.97.query_ref, bf16[1024,256]{1,0:T(8,128)(2,1)S(1)} %get-tuple-element.101.q_ref, ...), custom_call_target="tpu_custom_call" | custom-call | flops 1610612736 | bytes 7340032 | tf_op jit(solution)/shard_map/afwd/pallas_call | solution.py:950
  96.6 4.3 %collective-permute-done.26 = bf16[192,768]{1,0:T(8,128)(2,1)S(1)} collective-permute-done((bf16[192,768]{1,0:T(8,128)(2,1)S(1)}, bf16[192,768]{1,0:T(8,128)(2,1)S(1)}, u32[]{:S(2)}, u32[]{:S(2)}) %collective-permute-start.26) | collective-permute-done | bytes 294944 | tf_op jit(solution)/shard_map/ppermute | solution.py:103
  104.4 6.5 %collective-permute-done.21.got_ref = bf16[256,768]{1,0:T(8,128)(2,1)S(1)} collective-permute-done((bf16[256,768]{1,0:T(8,128)(2,1)S(1)}, bf16[256,768]{1,0:T(8,128)(2,1)S(1)}, u32[]{:S(2)}, u32[]{:S(2)}) %collective-permute-start.21) | collective-permute-done | bytes 393248 | tf_op jit(solution)/shard_map/ppermute | solution.py:93
  113.7 6.8 %collective-permute-done.29.xa_ref = bf16[256,768]{1,0:T(8,128)(2,1)S(1)} collective-permute-done((bf16[256,768]{1,0:T(8,128)(2,1)S(1)}, bf16[256,768]{1,0:T(8,128)(2,1)S(1)}, u32[]{:S(2)}, u32[]{:S(2)}) %collective-permute-start.29) | collective-permute-done | bytes 393248 | tf_op jit(solution)/shard_map/ppermute | solution.py:93
  124.1 4.9 %collective-permute-done.27.far_ref = bf16[4,192,768]{2,1,0:T(8,128)(2,1)S(1)} collective-permute-done((bf16[4,192,768]{2,1,0:T(8,128)(2,1)S(1)}, bf16[4,192,768]{2,1,0:T(8,128)(2,1)S(1)}, u32[]{:S(2)}, u32[]{:S(2)}) %collective-permute-start.27) | collective-permute-done | bytes 1179680 | tf_op jit(solution)/shard_map/ppermute | solution.py:115
  139.4 9.4 %collective-permute-done.32.got_ref = bf16[256,768]{1,0:T(8,128)(2,1)S(1)} collective-permute-done((bf16[256,768]{1,0:T(8,128)(2,1)S(1)}, bf16[256,768]{1,0:T(8,128)(2,1)S(1)}, u32[]{:S(2)}, u32[]{:S(2)}) %collective-permute-start.32) | collective-permute-done | bytes 393248 | tf_op jit(solution)/shard_map/ppermute | solution.py:93
  151.2 9.5 %collective-permute-done.35.da_ref = bf16[256,768]{1,0:T(8,128)(2,1)S(1)} collective-permute-done((bf16[256,768]{1,0:T(8,128)(2,1)S(1)}, bf16[256,768]{1,0:T(8,128)(2,1)S(1)}, u32[]{:S(2)}, u32[]{:S(2)}) %collective-permute-start.35) | collective-permute-done | bytes 393248 | tf_op jit(solution)/shard_map/ppermute | solution.py:93
  171.8 8.9 %collective-permute-done.38.got_ref = bf16[256,768]{1,0:T(8,128)(2,1)S(1)} collective-permute-done((bf16[256,768]{1,0:T(8,128)(2,1)S(1)}, bf16[256,768]{1,0:T(8,128)(2,1)S(1)}, u32[]{:S(2)}, u32[]{:S(2)}) %collective-permute-start.38) | collective-permute-done | bytes 393248 | tf_op jit(solution)/shard_map/ppermute | solution.py:93
  184.6 7.7 %collective-permute-done.39.refs_2_ = bf16[256,768]{1,0:T(8,128)(2,1)S(1)} collective-permute-done((bf16[256,768]{1,0:T(8,128)(2,1)S(1)}, bf16[256,768]{1,0:T(8,128)(2,1)S(1)}, u32[]{:S(2)}, u32[]{:S(2)}) %collective-permute-start.39) | collective-permute-done | bytes 393248 | tf_op jit(solution)/shard_map/ppermute | solution.py:93
  200.9 13.3 %abwd.1 = (bf16[1024,256]{1,0:T(8,128)(2,1)S(1)}, bf16[4096,384]{1,0:T(8,128)(2,1)S(1)}, f32[8,256]{1,0:T(8,128)S(1)}, bf16[1024,768]{1,0:T(8,128)(2,1)S(1)}) custom-call(s32[128]{0:T(128)S(1)} %get-tuple-element.95.addr_ref, bf16[1024,256]{1,0:T(8,128)(2,1)S(1)} %get-tuple-element.101.q_ref, bf16[16,192,512]{2,1,0:T(8,128)(2,1)S(1)} %get-tuple-element.135.p_ref, ...), custom_call_target="tpu_custom_call" | custom-call | flops 3221225472 | bytes 11010048 | tf_op jit(solution)/shard_map/abwd/pallas_call | solution.py:1022
  216.6 5.4 %late.1 = (bf16[4,112,768]{2,1,0:T(8,128)(2,1)S(1)}, bf16[4,112,768]{2,1,0:T(8,128)(2,1)S(1)}) custom-call(s32[32]{0:T(128)S(1)} %get-tuple-element.94.turn_ref, bf16[4096,768]{1,0:T(8,128)(2,1)S(1)} %get-tuple-element.146.x_ref, bf16[4096,384]{1,0:T(8,128)(2,1)S(1)} %get-tuple-element.136.dkv_ref, bf16[1024,256]{1,0:T(8,128)(2,1)S(1)} %get-tuple-element.143.refs_0_.dq_ref, ...), custom_call_target="tpu_custom_call" | custom-call | flops 2415919104 | bytes 9437184 | tf_op jit(solution)/shard_map/late/pallas_call | solution.py:854
  232.5 6.7 %collective-permute-done.60 = bf16[4,112,768]{2,1,0:T(8,128)(2,1)S(1)} collective-permute-done((bf16[4,112,768]{2,1,0:T(8,128)(2,1)S(1)}, bf16[4,112,768]{2,1,0:T(8,128)(2,1)S(1)}, u32[]{:S(2)}, u32[]{:S(2)}) %collective-permute-start.60) | collective-permute-done | bytes 688160 | tf_op jit(solution)/shard_map/ppermute | solution.py:115
  240.2 8.9 %collective-permute-done.48 = bf16[256,768]{1,0:T(8,128)(2,1)S(1)} collective-permute-done((bf16[256,768]{1,0:T(8,128)(2,1)S(1)}, bf16[256,768]{1,0:T(8,128)(2,1)S(1)}, u32[]{:S(2)}, u32[]{:S(2)}) %collective-permute-start.48) | collective-permute-done | bytes 393248 | tf_op jit(solution)/shard_map/ppermute | solution.py:93
  263.5 10.7 %collective-permute-done.72.refs_10_ = bf16[96,768]{1,0:T(8,128)(2,1)S(1)} collective-permute-done((bf16[96,768]{1,0:T(8,128)(2,1)S(1)}, bf16[96,768]{1,0:T(8,128)(2,1)S(1)}, u32[]{:S(2)}, u32[]{:S(2)}) %collective-permute-start.72) | collective-permute-done | bytes 147488 | tf_op jit(solution)/shard_map/ppermute | solution.py:98
  275.5 5.6 %collective-permute-start.41 = (bf16[256,768]{1,0:T(8,128)(2,1)S(1)}, bf16[256,768]{1,0:T(8,128)(2,1)S(1)}, u32[]{:S(2)}, u32[]{:S(2)}) collective-permute-start(bf16[256,768]{1,0:T(8,128)(2,1)S(1)} %get-tuple-element.133.refs_0_), channel_id=1, source_target_pairs={{0,1},{1,0},{2,3},{3,2},{4,5},{5,4},{6,7},{7,6},{8,9},{9,8},{10,11... | collective-permute-start | bytes 1179656 | tf_op jit(solution)/shard_map/ppermute | solution.py:93
  282.5 6.3 %collective-permute-start.61 = (bf16[112,768]{1,0:T(8,128)(2,1)S(1)}, bf16[112,768]{1,0:T(8,128)(2,1)S(1)}, u32[]{:S(2)}, u32[]{:S(2)}) collective-permute-start(bf16[112,768]{1,0:T(8,128)(2,1)S(1)} %get-tuple-element.183), channel_id=1, source_target_pairs={{0,4},{4,8},{1,5},{5,9},{2,6},{6,10},{3,7},{7,11},{16,20},{20,24},... | collective-permute-start | bytes 516104 | tf_op jit(solution)/shard_map/ppermute | solution.py:108
  303.0 9.7 %collective-permute-done.64.refs_2_ = bf16[112,768]{1,0:T(8,128)(2,1)S(1)} collective-permute-done((bf16[112,768]{1,0:T(8,128)(2,1)}, bf16[112,768]{1,0:T(8,128)(2,1)S(1)}, u32[]{:S(2)}, u32[]{:S(2)}) %collective-permute-start.64) | collective-permute-done | bytes 172064 | tf_op jit(solution)/shard_map/ppermute | solution.py:98
  312.7 4.5 %collective-permute-done.62.refs_1_ = bf16[112,768]{1,0:T(8,128)(2,1)} collective-permute-done((bf16[112,768]{1,0:T(8,128)(2,1)}, bf16[112,768]{1,0:T(8,128)(2,1)}, u32[]{:S(2)}, u32[]{:S(2)}) %collective-permute-start.62) | collective-permute-done | bytes 172064 | tf_op jit(solution)/shard_map/ppermute | solution.py:98
  339.7 4.3 %shampoo.1 = (f32[24,96,96]{2,1,0:T(8,128)}, f32[24,96,96]{2,1,0:T(8,128)}, f32[24,96,96]{2,1,0:T(8,128)}, f32[24,96,96]{2,1,0:T(8,128)}) custom-call(s32[32]{0:T(128)S(1)} %get-tuple-element.94.turn_ref, bf16[96,768]{1,0:T(8,128)(2,1)S(1)} %collective-permute-done.73.refs_0_, bf16[96,768]{1,0:T(8,128)(2,1)S(1)} %collective-permute-done.74.refs_1_, ...), custom_call_target="tpu_custom_call" | custom-call | flops 339738624 | bytes 8847360 | tf_op jit(solution)/shard_map/shampoo/pallas_call | solution.py:1095
  (265 shorter events, 163.3 us)
Async XLA Ops:
  2.7 29.7 %collective-permute-start.9 = (bf16[256,768]{1,0:T(8,128)(2,1)S(1)}, bf16[256,768]{1,0:T(8,128)(2,1)S(1)}, u32[]{:S(2)}, u32[]{:S(2)}) collective-permute-start(bf16[256,768]{1,0:T(8,128)(2,1)S(1)} %pick.1), channel_id=1, source_target_pairs={{0,12},{4,0},{8,4},{12,8},{1,13},{5,1},{9,5},{13,9},{2,14},{6,2},{... | collective-permute-start | bytes 1179656 | tf_op jit(solution)/shard_map/ppermute | solution.py:98
  2.8 32.1 %collective-permute-start.7 = (bf16[256,768]{1,0:T(8,128)(2,1)S(1)}, bf16[256,768]{1,0:T(8,128)(2,1)S(1)}, u32[]{:S(2)}, u32[]{:S(2)}) collective-permute-start(bf16[256,768]{1,0:T(8,128)(2,1)S(1)} %pick.1), channel_id=1, source_target_pairs={{0,4},{4,8},{8,12},{12,0},{1,5},{5,9},{9,13},{13,1},{2,6},{6,10},{... | collective-permute-start | bytes 1179656 | tf_op jit(solution)/shard_map/ppermute | solution.py:98
  7.9 21.8 %collective-permute-start.1 = (bf16[96,768]{1,0:T(8,128)(2,1)S(1)}, bf16[96,768]{1,0:T(8,128)(2,1)S(1)}, u32[]{:S(2)}, u32[]{:S(2)}) collective-permute-start(bf16[96,768]{1,0:T(8,128)(2,1)S(1)} %get-tuple-element.194), channel_id=1, source_target_pairs={{0,4},{4,16},{8,28},{12,8},{16,20},{20,0},{24,12},{28,24},{1,5},{5... | collective-permute-start | bytes 442376 | tf_op jit(solution)/shard_map/ppermute | solution.py:119
  10.2 19.5 %collective-permute-start = (bf16[96,768]{1,0:T(8,128)(2,1)S(1)}, bf16[96,768]{1,0:T(8,128)(2,1)S(1)}, u32[]{:S(2)}, u32[]{:S(2)}) collective-permute-start(bf16[96,768]{1,0:T(8,128)(2,1)S(1)} %get-tuple-element.195), channel_id=1, source_target_pairs={{0,0},{4,12},{8,24},{12,4},{16,16},{20,28},{24,8},{28,20},{1,1},{5... | collective-permute-start | bytes 442376 | tf_op jit(solution)/shard_map/ppermute | solution.py:119
  32.5 20.5 %collective-permute-start.10 = (bf16[256,768]{1,0:T(8,128)(2,1)S(1)}, bf16[256,768]{1,0:T(8,128)(2,1)S(1)}, u32[]{:S(2)}, u32[]{:S(2)}) collective-permute-start(bf16[256,768]{1,0:T(8,128)(2,1)S(1)} %collective-permute-done.9.refs_0_), channel_id=1, source_target_pairs={{4,0},{8,4},{5,1},{9,5},{6,2},{10,6},{7,3},{11,7},{20,16},{24,20},... | collective-permute-start | bytes 1179656 | tf_op jit(solution)/shard_map/ppermute | solution.py:103
  34.9 19.6 %collective-permute-start.8 = (bf16[256,768]{1,0:T(8,128)(2,1)S(1)}, bf16[256,768]{1,0:T(8,128)(2,1)S(1)}, u32[]{:S(2)}, u32[]{:S(2)}) collective-permute-start(bf16[256,768]{1,0:T(8,128)(2,1)S(1)} %collective-permute-done.7.refs_0_), channel_id=1, source_target_pairs={{4,8},{8,12},{5,9},{9,13},{6,10},{10,14},{7,11},{11,15},{20,24},{2... | collective-permute-start | bytes 1179656 | tf_op jit(solution)/shard_map/ppermute | solution.py:102
  43.0 24.1 %collective-permute-start.6 = (bf16[4,96,768]{2,1,0:T(8,128)(2,1)S(1)}, bf16[4,96,768]{2,1,0:T(8,128)(2,1)S(1)}, u32[]{:S(2)}, u32[]{:S(2)}) collective-permute-start(bf16[4,96,768]{2,1,0:T(8,128)(2,1)S(1)} %pad_maximum_fusion.1.near_ref), channel_id=1, source_target_pairs={{0,16},{16,0},{1,17},{17,1},{2,18},{18,2},{3,19},{19,3},{4,20},{20... | collective-permute-start | bytes 1769480 | tf_op jit(solution)/shard_map/ppermute | solution.py:115
  56.0 18.6 %collective-permute-start.19 = (bf16[256,768]{1,0:T(8,128)(2,1)S(1)}, bf16[256,768]{1,0:T(8,128)(2,1)S(1)}, u32[]{:S(2)}, u32[]{:S(2)}) collective-permute-start(bf16[256,768]{1,0:T(8,128)(2,1)S(1)} %collective-permute-done.18.refs_2_), channel_id=1, source_target_pairs={{0,1},{1,0},{2,3},{3,2},{4,5},{5,4},{6,7},{7,6},{8,9},{9,8},{10,11... | collective-permute-start | bytes 1179656 | tf_op jit(solution)/shard_map/ppermute | solution.py:93
  59.2 20.6 %collective-permute-start.14 = (bf16[256,768]{1,0:T(8,128)(2,1)S(1)}, bf16[256,768]{1,0:T(8,128)(2,1)S(1)}, u32[]{:S(2)}, u32[]{:S(2)}) collective-permute-start(bf16[256,768]{1,0:T(8,128)(2,1)S(1)} %collective-permute-done.9.refs_0_), channel_id=1, source_target_pairs={{0,1},{1,0},{2,3},{3,2},{4,5},{5,4},{6,7},{7,6},{8,9},{9,8},{10,11... | collective-permute-start | bytes 1179656 | tf_op jit(solution)/shard_map/ppermute | solution.py:93
  103.4 25.5 %collective-permute-start.27 = (bf16[4,192,768]{2,1,0:T(8,128)(2,1)S(1)}, bf16[4,192,768]{2,1,0:T(8,128)(2,1)S(1)}, u32[]{:S(2)}, u32[]{:S(2)}) collective-permute-start(bf16[4,192,768]{2,1,0:T(8,128)(2,1)S(1)} %pad_maximum_fusion.near_ref), channel_id=1, source_target_pairs={{0,16},{16,0},{1,17},{17,1},{2,18},{18,2},{3,19},{19,3},{4,20},{20... | collective-permute-start | bytes 3538952 | tf_op jit(solution)/shard_map/ppermute | solution.py:115
  183.1 17.8 %collective-permute-start.44 = (bf16[256,768]{1,0:T(8,128)(2,1)S(1)}, bf16[256,768]{1,0:T(8,128)(2,1)S(1)}, u32[]{:S(2)}, u32[]{:S(2)}) collective-permute-start(bf16[256,768]{1,0:T(8,128)(2,1)S(1)} %get-tuple-element.132.refs_0_), channel_id=1, source_target_pairs={{0,1},{1,0},{2,3},{3,2},{4,5},{5,4},{6,7},{7,6},{8,9},{9,8},{10,11... | collective-permute-start | bytes 1179656 | tf_op jit(solution)/shard_map/ppermute | solution.py:93
  196.8 26.2 %collective-permute-start.65 = (bf16[4,96,768]{2,1,0:T(8,128)(2,1)S(1)}, bf16[4,96,768]{2,1,0:T(8,128)(2,1)S(1)}, u32[]{:S(2)}, u32[]{:S(2)}) collective-permute-start(bf16[4,96,768]{2,1,0:T(8,128)(2,1)S(1)} %get-tuple-element.161), channel_id=1, source_target_pairs={{0,16},{16,0},{1,17},{17,1},{2,18},{18,2},{3,19},{19,3},{4,20},{20... | collective-permute-start | bytes 1769480 | tf_op jit(solution)/shard_map/ppermute | solution.py:115
  200.3 27.4 %collective-permute-start.69 = (bf16[4,96,768]{2,1,0:T(8,128)(2,1)S(1)}, bf16[4,96,768]{2,1,0:T(8,128)(2,1)S(1)}, u32[]{:S(2)}, u32[]{:S(2)}) collective-permute-start(bf16[4,96,768]{2,1,0:T(8,128)(2,1)S(1)} %get-tuple-element.167), channel_id=1, source_target_pairs={{0,16},{16,0},{1,17},{17,1},{2,18},{18,2},{3,19},{19,3},{4,20},{20... | collective-permute-start | bytes 1769480 | tf_op jit(solution)/shard_map/ppermute | solution.py:115
  223.1 28.4 %collective-permute-start.68 = (bf16[96,768]{1,0:T(8,128)(2,1)S(1)}, bf16[96,768]{1,0:T(8,128)(2,1)S(1)}, u32[]{:S(2)}, u32[]{:S(2)}) collective-permute-start(bf16[96,768]{1,0:T(8,128)(2,1)S(1)} %get-tuple-element.189), channel_id=1, source_target_pairs={{0,8},{4,12},{8,0},{12,4},{1,9},{5,13},{9,1},{13,5},{2,10},{6,14},... | collective-permute-start | bytes 442376 | tf_op jit(solution)/shard_map/ppermute | solution.py:98
  230.0 25.4 %collective-permute-start.55 = (bf16[512,768]{1,0:T(8,128)(2,1)S(1)}, bf16[512,768]{1,0:T(8,128)(2,1)S(1)}, u32[]{:S(2)}, u32[]{:S(2)}) collective-permute-start(bf16[512,768]{1,0:T(8,128)(2,1)S(1)} %get-tuple-element.145), channel_id=1, source_target_pairs={{0,1},{1,0},{2,3},{3,2},{4,5},{5,4},{6,7},{7,6},{8,9},{9,8},{10,11... | collective-permute-start | bytes 2359304 | tf_op jit(solution)/shard_map/ppermute | solution.py:93
  231.9 20.0 %collective-permute-start.45 = (bf16[512,768]{1,0:T(8,128)(2,1)S(1)}, bf16[512,768]{1,0:T(8,128)(2,1)S(1)}, u32[]{:S(2)}, u32[]{:S(2)}) collective-permute-start(bf16[512,768]{1,0:T(8,128)(2,1)S(1)} %get-tuple-element.138), channel_id=1, source_target_pairs={{0,1},{1,0},{2,3},{3,2},{4,5},{5,4},{6,7},{7,6},{8,9},{9,8},{10,11... | collective-permute-start | bytes 2359304 | tf_op jit(solution)/shard_map/ppermute | solution.py:93
  254.0 27.2 %collective-permute-start.42 = (bf16[256,768]{1,0:T(8,128)(2,1)S(1)}, bf16[256,768]{1,0:T(8,128)(2,1)S(1)}, u32[]{:S(2)}, u32[]{:S(2)}) collective-permute-start(bf16[256,768]{1,0:T(8,128)(2,1)S(1)} %get-tuple-element.133.refs_0_), channel_id=1, source_target_pairs={{0,2},{1,3},{2,0},{3,1},{4,6},{5,7},{6,4},{7,5},{8,10},{9,11},{10,... | collective-permute-start | bytes 1179656 | tf_op jit(solution)/shard_map/ppermute | solution.py:93
  255.2 26.0 %collective-permute-start.46 = (bf16[256,768]{1,0:T(8,128)(2,1)S(1)}, bf16[256,768]{1,0:T(8,128)(2,1)S(1)}, u32[]{:S(2)}, u32[]{:S(2)}) collective-permute-start(bf16[256,768]{1,0:T(8,128)(2,1)S(1)} %add_convert_fusion.7), channel_id=1, source_target_pairs={{0,2},{1,3},{2,0},{3,1},{4,6},{5,7},{6,4},{7,5},{8,10},{9,11},{10,... | collective-permute-start | bytes 1179656 | tf_op jit(solution)/shard_map/ppermute | solution.py:93
  255.4 27.1 %collective-permute-start.49 = (bf16[256,768]{1,0:T(8,128)(2,1)S(1)}, bf16[256,768]{1,0:T(8,128)(2,1)S(1)}, u32[]{:S(2)}, u32[]{:S(2)}) collective-permute-start(bf16[256,768]{1,0:T(8,128)(2,1)S(1)} %add_convert_fusion.5), channel_id=1, source_target_pairs={{0,4},{4,8},{1,5},{5,9},{2,6},{6,10},{3,7},{7,11},{16,20},{20,24},... | collective-permute-start | bytes 1179656 | tf_op jit(solution)/shard_map/ppermute | solution.py:108
  275.5 19.8 %collective-permute-start.41 = (bf16[256,768]{1,0:T(8,128)(2,1)S(1)}, bf16[256,768]{1,0:T(8,128)(2,1)S(1)}, u32[]{:S(2)}, u32[]{:S(2)}) collective-permute-start(bf16[256,768]{1,0:T(8,128)(2,1)S(1)} %get-tuple-element.133.refs_0_), channel_id=1, source_target_pairs={{0,1},{1,0},{2,3},{3,2},{4,5},{5,4},{6,7},{7,6},{8,9},{9,8},{10,11... | collective-permute-start | bytes 1179656 | tf_op jit(solution)/shard_map/ppermute | solution.py:93
  289.8 29.0 %collective-permute-start.56 = (bf16[256,768]{1,0:T(8,128)(2,1)}, bf16[256,768]{1,0:T(8,128)(2,1)}, u32[]{:S(2)}, u32[]{:S(2)}) collective-permute-start(bf16[256,768]{1,0:T(8,128)(2,1)} %add_convert_fusion.1), channel_id=1, source_target_pairs={{0,2},{1,3},{2,0},{3,1},{4,6},{5,7},{6,4},{7,5},{8,10},{9,11},{10,... | collective-permute-start | bytes 1179656 | tf_op jit(solution)/shard_map/ppermute | solution.py:93
  291.2 27.6 %collective-permute-start.54 = (bf16[256,768]{1,0:T(8,128)(2,1)}, bf16[256,768]{1,0:T(8,128)(2,1)}, u32[]{:S(2)}, u32[]{:S(2)}) collective-permute-start(bf16[256,768]{1,0:T(8,128)(2,1)} %add_convert_fusion.2), channel_id=1, source_target_pairs={{0,12},{4,0},{8,4},{12,8},{1,13},{5,1},{9,5},{13,9},{2,14},{6,2},{... | collective-permute-start | bytes 1179656 | tf_op jit(solution)/shard_map/ppermute | solution.py:98
  292.1 26.7 %collective-permute-start.50 = (bf16[256,768]{1,0:T(8,128)(2,1)}, bf16[256,768]{1,0:T(8,128)(2,1)}, u32[]{:S(2)}, u32[]{:S(2)}) collective-permute-start(bf16[256,768]{1,0:T(8,128)(2,1)} %add_convert_fusion.4), channel_id=1, source_target_pairs={{0,4},{4,8},{8,12},{12,0},{1,5},{5,9},{9,13},{13,1},{2,6},{6,10},{... | collective-permute-start | bytes 1179656 | tf_op jit(solution)/shard_map/ppermute | solution.py:98
  296.8 20.5 %collective-permute-start.62 = (bf16[112,768]{1,0:T(8,128)(2,1)}, bf16[112,768]{1,0:T(8,128)(2,1)}, u32[]{:S(2)}, u32[]{:S(2)}) collective-permute-start(bf16[112,768]{1,0:T(8,128)(2,1)} %get-tuple-element.182), channel_id=1, source_target_pairs={{0,4},{4,8},{8,12},{12,0},{1,5},{5,9},{9,13},{13,1},{2,6},{6,10},{... | collective-permute-start | bytes 516104 | tf_op jit(solution)/shard_map/ppermute | solution.py:98
  (89 other events, 945.8 us)
